TPU v7x, 32 devices: a whole 2x2x4 slice. The times are simulated.
32 devices in a mesh: dp: 8 (over z, y), tensor: 4 (over x, core).
Axes of the slice: x: 2, y: 2, z: 4, core: 2. Of those that a mesh axis runs over, the one named last changes fastest.
Arguments:
- block_in: float32 [4096, 640], P(('dp', 'tensor')), may hold values from -6 to 6
- d_output: float32 [4096, 640], P(('dp', 'tensor')), may hold values from -6 to 6
- doc_ids: int32 [8, 512], P('dp'), may hold values from 0 to 3, never falling along the last dimension, each value on 1 to 256 neighbouring positions
- w_query: float32 [640, 1024], P('dp', 'tensor'), may hold values from -0.25 to 0.25
- w_key: float32 [640, 256], P('dp'), may hold values from -0.25 to 0.25
- w_value: float32 [640, 256], P('dp'), may hold values from -0.25 to 0.25
- w_output: float32 [640, 1024], P('dp', 'tensor'), may hold values from -0.1875 to 0.1875
- w_gate: float32 [640, 2048], P('dp', 'tensor'), may hold values from -0.25 to 0.25
- w_up: float32 [640, 2048], P('dp', 'tensor'), may hold values from -0.25 to 0.25
- w_down: float32 [640, 2048], P('dp', 'tensor'), may hold values from -0.125 to 0.125
- mom_query: float32 [640, 1024], P('dp', 'tensor'), may hold values from -112 to 112
- mom_key: float32 [640, 256], P('dp'), may hold values from -112 to 112
- mom_value: float32 [640, 256], P('dp'), may hold values from -112 to 112
- mom_output: float32 [640, 1024], P('dp', 'tensor'), may hold values from -112 to 112
- mom_gate: float32 [640, 2048], P('dp', 'tensor'), may hold values from -112 to 112
- mom_up: float32 [640, 2048], P('dp', 'tensor'), may hold values from -112 to 112
- mom_down: float32 [640, 2048], P('dp', 'tensor'), may hold values from -112 to 112
- gains: float32 [3072], replicated, may hold values from -0.4 to 0.6
- adam_first: float32 [3072], replicated, may hold values from -112 to 112
- adam_second: float32 [3072], replicated, may hold values from 204.8 to 8192
Outputs:
- block_out: float32 [4096, 640], P(('dp', 'tensor'))
- d_input: float32 [4096, 640], P(('dp', 'tensor'))
- grad_query: float32 [640, 1024], P('dp', 'tensor')
- grad_key: float32 [640, 256], P('dp')
- grad_value: float32 [640, 256], P('dp')
- grad_output: float32 [640, 1024], P('dp', 'tensor')
- grad_gate: float32 [640, 2048], P('dp', 'tensor')
- grad_up: float32 [640, 2048], P('dp', 'tensor')
- grad_down: float32 [640, 2048], P('dp', 'tensor')
- grad_gains: float32 [3072], replicated
- new_query: float32 [640, 1024], P('dp', 'tensor')
- new_key: float32 [640, 256], P('dp')
- new_value: float32 [640, 256], P('dp')
- new_output: float32 [640, 1024], P('dp', 'tensor')
- new_gate: float32 [640, 2048], P('dp', 'tensor')
- new_up: float32 [640, 2048], P('dp', 'tensor')
- new_down: float32 [640, 2048], P('dp', 'tensor')
- momentum_query: float32 [640, 1024], P('dp', 'tensor')
- momentum_key: float32 [640, 256], P('dp')
- momentum_value: float32 [640, 256], P('dp')
- momentum_output: float32 [640, 1024], P('dp', 'tensor')
- momentum_gate: float32 [640, 2048], P('dp', 'tensor')
- momentum_up: float32 [640, 2048], P('dp', 'tensor')
- momentum_down: float32 [640, 2048], P('dp', 'tensor')
- new_gains: float32 [3072], replicated
- next_first: float32 [3072], replicated
- next_second: float32 [3072], replicated
Inputs may be any that keep to these rules, and one draw needn't show every extreme that they name: `doc_ids`: along each sequence the document id never falls; each document covers 1 to half of 512 tokens, and some document covers exactly half of 512.
All inputs are finite; a program needn't handle non-finite values.
Results may differ from a plain program's by a relative error of at most 0.02.
Values may be sent and summed in bfloat16 or wider, within the bound.
No kernel may reach another device: no remote copies, remote signals or barrier semaphores. Data moves between devices by JAX's collectives and lax.ppermute only.
A program may use at most 64 MiB of HBM per device.

v0:
```python
import math

import jax
import jax.numpy as jnp
from jax import lax
from jax.experimental import pallas as pl
from jax.experimental.pallas import tpu as pltpu
from jax.sharding import Mesh
from jax.sharding import PartitionSpec as P

NS_STEPS = 5
STEP = 5


EPSILON = 1e-06
ROPE_BASE = 10000.0
MUON_BETA = 0.95
MUON_RATE = 0.04
MUON_DECAY = 0.1
POLY_FIRST = 3.4445
POLY_SECOND = -4.775
POLY_THIRD = 2.0315
FIRST_DECAY = 0.9
SECOND_DECAY = 0.95
ADAM_RATE = 0.05
ADAM_EPSILON = 1e-08
MASKED = -1e30


def rms_factor(values):
    return lax.rsqrt(jnp.mean(values * values, axis=-1, keepdims=True) + EPSILON)


def rms_norm(values, gain):
    return values * rms_factor(values) * (1.0 + gain)


def rms_pull(values, gain, cotangent):
    factor = rms_factor(values)
    scaled = cotangent * (1.0 + gain)
    inner = jnp.mean(values * scaled, axis=-1, keepdims=True)
    d_values = factor * scaled - values * (factor * factor * factor * inner)
    return d_values, cotangent * values * factor


def rotate(values, cosine, sine):
    half = values.shape[-1] // 2
    turned = jnp.concatenate([-values[..., half:], values[..., :half]], axis=-1)
    return values * cosine + turned * sine


def rotate_back(values, cosine, sine):
    half = values.shape[-1] // 2
    turned = values * sine
    turned = jnp.concatenate([turned[..., half:], -turned[..., :half]], axis=-1)
    return values * cosine + turned


def gated(gate, upper):
    return jax.nn.gelu(gate, approximate=True) * upper


def swap(values, axis, mask):
    count = lax.axis_size(axis)
    return lax.ppermute(values, axis, [(i, i ^ mask) for i in range(count)])


def dot(left, right):
    return jnp.dot(left, right, preferred_element_type=jnp.float32)


def dot_rows(left, right):
    return lax.dot_general(
        left, right, (((0,), (0,)), ((), ())), preferred_element_type=jnp.float32
    )


def dot_cols(left, right):
    return lax.dot_general(
        left, right, (((1,), (1,)), ((), ())), preferred_element_type=jnp.float32
    )


def half_sum(part):
    half = part.shape[0] // 2
    got = swap(part[half:].astype(jnp.bfloat16), "tensor", 1)
    return (part[:half] + got.astype(jnp.float32)).astype(jnp.bfloat16)


def row_sum(part):
    kept = half_sum(part)
    got = swap(kept, "tensor", 2)
    block = kept.shape[0] // 2
    got = jnp.concatenate([got[block:], got[:block]], axis=0)
    return kept.astype(jnp.float32) + got.astype(jnp.float32)


def row_sum_own(part):
    kept = half_sum(part)
    block = kept.shape[0] // 2
    got = swap(kept[block:], "tensor", 2)
    return kept[:block].astype(jnp.float32) + got.astype(jnp.float32)


def both_halves(half):
    return jnp.concatenate([half, swap(half, "tensor", 1)], axis=0)


DATA = ("major", "minor")


def exchange(values, axis):
    return lax.all_to_all(values, axis, split_axis=0, concat_axis=0, tiled=True)


def repeated(values, count):
    return jnp.broadcast_to(values[None], (count,) + values.shape)


def gather_major(block):
    return exchange(repeated(block, lax.axis_size("major")), "major")


def gather_minor(mine):
    other = swap(mine, "minor", 1)
    even = lax.axis_index("minor") == 0
    both = jnp.stack([jnp.where(even, mine, other), jnp.where(even, other, mine)], axis=1)
    return both.reshape(-1, mine.shape[-1])


def pair_sum(part):
    low = lax.axis_index("minor")
    rows = part.shape[0] // lax.axis_size(DATA)
    blocks = part.reshape(-1, 2, rows, part.shape[1])
    away = lax.dynamic_index_in_dim(blocks, 1 - low, 1, keepdims=False).astype(jnp.bfloat16)
    here = lax.dynamic_index_in_dim(blocks, low, 1, keepdims=False)
    return (here + swap(away, "minor", 1).astype(jnp.float32)).astype(jnp.bfloat16)


def butterfly(values, axes):
    for axis in axes:
        mask = 1
        while mask < lax.axis_size(axis):
            values = values + swap(values, axis, mask)
            mask *= 2
    return values


def total_of(blocks):
    return jnp.sum(blocks.astype(jnp.float32), axis=0)


def on_chip(math_fn, shapes, *operands, flags=None, fetch=False):
    if shapes[0].shape[-2] % 16:
        if flags is None:
            return math_fn(*operands)
        return math_fn(flags, *operands)

    def kernel(*refs):
        scalars = () if flags is None else (refs[0],)
        ins = refs[len(scalars) : len(scalars) + len(operands)]
        outs = refs[len(scalars) + len(operands) :][: len(shapes)]
        if fetch:
            held = refs[len(scalars) + len(operands) + len(shapes) : -1]
            copies = [
                pltpu.make_async_copy(ref, spot, refs[-1].at[index])
                for index, (ref, spot) in enumerate(zip(ins, held))
            ]
            for copy in copies:
                copy.start()
            for copy in copies:
                copy.wait()
            ins = held
        results = math_fn(*scalars, *[ref[...] for ref in ins])
        for out, result in zip(outs, results):
            out[...] = result

    space = pl.ANY if fetch else pltpu.VMEM
    specs = [pl.BlockSpec(memory_space=space)] * len(operands)
    scratch = []
    if fetch:
        scratch = [pltpu.VMEM(operand.shape, operand.dtype) for operand in operands]
        scratch.append(pltpu.SemaphoreType.DMA((len(operands),)))
    if flags is not None:
        specs = [pl.BlockSpec(memory_space=pltpu.SMEM)] + specs
        operands_all = (flags,) + operands
    else:
        operands_all = operands
    return pl.pallas_call(
        kernel,
        out_shape=tuple(shapes),
        in_specs=specs,
        out_specs=tuple([pl.BlockSpec(memory_space=pltpu.VMEM)] * len(shapes)),
        scratch_shapes=scratch,
    )(*operands_all)


def diagonal_mask(size):
    rows = lax.broadcasted_iota(jnp.int32, (size, size), 0)
    return rows == lax.broadcasted_iota(jnp.int32, (size, size), 1)


def newton_schulz(flags, owned, near, across, far, pair_width):
    f32 = jnp.float32
    bf16 = jnp.bfloat16
    size, slot = owned.shape

    def kernel(flag_ref, own_ref, near_ref, across_ref, far_ref, out_ref, gram, product, both, inv):
        turned = flag_ref[0] == 1

        @pl.when(jnp.logical_not(turned))
        def _():
            total = dot_cols(own_ref[...], own_ref[...])
            for ref in (near_ref, across_ref, far_ref):
                total = total + dot_cols(ref[...], ref[...])
            norm = jnp.sum(jnp.where(diagonal_mask(size), total, 0.0))
            inverse = 1.0 / (jnp.sqrt(jnp.full((1, slot), norm, f32)) + 1e-07)
            inv[...] = inverse
            gram[...] = total * (inverse[:, :1] * inverse[:, :1])

        @pl.when(turned)
        def _():
            total = own_ref[...].astype(f32)
            for ref in (near_ref, across_ref, far_ref):
                total = total + ref[...].astype(f32)
            joined = total.astype(bf16)
            both[...] = joined
            wide = joined.astype(f32)
            squares = jnp.sum(wide * wide, axis=0, keepdims=True)
            lane = lax.broadcasted_iota(jnp.int32, (1, slot), 1)
            left = jnp.sum(jnp.where(lane < pair_width, squares, 0.0))
            right = jnp.sum(jnp.where(lane < pair_width, 0.0, squares))
            norms = jnp.where(lane < pair_width, left, right)
            inverse = 1.0 / (jnp.sqrt(norms) + 1e-07)
            inv[...] = inverse
            square = dot_rows(joined, joined)
            rows = lax.broadcasted_iota(jnp.int32, (slot, slot), 0)
            cols = lax.broadcasted_iota(jnp.int32, (slot, slot), 1)
            same = (rows < pair_width) == (cols < pair_width)
            gram[...] = jnp.zeros((size, size), f32)
            gram[:slot, :slot] = jnp.where(same, square * (inverse * inverse), 0.0)

        product[...] = jnp.where(diagonal_mask(size), 1.0, 0.0)

        def step(index, carry):
            eye = diagonal_mask(size)
            square = gram[...]
            mean = jnp.sum(jnp.where(eye, square, 0.0)) / size
            shift = square - jnp.where(eye, mean, 0.0)
            level = POLY_FIRST + POLY_SECOND * mean + POLY_THIRD * mean * mean
            slope = POLY_SECOND + 2.0 * POLY_THIRD * mean
            shift16 = shift.astype(bf16)
            rest = slope * shift + POLY_THIRD * dot(shift16, shift16)
            rest16 = rest.astype(bf16)
            before = product[...]
            product[...] = level * before + dot(rest16, before.astype(bf16))

            @pl.when(index < NS_STEPS - 1)
            def _():
                wide = 2.0 * level * rest + dot(rest16, rest16)
                gram[...] = (
                    jnp.where(eye, level * level * mean, 0.0)
                    + level * level * shift
                    + mean * wide
                    + dot(wide.astype(bf16), shift16)
                )

            return carry

        lax.fori_loop(0, NS_STEPS, step, 0)
        narrow = product[...].astype(bf16)

        @pl.when(jnp.logical_not(turned))
        def _():
            out_ref[...] = (dot(narrow, own_ref[...]) * inv[...]).astype(bf16)

        @pl.when(turned)
        def _():
            out_ref[...] = (dot(both[...], narrow[:slot, :slot]) * inv[...]).astype(bf16)

    vmem = pl.BlockSpec(memory_space=pltpu.VMEM)
    return pl.pallas_call(
        kernel,
        out_shape=jax.ShapeDtypeStruct((size, slot), bf16),
        in_specs=[pl.BlockSpec(memory_space=pltpu.SMEM), vmem, vmem, vmem, vmem],
        out_specs=vmem,
        scratch_shapes=[
            pltpu.VMEM((size, size), f32),
            pltpu.VMEM((size, size), f32),
            pltpu.VMEM((size, slot), bf16),
            pltpu.VMEM((1, slot), f32),
        ],
        compiler_params=pltpu.CompilerParams(vmem_limit_bytes=24 * 1024 * 1024),
    )(flags, owned, near, across, far)


def body(
    block_in,
    d_output,
    doc_ids,
    w_query,
    w_key,
    w_value,
    w_output,
    w_gate,
    w_up,
    w_down,
    mom_query,
    mom_key,
    mom_value,
    mom_output,
    mom_gate,
    mom_up,
    mom_down,
    gains,
    adam_first,
    adam_second,
):
    f32 = jnp.float32
    bf16 = jnp.bfloat16
    tensor_count = lax.axis_size("tensor")
    data_count = lax.axis_size(DATA)
    my_data = lax.axis_index(DATA)
    my_tensor = lax.axis_index("tensor")
    own = block_in.shape[0]
    model_width = block_in.shape[1]
    head_width = w_key.shape[1]
    hidden_width = w_gate.shape[1]
    seq_len = doc_ids.shape[1]
    shard_rows = w_key.shape[0]
    assert tensor_count == 4 and doc_ids.shape[0] == 1 and w_query.shape[1] == head_width
    assert own * tensor_count == seq_len and hidden_width == 2 * head_width
    scale = head_width ** (-0.5)
    pre_attn = gains[0:model_width]
    post_attn = gains[model_width : 2 * model_width]
    pre_ffn = gains[2 * model_width : 3 * model_width]
    post_ffn = gains[3 * model_width : 4 * model_width]
    gain_q = gains[4 * model_width : 4 * model_width + head_width]
    gain_k = gains[4 * model_width + head_width :]
    first_core = (my_tensor & 1) == 0

    order = (0, 2, 1, 3)

    def pack(flags, query, key, value, output, gate, upper, down):
        half = jnp.where(flags[0] == 0, key, value)
        attn = jnp.concatenate([query, half, output], axis=1).astype(bf16)
        gate_up = jnp.concatenate([gate, upper], axis=1).astype(bf16)
        return repeated(attn, data_count), gate_up, down.astype(bf16)

    packed_attn, packed_gu, packed_d = on_chip(
        pack,
        [
            jax.ShapeDtypeStruct((data_count, shard_rows, 3 * head_width), bf16),
            jax.ShapeDtypeStruct((shard_rows, 2 * hidden_width), bf16),
            jax.ShapeDtypeStruct((shard_rows, hidden_width), bf16),
        ],
        w_query,
        w_key,
        w_value,
        w_output,
        w_gate,
        w_up,
        w_down,
        flags=(my_tensor & 1).reshape(1),
        fetch=True,
    )
    weights_attn = exchange(packed_attn, DATA).reshape(model_width, 3 * head_width)
    packed_gu, weights_attn = lax.optimization_barrier((packed_gu, weights_attn))
    major_gu = gather_major(packed_gu)
    packed_d, major_gu = lax.optimization_barrier((packed_d, major_gu))
    weights_gu = gather_minor(major_gu)
    major_d = gather_major(packed_d)
    weight_d = gather_minor(major_d)
    weight_q = weights_attn[:, :head_width]
    weight_half = weights_attn[:, head_width : 2 * head_width]
    weight_o = weights_attn[:, 2 * head_width :]
    weight_other = swap(weight_half, "tensor", 1)
    weights_qkv = jnp.concatenate(
        [
            weight_q,
            jnp.where(first_core, weight_half, weight_other),
            jnp.where(first_core, weight_other, weight_half),
        ],
        axis=1,
    )

    rows_in = jnp.concatenate([block_in, swap(block_in, "tensor", 2)], axis=0)
    normed_one = both_halves(rms_norm(rows_in, pre_attn).astype(bf16))
    cot_rows = jnp.concatenate([d_output, swap(d_output, "tensor", 2)], axis=0)
    normed_one, cot_rows = lax.optimization_barrier((normed_one, cot_rows))

    doc_blocks = doc_ids.reshape(tensor_count, own)
    docs = jnp.concatenate(
        [lax.dynamic_index_in_dim(doc_blocks, my_tensor ^ j, 0, keepdims=False) for j in order]
    )
    places = jnp.concatenate(
        [(my_tensor ^ j) * own + jnp.arange(own, dtype=jnp.int32) for j in order]
    )
    first = jnp.sum((docs[None, :] < docs[:, None]).astype(jnp.int32), axis=-1)
    offset = (places - first).astype(f32)
    freqs = ROPE_BASE ** (-(2.0 * jnp.arange(head_width // 2, dtype=f32)) / head_width)
    angles = offset[:, None] * freqs
    cosine, sine = jnp.cos(angles), jnp.sin(angles)
    cosine = jnp.concatenate([cosine, cosine], axis=-1)
    sine = jnp.concatenate([sine, sine], axis=-1)
    allowed = (docs[None, :] == docs[:, None]) & (places[None, :] <= places[:, None])

    raw = dot(normed_one, weights_qkv)
    queries = raw[:, :head_width]
    keys = raw[:, head_width : 2 * head_width]
    values = raw[:, 2 * head_width :].astype(bf16)
    query_rot = rotate(rms_norm(queries, gain_q), cosine, sine).astype(bf16)
    key_rot = rotate(rms_norm(keys, gain_k), cosine, sine).astype(bf16)
    scores = jnp.where(allowed, dot_cols(query_rot, key_rot) * scale, MASKED)
    top = jnp.max(scores, axis=-1, keepdims=True)
    log_total = top + jnp.log(jnp.sum(jnp.exp(scores - top), axis=-1, keepdims=True))
    prob_full = jnp.exp(scores - log_total)
    probs = prob_full.astype(bf16)
    heads = dot(probs, values).astype(bf16)

    attn = row_sum(dot_cols(heads, weight_o))
    middle = rows_in + rms_norm(attn, post_attn)
    normed_two = both_halves(rms_norm(middle, pre_ffn).astype(bf16))
    gate_up = dot(normed_two, weights_gu)
    gate = gate_up[:, :hidden_width]
    upper = gate_up[:, hidden_width:]
    hidden = gated(gate, upper).astype(bf16)
    branch = row_sum(dot_cols(hidden, weight_d))
    block_out = middle[:own] + rms_norm(branch[:own], post_ffn)

    d_branch, g_post_ffn = rms_pull(branch, post_ffn, cot_rows)
    branch_low = both_halves(d_branch.astype(bf16))
    pair_d = pair_sum(dot_rows(branch_low, hidden))
    arrived_d = exchange(pair_d, "major")
    d_hidden = dot(branch_low, weight_d)
    d_gate, d_upper = jax.vjp(gated, gate, upper)[1](d_hidden)
    gu_low = jnp.concatenate([d_gate.astype(bf16), d_upper.astype(bf16)], axis=1)
    pair_gu = pair_sum(dot_rows(normed_two, gu_low))
    pair_gu, arrived_d = lax.optimization_barrier((pair_gu, arrived_d))
    arrived_gu = exchange(pair_gu, "major")
    d_normed_two = row_sum(dot_cols(gu_low, weights_gu))
    d_mid_extra, g_pre_ffn = rms_pull(middle, pre_ffn, d_normed_two)
    d_middle = cot_rows + d_mid_extra
    d_attn, g_post_attn = rms_pull(attn, post_attn, d_middle)
    attn_low = both_halves(d_attn.astype(bf16))
    grad_o = dot_rows(attn_low, heads).astype(bf16)

    d_heads = dot(attn_low, weight_o).astype(bf16)
    delta = jnp.sum(d_heads.astype(f32) * heads.astype(f32), axis=-1, keepdims=True)
    d_probs = dot_cols(d_heads, values)
    d_scores = (prob_full * (d_probs - delta) * scale).astype(bf16)
    d_qrot = dot(d_scores, key_rot)
    d_krot = dot_rows(d_scores, query_rot)
    d_vals = dot_rows(probs, d_heads)
    d_queries, g_query = rms_pull(queries, gain_q, rotate_back(d_qrot, cosine, sine))
    d_keys, g_key = rms_pull(keys, gain_k, rotate_back(d_krot, cosine, sine))
    qkv_low = jnp.concatenate(
        [d_queries.astype(bf16), d_keys.astype(bf16), d_vals.astype(bf16)], axis=1
    )
    grad_qkv = dot_rows(normed_one, qkv_low).astype(bf16)
    grad_attn = jnp.concatenate([grad_qkv, grad_o], axis=1)
    grad_attn, arrived_gu = lax.optimization_barrier((grad_attn, arrived_gu))
    arrived_attn = exchange(grad_attn.reshape(data_count, shard_rows, -1), DATA)

    d_normed_one = row_sum_own(dot_cols(qkv_low, weights_qkv))
    d_in_extra, g_pre_attn = rms_pull(block_in, pre_attn, d_normed_one)
    d_input = d_middle[:own] + d_in_extra
    gain_term = jnp.concatenate(
        [
            jnp.sum(g_pre_attn, axis=0),
            jnp.sum(g_post_attn[:own], axis=0),
            jnp.sum(g_pre_ffn[:own], axis=0),
            jnp.sum(g_post_ffn[:own], axis=0),
            jnp.sum(g_query, axis=0),
            jnp.sum(g_key, axis=0),
        ]
    )

    slot = hidden_width
    owners = [index * data_count // 6 for index in range(6)]

    def advance(flags, moved_d, moved_gu, moved_attn, *moments):
        m_query, m_key, m_value, m_output, m_gate, m_up, m_down = moments
        low = total_of(moved_attn)
        wide = total_of(moved_gu)
        terms = (
            low[:, :head_width],
            low[:, head_width : 3 * head_width],
            low[:, 3 * head_width :],
            wide[:, :hidden_width],
            wide[:, hidden_width:],
            total_of(moved_d),
        )
        share = jnp.where(flags[0] == 0, 1.0, 0.0)
        held = (
            m_query,
            jnp.concatenate([m_key, m_value], axis=1) * share,
            m_output,
            m_gate,
            m_up,
            m_down,
        )
        moved = [MUON_BETA * moment + term for moment, term in zip(held, terms)]
        blocks = []
        for index in range(data_count):
            if index not in owners:
                blocks.append(jnp.zeros((shard_rows, slot), bf16))
                continue
            which = owners.index(index)
            push = (terms[which] + MUON_BETA * moved[which]).astype(bf16)
            if push.shape[1] < slot:
                empty = jnp.zeros((shard_rows, slot - push.shape[1]), bf16)
                push = jnp.concatenate([push, empty], axis=1)
            blocks.append(push)
        keep = (0, 2, 3, 4, 5)
        return (
            (jnp.stack(blocks),)
            + tuple(terms)
            + tuple(moved[index] for index in keep)
        )

    def rows_of(width):
        return jax.ShapeDtypeStruct((shard_rows, width), f32)

    widths = (head_width, 2 * head_width, head_width, hidden_width, hidden_width, hidden_width)
    made = on_chip(
        advance,
        [jax.ShapeDtypeStruct((data_count, shard_rows, slot), bf16)]
        + [rows_of(width) for width in widths]
        + [rows_of(widths[index]) for index in (0, 2, 3, 4, 5)],
        arrived_d,
        arrived_gu,
        arrived_attn,
        mom_query,
        mom_key,
        mom_value,
        mom_output,
        mom_gate,
        mom_up,
        mom_down,
        flags=my_tensor.reshape(1),
        fetch=True,
    )
    outgoing, sum_query, part_kv, sum_output, sum_gate, sum_up, sum_down = made[:7]
    moved_query, moved_output, moved_gate, moved_up, moved_down = made[7:]

    owned = exchange(outgoing, DATA).reshape(data_count * shard_rows, slot)

    sum_kv = part_kv + swap(part_kv, "tensor", 1)
    sum_kv = sum_kv + swap(sum_kv, "tensor", 2)
    sum_key, sum_value = sum_kv[:, :head_width], sum_kv[:, head_width:]
    moved_key = MUON_BETA * mom_key + sum_key
    moved_value = MUON_BETA * mom_value + sum_value
    gain_half = butterfly(gain_term, ("tensor",))
    owned, gain_half, d_input = lax.optimization_barrier((owned, gain_half, d_input))
    across = swap(owned, "tensor", 2)
    grad_gains = butterfly(gain_half, ("minor", "major"))
    across, grad_gains = lax.optimization_barrier((across, grad_gains))
    near = swap(owned, "tensor", 1)
    far = swap(across, "tensor", 1)
    turned = (my_data == owners[1]).astype(jnp.int32).reshape(1)
    ortho = newton_schulz(turned, owned, near, across, far, head_width)
    returned = exchange(ortho.reshape(data_count, shard_rows, slot), DATA)

    weights = (w_query, w_key, w_value, w_output, w_gate, w_up, w_down)
    whole_cols = [
        weights[index].shape[1] * (1 if index in (1, 2) else tensor_count) for index in range(7)
    ]
    places_of = ((0, 0), (1, 0), (1, head_width), (2, 0), (3, 0), (4, 0), (5, 0))

    def renew(back, *held):
        results = []
        for index, weight in enumerate(held):
            which, start = places_of[index]
            update = back[owners[which]][:, start : start + weight.shape[1]].astype(f32)
            factor = 0.2 * math.sqrt(max(model_width, whole_cols[index]))
            results.append(weight - MUON_RATE * (factor * update + MUON_DECAY * weight))
        return tuple(results)

    updated = on_chip(
        renew, [rows_of(weight.shape[1]) for weight in weights], returned, *weights, fetch=True
    )
    next_first = FIRST_DECAY * adam_first + (1.0 - FIRST_DECAY) * grad_gains
    next_second = SECOND_DECAY * adam_second + (1.0 - SECOND_DECAY) * grad_gains * grad_gains
    first_fix = 1.0 - FIRST_DECAY**STEP
    second_fix = 1.0 - SECOND_DECAY**STEP
    new_gains = gains - ADAM_RATE * (next_first / first_fix) / (
        jnp.sqrt(next_second / second_fix) + ADAM_EPSILON
    )
    return (
        block_out,
        d_input,
        sum_query,
        sum_key,
        sum_value,
        sum_output,
        sum_gate,
        sum_up,
        sum_down,
        grad_gains,
        *updated,
        moved_query,
        moved_key,
        moved_value,
        moved_output,
        moved_gate,
        moved_up,
        moved_down,
        new_gains,
        next_first,
        next_second,
    )


def solution(mesh):
    tensor_count = mesh.shape["tensor"]
    split = Mesh(
        mesh.devices.reshape(-1, 2, tensor_count), ("major", "minor", "tensor")
    )
    rows = P(("major", "minor", "tensor"), None)
    both = P(DATA, "tensor")
    data = P(DATA, None)
    matrices = (both, data, data, both, both, both, both)

    return jax.shard_map(
        body,
        mesh=split,
        in_specs=(rows, rows, data) + matrices + matrices + (P(), P(), P()),
        out_specs=(rows, rows) + matrices + (P(),) + matrices + matrices + (P(), P(), P()),
        check_vma=False,
    )
```

profile of v0, /device:TPU:0, one launch (start us, length us, event | category | flops | bytes accessed | tf_op | source)
XLA Modules:
  0.0 288.3 jit_solution(5827391627215930556)
XLA Ops:
  0.7 2.4 shard_map.403
  3.1 7.3 %all-to-all-start = ((bf16[8,80,768]{2,1,0:T(8,128)(2,1)}), bf16[8,80,768]{2,1,0:T(8,128)(2,1)S(1)}, u32[]{:S(2)}, u32[]{:S(2)}) async-start(bf16[8,80,768]{2,1,0:T(8,128)(2,1)} %get-tuple-element.66), calls=%async_computation | async-start | bytes 1966080 | tf_op jit(solution)/shard_map/all_to_all | solution.py:113
  10.5 1.6 collective-permute-start
  14.5 6.7 %collective-permute-done = f32[128,640]{1,0:T(8,128)} collective-permute-done((f32[128,640]{1,0:T(8,128)S(1)}, f32[128,640]{1,0:T(8,128)}, u32[]{:S(2)}, u32[]{:S(2)}) %collective-permute-start) | collective-permute-done | bytes 327712 | tf_op jit(solution)/shard_map/ppermute | solution.py:65
  22.6 12.3 %all-to-all-done = bf16[8,80,768]{2,1,0:T(8,128)(2,1)S(1)} async-done(((bf16[8,80,768]{2,1,0:T(8,128)(2,1)}), bf16[8,80,768]{2,1,0:T(8,128)(2,1)S(1)}, u32[]{:S(2)}, u32[]{:S(2)}) %all-to-all-start) | async-done | bytes 983072 | tf_op jit(solution)/shard_map/all_to_all | solution.py:113
  42.5 1.5 fusion.48
  47.0 4.2 %all-to-all-start.1 = ((bf16[4,80,1024]{2,1,0:T(8,128)(2,1)}), bf16[4,80,1024]{2,1,0:T(8,128)(2,1)}, u32[]{:S(2)}, u32[]{:S(2)}) async-start(bf16[4,80,1024]{2,1,0:T(8,128)(2,1)} %broadcast_in_dim.8), calls=%async_computation.1 | async-start | bytes 1310720 | tf_op jit(solution)/shard_map/all_to_all | solution.py:113
  51.2 2.0 fusion.19
  53.2 1.5 collective-permute-start.5
  54.7 8.8 %collective-permute-done.5 = bf16[256,640]{1,0:T(8,128)(2,1)} collective-permute-done((bf16[256,640]{1,0:T(8,128)(2,1)}, bf16[256,640]{1,0:T(8,128)(2,1)}, u32[]{:S(2)}, u32[]{:S(2)}) %collective-permute-start.5) | collective-permute-done | bytes 327712 | tf_op jit(solution)/shard_map/ppermute | solution.py:65
  66.4 3.0 %all-to-all-done.1 = bf16[4,80,1024]{2,1,0:T(8,128)(2,1)} async-done(((bf16[4,80,1024]{2,1,0:T(8,128)(2,1)}), bf16[4,80,1024]{2,1,0:T(8,128)(2,1)}, u32[]{:S(2)}, u32[]{:S(2)}) %all-to-all-start.1) | async-done | bytes 655392 | tf_op jit(solution)/shard_map/all_to_all | solution.py:113
  69.3 1.4 collective-permute-start.7
  71.5 4.3 %all-to-all-start.2 = ((bf16[4,80,512]{2,1,0:T(8,128)(2,1)}), bf16[4,80,512]{2,1,0:T(8,128)(2,1)}, u32[]{:S(2)}, u32[]{:S(2)}) async-start(bf16[4,80,512]{2,1,0:T(8,128)(2,1)} %broadcast_in_dim.9), calls=%async_computation.2 | async-start | bytes 655360 | tf_op jit(solution)/shard_map/all_to_all | solution.py:113
  75.8 1.5 multiply_reduce_fusion.4
  79.0 6.6 %all-to-all-done.2 = bf16[4,80,512]{2,1,0:T(8,128)(2,1)} async-done(((bf16[4,80,512]{2,1,0:T(8,128)(2,1)}), bf16[4,80,512]{2,1,0:T(8,128)(2,1)}, u32[]{:S(2)}, u32[]{:S(2)}) %all-to-all-start.2) | async-done | bytes 327712 | tf_op jit(solution)/shard_map/all_to_all | solution.py:113
  86.3 1.4 select_bitcast_fusion.1
  87.8 2.5 fusion.36
  91.7 1.7 collective-permute-done.8
  95.3 1.6 collective-permute-done.9
  97.0 1.6 collective-permute-start.10
  98.6 8.3 %collective-permute-done.10 = bf16[256,640]{1,0:T(8,128)(2,1)S(1)} collective-permute-done((bf16[256,640]{1,0:T(8,128)(2,1)S(1)}, bf16[256,640]{1,0:T(8,128)(2,1)S(1)}, u32[]{:S(2)}, u32[]{:S(2)}) %collective-permute-start.10) | collective-permute-done | bytes 327712 | tf_op jit(solution)/shard_map/ppermute | solution.py:65
  108.3 2.0 collective-permute-done.11
  110.3 3.1 %fusion.11 = (bf16[512,512]{1,0:T(8,128)(2,1)S(1)}, bf16[512,512]{1,0:T(8,128)(2,1)S(1)}) fusion(f32[512,1024]{1,0:T(8,128)} %copy-done.3, bf16[640,512]{1,0:T(8,128)(2,1)} %bitcast.80, bf16[256,640]{1,0:T(8,128)(2,1)} %collective-permute-done.11, bf16[256,640]{1,0:T(8,128)(2,1)} %get-tuple-element.145), kind=kOutput, calls=%fused_computation.24 | convolution fusion | flops 343146496 | bytes 4456448 | tf_op jit(solution)/shard_map/dot_general | solution.py:69
  114.7 1.6 fusion.34
  117.2 2.0 fusion.14
  120.0 1.5 collective-permute-start.15
  122.5 1.3 collective-permute-start.12
  123.8 3.3 %collective-permute-done.13 = bf16[4,80,512]{2,1,0:T(8,128)(2,1)S(1)} collective-permute-done((bf16[4,80,512]{2,1,0:T(8,128)(2,1)S(1)}, bf16[4,80,512]{2,1,0:T(8,128)(2,1)S(1)}, u32[]{:S(2)}, u32[]{:S(2)}) %collective-permute-start.13) | collective-permute-done | bytes 327712 | tf_op jit(solution)/shard_map/ppermute | solution.py:65
  127.9 4.1 %all-to-all-start.3 = ((bf16[4,80,512]{2,1,0:T(8,128)(2,1)}), bf16[4,80,512]{2,1,0:T(8,128)(2,1)}, u32[]{:S(2)}, u32[]{:S(2)}) async-start(bf16[4,80,512]{2,1,0:T(8,128)(2,1)} %fusion.20), calls=%async_computation.3 | async-start | bytes 655360 | tf_op jit(solution)/shard_map/all_to_all | solution.py:113
  133.1 1.4 multiply_reduce_fusion.1
  134.6 2.6 multiply_reduce_fusion
  137.3 2.1 subtract_convert_fusion
  139.4 1.2 collective-permute-done.12
  140.6 2.1 fusion.3
  142.8 4.3 %all-to-all-start.4 = ((bf16[4,80,1024]{2,1,0:T(8,128)(2,1)}), bf16[4,80,1024]{2,1,0:T(8,128)(2,1)}, u32[]{:S(2)}, u32[]{:S(2)}) async-start(bf16[4,80,1024]{2,1,0:T(8,128)(2,1)} %fusion.3), calls=%async_computation.4 | async-start | bytes 1310720 | tf_op jit(solution)/shard_map/all_to_all | solution.py:113
  147.1 1.6 multiply_reduce_fusion.11
  152.3 1.5 convolution_convert_fusion.1
  156.1 1.3 pad_maximum_fusion.1
  157.4 7.4 %all-to-all-done.4.refs_2_ = bf16[4,80,1024]{2,1,0:T(8,128)(2,1)} async-done(((bf16[4,80,1024]{2,1,0:T(8,128)(2,1)}), bf16[4,80,1024]{2,1,0:T(8,128)(2,1)}, u32[]{:S(2)}, u32[]{:S(2)}) %all-to-all-start.4) | async-done | bytes 655392 | tf_op jit(solution)/shard_map/all_to_all | solution.py:113
  164.8 3.9 %all-to-all-start.5 = ((bf16[8,80,1024]{2,1,0:T(8,128)(2,1)}), bf16[8,80,1024]{2,1,0:T(8,128)(2,1)S(1)}, u32[]{:S(2)}, u32[]{:S(2)}) async-start(bf16[8,80,1024]{2,1,0:T(8,128)(2,1)} %bitcast.22), calls=%async_computation.5 | async-start | bytes 2621440 | tf_op jit(solution)/shard_map/all_to_all | solution.py:113
  168.9 1.8 fusion.37
  171.0 1.4 collective-permute-done.17
  172.6 1.6 collective-permute-start.18
  175.0 3.9 %collective-permute-done.18 = bf16[128,640]{1,0:T(8,128)(2,1)S(1)} collective-permute-done((bf16[128,640]{1,0:T(8,128)(2,1)S(1)}, bf16[128,640]{1,0:T(8,128)(2,1)S(1)}, u32[]{:S(2)}, u32[]{:S(2)}) %collective-permute-start.18) | collective-permute-done | bytes 163872 | tf_op jit(solution)/shard_map/ppermute | solution.py:65
  179.0 20.4 %all-to-all-done.5.refs_3_ = bf16[8,80,1024]{2,1,0:T(8,128)(2,1)S(1)} async-done(((bf16[8,80,1024]{2,1,0:T(8,128)(2,1)}), bf16[8,80,1024]{2,1,0:T(8,128)(2,1)S(1)}, u32[]{:S(2)}, u32[]{:S(2)}) %all-to-all-start.5) | async-done | bytes 1310752 | tf_op jit(solution)/shard_map/all_to_all | solution.py:113
  200.5 3.3 %shard_map.404 = (bf16[8,80,512]{2,1,0:T(8,128)(2,1)}, f32[80,256]{1,0:T(8,128)}, f32[80,512]{1,0:T(8,128)}, f32[80,256]{1,0:T(8,128)}, f32[80,512]{1,0:T(8,128)...) custom-call(s32[1]{0:T(128)} %bitcast.15.refs_0_, ...), custom_call_target="tpu_custom_call" | custom-call | tf_op jit(solution)/shard_map/pallas_call | solution.py:189
  203.9 3.7 %all-to-all-start.6 = ((bf16[8,80,512]{2,1,0:T(8,128)(2,1)}), bf16[8,80,512]{2,1,0:T(8,128)(2,1)S(1)}, u32[]{:S(2)}, u32[]{:S(2)}) async-start(bf16[8,80,512]{2,1,0:T(8,128)(2,1)} %get-tuple-element.77), calls=%async_computation.6 | async-start | bytes 1310720 | tf_op jit(solution)/shard_map/all_to_all | solution.py:113
  209.9 1.5 collective-permute-start.20
  211.4 2.2 collective-permute-done.20
  213.6 11.5 %all-to-all-done.6 = bf16[8,80,512]{2,1,0:T(8,128)(2,1)S(1)} async-done(((bf16[8,80,512]{2,1,0:T(8,128)(2,1)}), bf16[8,80,512]{2,1,0:T(8,128)(2,1)S(1)}, u32[]{:S(2)}, u32[]{:S(2)}) %all-to-all-start.6) | async-done | bytes 655392 | tf_op jit(solution)/shard_map/all_to_all | solution.py:113
  225.1 1.5 collective-permute-start.23
  226.6 1.5 collective-permute-start.24
  228.0 2.2 collective-permute-done.24
  230.9 3.1 %collective-permute-done.25 = f32[3072]{0:T(1024)S(1)} collective-permute-done((f32[3072]{0:T(1024)S(1)}, f32[3072]{0:T(1024)S(1)}, u32[]{:S(2)}, u32[]{:S(2)}) %collective-permute-start.25) | collective-permute-done | bytes 12320 | tf_op jit(solution)/shard_map/ppermute | solution.py:65
  234.0 4.7 %collective-permute-done.26 = f32[3072]{0:T(1024)S(1)} collective-permute-done((f32[3072]{0:T(1024)S(1)}, f32[3072]{0:T(1024)S(1)}, u32[]{:S(2)}, u32[]{:S(2)}) %collective-permute-start.26) | collective-permute-done | bytes 12320 | tf_op jit(solution)/shard_map/ppermute | solution.py:65
  238.7 1.6 collective-permute-done.23.across_ref
  240.3 2.1 collective-permute-done.28.far_ref
  242.4 19.7 %shard_map.405 = bf16[640,512]{1,0:T(8,128)(2,1)} custom-call(s32[1]{0:T(128)} %bitcast.24.flag_ref, bf16[640,512]{1,0:T(8,128)(2,1)S(1)} %bitcast.72, bf16[640,512]{1,0:T(8,128)(2,1)S(1)} %collective-permute-done.27.near_ref, bf16[640,512]{1,0:T(8,128)(2,1)S(1)} %collective-permute-done.23.across_ref, bf16[640,512]{1,0:T(8,128)(2,1)S(1)} %collective-permute-done.28.far_ref), custom_call_target="tpu_custom_call" | custom-call | tf_op jit(solution)/shard_map/pallas_call | solution.py:282
  262.2 5.2 %all-to-all-start.7 = ((bf16[8,80,512]{2,1,0:T(8,128)(2,1)}), bf16[8,80,512]{2,1,0:T(8,128)(2,1)S(1)}, u32[]{:S(2)}, u32[]{:S(2)}) async-start(bf16[8,80,512]{2,1,0:T(8,128)(2,1)} %bitcast.25), calls=%async_computation.7 | async-start | bytes 1310720 | tf_op jit(solution)/shard_map/all_to_all | solution.py:113
  267.5 1.4 collective-permute-done.21
  268.9 1.6 collective-permute-start.22
  270.4 4.8 %collective-permute-done.22 = f32[80,512]{1,0:T(8,128)S(1)} collective-permute-done((f32[80,512]{1,0:T(8,128)S(1)}, f32[80,512]{1,0:T(8,128)S(1)}, u32[]{:S(2)}, u32[]{:S(2)}) %collective-permute-start.22) | collective-permute-done | bytes 163872 | tf_op jit(solution)/shard_map/ppermute | solution.py:65
  276.6 8.4 %all-to-all-done.7.refs_0_ = bf16[8,80,512]{2,1,0:T(8,128)(2,1)S(1)} async-done(((bf16[8,80,512]{2,1,0:T(8,128)(2,1)}), bf16[8,80,512]{2,1,0:T(8,128)(2,1)S(1)}, u32[]{:S(2)}, u32[]{:S(2)}) %all-to-all-start.7) | async-done | bytes 655392 | tf_op jit(solution)/shard_map/all_to_all | solution.py:113
  285.8 2.3 shard_map.406
  (292 shorter events, 44.3 us)
Async XLA Ops:
  0.7 9.8 %copy-start.14 = (f32[128,640]{1,0:T(8,128)S(1)}, f32[128,640]{1,0:T(8,128)}, u32[]{:S(2)}) copy-start(f32[128,640]{1,0:T(8,128)} %param.20) | copy-start | bytes 983044
  0.7 11.3 %copy-start.39 = (f32[128,640]{1,0:T(8,128)S(1)}, f32[128,640]{1,0:T(8,128)}, u32[]{:S(2)}) copy-start(f32[128,640]{1,0:T(8,128)} %param.21) | copy-start | bytes 983044
  0.7 11.9 %copy-start.78 = (s32[1,512]{1,0:T(1,128)S(1)}, s32[1,512]{1,0:T(1,128)}, u32[]{:S(2)}) copy-start(s32[1,512]{1,0:T(1,128)} %param.22) | copy-start | bytes 6148
  3.1 10.7 %copy-start.50 = (f32[3072]{0:T(1024)S(1)}, f32[3072]{0:T(1024)}, u32[]{:S(2)}) copy-start(f32[3072]{0:T(1024)} %param.37) | copy-start | bytes 36868
  3.1 31.7 %all-to-all-start = ((bf16[8,80,768]{2,1,0:T(8,128)(2,1)}), bf16[8,80,768]{2,1,0:T(8,128)(2,1)S(1)}, u32[]{:S(2)}, u32[]{:S(2)}) async-start(bf16[8,80,768]{2,1,0:T(8,128)(2,1)} %get-tuple-element.66), calls=%async_computation | async-start | bytes 1966080 | tf_op jit(solution)/shard_map/all_to_all | solution.py:113
  10.5 10.8 %collective-permute-start = (f32[128,640]{1,0:T(8,128)S(1)}, f32[128,640]{1,0:T(8,128)}, u32[]{:S(2)}, u32[]{:S(2)}) collective-permute-start(f32[128,640]{1,0:T(8,128)S(1)} %copy-done.14), channel_id=1, source_target_pairs={{0,2},{1,3},{2,0},{3,1},{4,6},{5,7},{6,4},{7,5},{8,10},{9,11},{10,... | collective-permute-start | bytes 983048 | tf_op jit(solution)/shard_map/ppermute | solution.py:65
  12.0 23.6 %collective-permute-start.2 = (f32[128,640]{1,0:T(8,128)S(1)}, f32[128,640]{1,0:T(8,128)S(1)}, u32[]{:S(2)}, u32[]{:S(2)}) collective-permute-start(f32[128,640]{1,0:T(8,128)S(1)} %copy-done.39), channel_id=1, source_target_pairs={{0,2},{1,3},{2,0},{3,1},{4,6},{5,7},{6,4},{7,5},{8,10},{9,11},{10,... | collective-permute-start | bytes 983048 | tf_op jit(solution)/shard_map/ppermute | solution.py:65
  13.8 27.2 %copy-start.19 = (f32[512,128]{1,0:T(8,128)}, f32[512,128]{1,0:T(8,128)S(1)}, u32[]{:S(2)}) copy-start(f32[512,128]{1,0:T(8,128)S(1)} %get-tuple-element.178) | copy-start | bytes 786436
  13.9 27.2 %copy-start.21 = (f32[512,128]{1,0:T(8,128)}, f32[512,128]{1,0:T(8,128)S(1)}, u32[]{:S(2)}) copy-start(f32[512,128]{1,0:T(8,128)S(1)} %get-tuple-element.177) | copy-start | bytes 786436
  13.9 8.6 %copy-start.51 = (f32[640]{0:T(1024)}, f32[640]{0:T(1024)S(1)}, u32[]{:S(2)}) copy-start(f32[640]{0:T(1024)S(1)} %get-tuple-element.174) | copy-start | bytes 7684
  22.2 13.4 %copy-start.4 = (f32[256,640]{1,0:T(8,128)}, f32[256,640]{1,0:T(8,128)S(1)}, u32[]{:S(2)}) copy-start(f32[256,640]{1,0:T(8,128)S(1)} %constant_dynamic-update-slice_fusion) | copy-start | bytes 1966084
  22.5 13.2 %collective-permute-start.1 = (bf16[256,640]{1,0:T(8,128)(2,1)S(1)}, bf16[256,640]{1,0:T(8,128)(2,1)}, u32[]{:S(2)}, u32[]{:S(2)}) collective-permute-start(bf16[256,640]{1,0:T(8,128)(2,1)S(1)} %multiply_convert_fusion.3), channel_id=1, source_target_pairs={{0,1},{1,0},{2,3},{3,2},{4,5},{5,4},{6,7},{7,6},{8,9},{9,8},{10,11... | collective-permute-start | bytes 983048 | tf_op jit(solution)/shard_map/ppermute | solution.py:65
  35.6 2.0 collective-permute-start.3
  35.6 4.8 %copy-start.64 = (f32[256]{0:T(256)}, f32[256]{0:T(256)S(1)}, u32[]{:S(2)}) copy-start(f32[256]{0:T(256)S(1)} %get-tuple-element.175) | copy-start | bytes 3076
  35.6 4.8 %copy-start.66 = (f32[256]{0:T(256)}, f32[256]{0:T(256)S(1)}, u32[]{:S(2)}) copy-start(f32[256]{0:T(256)S(1)} %get-tuple-element.176) | copy-start | bytes 3076
  45.9 5.2 %collective-permute-start.4 = (bf16[256,640]{1,0:T(8,128)(2,1)}, bf16[256,640]{1,0:T(8,128)(2,1)}, u32[]{:S(2)}, u32[]{:S(2)}) collective-permute-start(bf16[256,640]{1,0:T(8,128)(2,1)} %slice.318), channel_id=1, source_target_pairs={{0,1},{1,0},{2,3},{3,2},{4,5},{5,4},{6,7},{7,6},{8,9},{9,8},{10,11... | collective-permute-start | bytes 983048 | tf_op jit(solution)/shard_map/ppermute | solution.py:65
  47.0 22.3 %all-to-all-start.1 = ((bf16[4,80,1024]{2,1,0:T(8,128)(2,1)}), bf16[4,80,1024]{2,1,0:T(8,128)(2,1)}, u32[]{:S(2)}, u32[]{:S(2)}) async-start(bf16[4,80,1024]{2,1,0:T(8,128)(2,1)} %broadcast_in_dim.8), calls=%async_computation.1 | async-start | bytes 1310720 | tf_op jit(solution)/shard_map/all_to_all | solution.py:113
  51.2 19.6 %copy-start.49 = (bf16[80,512]{1,0:T(8,128)(2,1)S(1)}, bf16[80,512]{1,0:T(8,128)(2,1)}, u32[]{:S(2)}) copy-start(bf16[80,512]{1,0:T(8,128)(2,1)} %get-tuple-element.71) | copy-start | bytes 245764
  53.2 10.3 %collective-permute-start.5 = (bf16[256,640]{1,0:T(8,128)(2,1)}, bf16[256,640]{1,0:T(8,128)(2,1)}, u32[]{:S(2)}, u32[]{:S(2)}) collective-permute-start(bf16[256,640]{1,0:T(8,128)(2,1)} %fusion.19), channel_id=1, source_target_pairs={{0,2},{1,3},{2,0},{3,1},{4,6},{5,7},{6,4},{7,5},{8,10},{9,11},{10,... | collective-permute-start | bytes 983048 | tf_op jit(solution)/shard_map/ppermute | solution.py:65
  66.3 10.9 %copy-start.72 = (f32[256]{0:T(256)}, f32[256]{0:T(256)S(1)}, u32[]{:S(2)}) copy-start(f32[256]{0:T(256)S(1)} %multiply_reduce_fusion.5) | copy-start | bytes 3076
  66.4 70.9 %copy-start.70 = (f32[256]{0:T(256)}, f32[256]{0:T(256)S(1)}, u32[]{:S(2)}) copy-start(f32[256]{0:T(256)S(1)} %add_rsqrt_fusion.4) | copy-start | bytes 3076
  69.3 16.9 %collective-permute-start.7 = (bf16[4,80,1024]{2,1,0:T(8,128)(2,1)}, bf16[4,80,1024]{2,1,0:T(8,128)(2,1)}, u32[]{:S(2)}, u32[]{:S(2)}) collective-permute-start(bf16[4,80,1024]{2,1,0:T(8,128)(2,1)} %all-to-all-done.1), channel_id=1, source_target_pairs={{0,4},{4,0},{1,5},{5,1},{2,6},{6,2},{3,7},{7,3},{8,12},{12,8},{9,1... | collective-permute-start | bytes 1966088 | tf_op jit(solution)/shard_map/ppermute | solution.py:65
  71.5 14.2 %all-to-all-start.2 = ((bf16[4,80,512]{2,1,0:T(8,128)(2,1)}), bf16[4,80,512]{2,1,0:T(8,128)(2,1)}, u32[]{:S(2)}, u32[]{:S(2)}) async-start(bf16[4,80,512]{2,1,0:T(8,128)(2,1)} %broadcast_in_dim.9), calls=%async_computation.2 | async-start | bytes 655360 | tf_op jit(solution)/shard_map/all_to_all | solution.py:113
  77.3 57.3 %copy-start.71 = (f32[256]{0:T(256)}, f32[256]{0:T(256)S(1)}, u32[]{:S(2)}) copy-start(f32[256]{0:T(256)S(1)} %add_rsqrt_fusion.3) | copy-start | bytes 3076
  79.0 8.8 %collective-permute-start.6 = (bf16[256,640]{1,0:T(8,128)(2,1)}, bf16[256,640]{1,0:T(8,128)(2,1)}, u32[]{:S(2)}, u32[]{:S(2)}) collective-permute-start(bf16[256,640]{1,0:T(8,128)(2,1)} %multiply_convert_fusion.2), channel_id=1, source_target_pairs={{0,1},{1,0},{2,3},{3,2},{4,5},{5,4},{6,7},{7,6},{8,9},{9,8},{10,11... | collective-permute-start | bytes 983048 | tf_op jit(solution)/shard_map/ppermute | solution.py:65
  85.6 7.8 %collective-permute-start.8 = (bf16[4,80,512]{2,1,0:T(8,128)(2,1)}, bf16[4,80,512]{2,1,0:T(8,128)(2,1)S(1)}, u32[]{:S(2)}, u32[]{:S(2)}) collective-permute-start(bf16[4,80,512]{2,1,0:T(8,128)(2,1)} %all-to-all-done.2), channel_id=1, source_target_pairs={{0,4},{4,0},{1,5},{5,1},{2,6},{6,2},{3,7},{7,3},{8,12},{12,8},{9,1... | collective-permute-start | bytes 983048 | tf_op jit(solution)/shard_map/ppermute | solution.py:65
  95.3 1.6 collective-permute-start.9
  97.0 9.8 %collective-permute-start.10 = (bf16[256,640]{1,0:T(8,128)(2,1)S(1)}, bf16[256,640]{1,0:T(8,128)(2,1)S(1)}, u32[]{:S(2)}, u32[]{:S(2)}) collective-permute-start(bf16[256,640]{1,0:T(8,128)(2,1)S(1)} %fusion.18), channel_id=1, source_target_pairs={{0,2},{1,3},{2,0},{3,1},{4,6},{5,7},{6,4},{7,5},{8,10},{9,11},{10,... | collective-permute-start | bytes 983048 | tf_op jit(solution)/shard_map/ppermute | solution.py:65
  107.1 6.3 %copy-start.76 = (f32[256]{0:T(256)}, f32[256]{0:T(256)S(1)}, u32[]{:S(2)}) copy-start(f32[256]{0:T(256)S(1)} %get-tuple-element.186) | copy-start | bytes 3076
  108.3 2.0 collective-permute-start.11
  108.3 5.1 %copy-start.8 = (bf16[4,2,80,1024]{3,2,1,0:T(8,128)(2,1)S(1)}, bf16[4,2,80,1024]{3,2,1,0:T(8,128)(2,1)}, u32[]{:S(2)}) copy-start(bf16[4,2,80,1024]{3,2,1,0:T(8,128)(2,1)} %copy-done.7) | copy-start | bytes 3932164
  114.6 4.6 %collective-permute-start.14 = (bf16[256,640]{1,0:T(8,128)(2,1)S(1)}, bf16[256,640]{1,0:T(8,128)(2,1)S(1)}, u32[]{:S(2)}, u32[]{:S(2)}) collective-permute-start(bf16[256,640]{1,0:T(8,128)(2,1)S(1)} %slice.316), channel_id=1, source_target_pairs={{0,1},{1,0},{2,3},{3,2},{4,5},{5,4},{6,7},{7,6},{8,9},{9,8},{10,11... | collective-permute-start | bytes 983048 | tf_op jit(solution)/shard_map/ppermute | solution.py:65
  116.4 10.6 %collective-permute-start.13 = (bf16[4,80,512]{2,1,0:T(8,128)(2,1)S(1)}, bf16[4,80,512]{2,1,0:T(8,128)(2,1)S(1)}, u32[]{:S(2)}, u32[]{:S(2)}) collective-permute-start(bf16[4,80,512]{2,1,0:T(8,128)(2,1)S(1)} %fusion.39), channel_id=1, source_target_pairs={{0,4},{4,0},{1,5},{5,1},{2,6},{6,2},{3,7},{7,3},{8,12},{12,8},{9,1... | collective-permute-start | bytes 983048 | tf_op jit(solution)/shard_map/ppermute | solution.py:65
  120.0 12.0 %collective-permute-start.15 = (bf16[256,640]{1,0:T(8,128)(2,1)}, bf16[256,640]{1,0:T(8,128)(2,1)}, u32[]{:S(2)}, u32[]{:S(2)}) collective-permute-start(bf16[256,640]{1,0:T(8,128)(2,1)} %fusion.17), channel_id=1, source_target_pairs={{0,2},{1,3},{2,0},{3,1},{4,6},{5,7},{6,4},{7,5},{8,10},{9,11},{10,... | collective-permute-start | bytes 983048 | tf_op jit(solution)/shard_map/ppermute | solution.py:65
  122.5 18.2 %collective-permute-start.12 = (bf16[4,80,1024]{2,1,0:T(8,128)(2,1)}, bf16[4,80,1024]{2,1,0:T(8,128)(2,1)}, u32[]{:S(2)}, u32[]{:S(2)}) collective-permute-start(bf16[4,80,1024]{2,1,0:T(8,128)(2,1)} %fusion.15), channel_id=1, source_target_pairs={{0,4},{4,0},{1,5},{5,1},{2,6},{6,2},{3,7},{7,3},{8,12},{12,8},{9,1... | collective-permute-start | bytes 1966088 | tf_op jit(solution)/shard_map/ppermute | solution.py:65
  127.9 14.9 %all-to-all-start.3 = ((bf16[4,80,512]{2,1,0:T(8,128)(2,1)}), bf16[4,80,512]{2,1,0:T(8,128)(2,1)}, u32[]{:S(2)}, u32[]{:S(2)}) async-start(bf16[4,80,512]{2,1,0:T(8,128)(2,1)} %fusion.20), calls=%async_computation.3 | async-start | bytes 655360 | tf_op jit(solution)/shard_map/all_to_all | solution.py:113
  134.6 6.0 %copy-start.28 = (f32[640,1024]{1,0:T(8,128)S(1)}, f32[640,1024]{1,0:T(8,128)}, u32[]{:S(2)}) copy-start(f32[640,1024]{1,0:T(8,128)} %copy-done.27) | copy-start | bytes 7864324
  139.4 7.7 %collective-permute-start.16 = (bf16[256,640]{1,0:T(8,128)(2,1)}, bf16[256,640]{1,0:T(8,128)(2,1)}, u32[]{:S(2)}, u32[]{:S(2)}) collective-permute-start(bf16[256,640]{1,0:T(8,128)(2,1)} %subtract_convert_fusion), channel_id=1, source_target_pairs={{0,1},{1,0},{2,3},{3,2},{4,5},{5,4},{6,7},{7,6},{8,9},{9,8},{10,11... | collective-permute-start | bytes 983048 | tf_op jit(solution)/shard_map/ppermute | solution.py:65
  142.8 22.0 %all-to-all-start.4 = ((bf16[4,80,1024]{2,1,0:T(8,128)(2,1)}), bf16[4,80,1024]{2,1,0:T(8,128)(2,1)}, u32[]{:S(2)}, u32[]{:S(2)}) async-start(bf16[4,80,1024]{2,1,0:T(8,128)(2,1)} %fusion.3), calls=%async_computation.4 | async-start | bytes 1310720 | tf_op jit(solution)/shard_map/all_to_all | solution.py:113
  164.8 34.6 %all-to-all-start.5 = ((bf16[8,80,1024]{2,1,0:T(8,128)(2,1)}), bf16[8,80,1024]{2,1,0:T(8,128)(2,1)S(1)}, u32[]{:S(2)}, u32[]{:S(2)}) async-start(bf16[8,80,1024]{2,1,0:T(8,128)(2,1)} %bitcast.22), calls=%async_computation.5 | async-start | bytes 2621440 | tf_op jit(solution)/shard_map/all_to_all | solution.py:113
  170.8 1.7 collective-permute-start.17
  171.0 7.9 %copy-start.15 = (f32[128,640]{1,0:T(8,128)S(1)}, f32[128,640]{1,0:T(8,128)}, u32[]{:S(2)}) copy-start(f32[128,640]{1,0:T(8,128)} %param.20) | copy-start | bytes 983044
  171.0 7.9 %copy-start.52 = (f32[640]{0:T(1024)S(1)}, f32[640]{0:T(1024)}, u32[]{:S(2)}) copy-start(f32[640]{0:T(1024)} %copy-done.51) | copy-start | bytes 7684
  172.6 6.3 %collective-permute-start.18 = (bf16[128,640]{1,0:T(8,128)(2,1)S(1)}, bf16[128,640]{1,0:T(8,128)(2,1)S(1)}, u32[]{:S(2)}, u32[]{:S(2)}) collective-permute-start(bf16[128,640]{1,0:T(8,128)(2,1)S(1)} %slice.219), channel_id=1, source_target_pairs={{0,2},{1,3},{2,0},{3,1},{4,6},{5,7},{6,4},{7,5},{8,10},{9,11},{10,... | collective-permute-start | bytes 491528 | tf_op jit(solution)/shard_map/ppermute | solution.py:65
  203.9 4.7 %copy-start.75 = (f32[256]{0:T(256)S(1)}, f32[256]{0:T(256)}, u32[]{:S(2)}) copy-start(f32[256]{0:T(256)} %get-tuple-element.106) | copy-start | bytes 3076
  203.9 4.7 %copy-start.74 = (f32[256]{0:T(256)S(1)}, f32[256]{0:T(256)}, u32[]{:S(2)}) copy-start(f32[256]{0:T(256)} %get-tuple-element.101) | copy-start | bytes 3076
  203.9 21.2 %all-to-all-start.6 = ((bf16[8,80,512]{2,1,0:T(8,128)(2,1)}), bf16[8,80,512]{2,1,0:T(8,128)(2,1)S(1)}, u32[]{:S(2)}, u32[]{:S(2)}) async-start(bf16[8,80,512]{2,1,0:T(8,128)(2,1)} %get-tuple-element.77), calls=%async_computation.6 | async-start | bytes 1310720 | tf_op jit(solution)/shard_map/all_to_all | solution.py:113
  208.6 1.2 collective-permute-start.19
  209.9 3.7 %collective-permute-start.20 = (f32[3072]{0:T(1024)S(1)}, f32[3072]{0:T(1024)S(1)}, u32[]{:S(2)}, u32[]{:S(2)}) collective-permute-start(f32[3072]{0:T(1024)S(1)} %add.327), channel_id=1, source_target_pairs={{0,2},{1,3},{2,0},{3,1},{4,6},{5,7},{6,4},{7,5},{8,10},{9,11},{10,... | collective-permute-start | bytes 36872 | tf_op jit(solution)/shard_map/ppermute | solution.py:65
  225.1 15.2 %collective-permute-start.23 = (bf16[640,512]{1,0:T(8,128)(2,1)S(1)}, bf16[640,512]{1,0:T(8,128)(2,1)S(1)}, u32[]{:S(2)}, u32[]{:S(2)}) collective-permute-start(bf16[640,512]{1,0:T(8,128)(2,1)S(1)} %bitcast.70), channel_id=1, source_target_pairs={{0,2},{1,3},{2,0},{3,1},{4,6},{5,7},{6,4},{7,5},{8,10},{9,11},{10,... | collective-permute-start | bytes 1966088 | tf_op jit(solution)/shard_map/ppermute | solution.py:65
  226.6 3.7 %collective-permute-start.24 = (f32[3072]{0:T(1024)S(1)}, f32[3072]{0:T(1024)S(1)}, u32[]{:S(2)}, u32[]{:S(2)}) collective-permute-start(f32[3072]{0:T(1024)S(1)} %add.328), channel_id=1, source_target_pairs={{0,4},{4,0},{1,5},{5,1},{2,6},{6,2},{3,7},{7,3},{8,12},{12,8},{9,1... | collective-permute-start | bytes 36872 | tf_op jit(solution)/shard_map/ppermute | solution.py:65
  230.3 3.7 %collective-permute-start.25 = (f32[3072]{0:T(1024)S(1)}, f32[3072]{0:T(1024)S(1)}, u32[]{:S(2)}, u32[]{:S(2)}) collective-permute-start(f32[3072]{0:T(1024)S(1)} %add.332), channel_id=1, source_target_pairs={{0,8},{8,0},{16,24},{24,16},{1,9},{9,1},{17,25},{25,17},{2,10},{10... | collective-permute-start | bytes 36872 | tf_op jit(solution)/shard_map/ppermute | solution.py:65
  234.0 4.7 %collective-permute-start.26 = (f32[3072]{0:T(1024)S(1)}, f32[3072]{0:T(1024)S(1)}, u32[]{:S(2)}, u32[]{:S(2)}) collective-permute-start(f32[3072]{0:T(1024)S(1)} %add.333), channel_id=1, source_target_pairs={{0,16},{8,24},{16,0},{24,8},{1,17},{9,25},{17,1},{25,9},{2,18},{10... | collective-permute-start | bytes 36872 | tf_op jit(solution)/shard_map/ppermute | solution.py:65
  234.0 6.3 %collective-permute-start.27 = (bf16[640,512]{1,0:T(8,128)(2,1)S(1)}, bf16[640,512]{1,0:T(8,128)(2,1)S(1)}, u32[]{:S(2)}, u32[]{:S(2)}) collective-permute-start(bf16[640,512]{1,0:T(8,128)(2,1)S(1)} %bitcast.71), channel_id=1, source_target_pairs={{0,1},{1,0},{2,3},{3,2},{4,5},{5,4},{6,7},{7,6},{8,9},{9,8},{10,11... | collective-permute-start | bytes 1966088 | tf_op jit(solution)/shard_map/ppermute | solution.py:65
  238.7 37.3 %copy-start.53 = (f32[3072]{0:T(1024)}, f32[3072]{0:T(1024)S(1)}, u32[]{:S(2)}) copy-start(f32[3072]{0:T(1024)S(1)} %add.334) | copy-start | bytes 36868
  240.3 2.1 collective-permute-start.28
  262.1 5.2 %copy-start.48 = (f32[80,512]{1,0:T(8,128)S(1)}, f32[80,512]{1,0:T(8,128)}, u32[]{:S(2)}) copy-start(f32[80,512]{1,0:T(8,128)} %get-tuple-element.80) | copy-start | bytes 491524
  262.2 13.1 %copy-start.37 = (f32[80,256]{1,0:T(8,128)S(1)}, f32[80,256]{1,0:T(8,128)}, u32[]{:S(2)}) copy-start(f32[80,256]{1,0:T(8,128)} %refs_5_.4) | copy-start | bytes 245764
  262.2 13.1 %copy-start.38 = (f32[80,256]{1,0:T(8,128)S(1)}, f32[80,256]{1,0:T(8,128)}, u32[]{:S(2)}) copy-start(f32[80,256]{1,0:T(8,128)} %refs_6_.4) | copy-start | bytes 245764
  262.2 13.8 %copy-start.68 = (f32[3072]{0:T(1024)S(1)}, f32[3072]{0:T(1024)}, u32[]{:S(2)}) copy-start(f32[3072]{0:T(1024)} %param.38) | copy-start | bytes 36868
  262.2 13.8 %copy-start.69 = (f32[3072]{0:T(1024)S(1)}, f32[3072]{0:T(1024)}, u32[]{:S(2)}) copy-start(f32[3072]{0:T(1024)} %param.39) | copy-start | bytes 36868
  262.2 22.8 %all-to-all-start.7 = ((bf16[8,80,512]{2,1,0:T(8,128)(2,1)}), bf16[8,80,512]{2,1,0:T(8,128)(2,1)S(1)}, u32[]{:S(2)}, u32[]{:S(2)}) async-start(bf16[8,80,512]{2,1,0:T(8,128)(2,1)} %bitcast.25), calls=%async_computation.7 | async-start | bytes 1310720 | tf_op jit(solution)/shard_map/all_to_all | solution.py:113
  267.4 1.5 collective-permute-start.21
  268.9 6.3 %collective-permute-start.22 = (f32[80,512]{1,0:T(8,128)S(1)}, f32[80,512]{1,0:T(8,128)S(1)}, u32[]{:S(2)}, u32[]{:S(2)}) collective-permute-start(f32[80,512]{1,0:T(8,128)S(1)} %add.330), channel_id=1, source_target_pairs={{0,2},{1,3},{2,0},{3,1},{4,6},{5,7},{6,4},{7,5},{8,10},{9,11},{10,... | collective-permute-start | bytes 491528 | tf_op jit(solution)/shard_map/ppermute | solution.py:65
  (55 other events, 110.3 us)
where the time goes:
time: 290 us; the launch traced here: 288 us
  waiting for transfers between devices  132 us (46%)
  starting transfers between devices  56.6 us (20%)
  other arithmetic  31.5 us (11%)
  Pallas kernels  27.8 us (10%)
  matrix products  20.9 us (7%)
  local copies, waits for them, and re-layouts  16.8 us (6%)
    all_to_all x8, waiting for transfers between devices, exchange(): return lax.all_to_all(values, axis, split_axis=0, concat_axis=0, tiled=True)  69.5 us
    ppermute x29, waiting for transfers between devices, swap(): return lax.ppermute(values, axis, [(i, i ^ mask) for i in range(count)])  63 us
    all_to_all x8, starting transfers between devices, exchange(): return lax.all_to_all(values, axis, split_axis=0, concat_axis=0, tiled=True)  37 us
    pallas_call x1, Pallas kernels, newton_schulz(): pl.pallas_call(kernel, out_shape=jax.ShapeDtypeStruct((size, slot), bf16)...  19.7 us
    ppermute x29, starting transfers between devices, swap(): return lax.ppermute(values, axis, [(i, i ^ mask) for i in range(count)])  19.6 us
    unnamed x165, local copies, waits for them, and re-layouts  9.31 us
    dot_general x6, matrix products, dot(): return jnp.dot(left, right, preferred_element_type=jnp.float32)  8.75 us
    pallas_call x3, Pallas kernels, on_chip(): pl.pallas_call(kernel, out_shape=tuple(shapes), in_specs=specs, out_specs...  8.03 us
  transfers between devices with their start and end apart: 37, of which 27 were waited for; matrix products, arithmetic and copies ran while one was open for 16% of the time, Pallas kernels for 0%

commit v1 on v0

--- a/solution.py
+++ b/solution.py
@@ -117,10 +117,6 @@
     return jnp.broadcast_to(values[None], (count,) + values.shape)
 
 
-def gather_major(block):
-    return exchange(repeated(block, lax.axis_size("major")), "major")
-
-
 def gather_minor(mine):
     other = swap(mine, "minor", 1)
     even = lax.axis_index("minor") == 0
@@ -132,9 +128,9 @@
     low = lax.axis_index("minor")
     rows = part.shape[0] // lax.axis_size(DATA)
     blocks = part.reshape(-1, 2, rows, part.shape[1])
-    away = lax.dynamic_index_in_dim(blocks, 1 - low, 1, keepdims=False).astype(jnp.bfloat16)
+    away = swap(lax.dynamic_index_in_dim(blocks, 1 - low, 1, keepdims=False), "minor", 1)
     here = lax.dynamic_index_in_dim(blocks, low, 1, keepdims=False)
-    return (here + swap(away, "minor", 1).astype(jnp.float32)).astype(jnp.bfloat16)
+    return (here.astype(jnp.float32) + away.astype(jnp.float32)).astype(jnp.bfloat16)
 
 
 def butterfly(values, axes):
@@ -150,7 +146,7 @@
     return jnp.sum(blocks.astype(jnp.float32), axis=0)
 
 
-def on_chip(math_fn, shapes, *operands, flags=None, fetch=False):
+def on_chip(math_fn, shapes, *operands, flags=None, fetch=None, limit=None):
     if shapes[0].shape[-2] % 16:
         if flags is None:
             return math_fn(*operands)
@@ -160,27 +156,27 @@
         scalars = () if flags is None else (refs[0],)
         ins = refs[len(scalars) : len(scalars) + len(operands)]
         outs = refs[len(scalars) + len(operands) :][: len(shapes)]
-        if fetch:
+        if fetch is not None:
             held = refs[len(scalars) + len(operands) + len(shapes) : -1]
             copies = [
                 pltpu.make_async_copy(ref, spot, refs[-1].at[index])
-                for index, (ref, spot) in enumerate(zip(ins, held))
+                for index, (ref, spot) in enumerate(zip(ins[fetch:], held))
             ]
             for copy in copies:
                 copy.start()
             for copy in copies:
                 copy.wait()
-            ins = held
+            ins = ins[:fetch] + held
         results = math_fn(*scalars, *[ref[...] for ref in ins])
         for out, result in zip(outs, results):
             out[...] = result
 
-    space = pl.ANY if fetch else pltpu.VMEM
-    specs = [pl.BlockSpec(memory_space=space)] * len(operands)
+    specs = [pl.BlockSpec(memory_space=pltpu.VMEM)] * len(operands)
     scratch = []
-    if fetch:
-        scratch = [pltpu.VMEM(operand.shape, operand.dtype) for operand in operands]
-        scratch.append(pltpu.SemaphoreType.DMA((len(operands),)))
+    if fetch is not None:
+        specs[fetch:] = [pl.BlockSpec(memory_space=pl.ANY)] * (len(operands) - fetch)
+        scratch = [pltpu.VMEM(operand.shape, operand.dtype) for operand in operands[fetch:]]
+        scratch.append(pltpu.SemaphoreType.DMA((len(operands) - fetch,)))
     if flags is not None:
         specs = [pl.BlockSpec(memory_space=pltpu.SMEM)] + specs
         operands_all = (flags,) + operands
@@ -192,6 +188,7 @@
         in_specs=specs,
         out_specs=tuple([pl.BlockSpec(memory_space=pltpu.VMEM)] * len(shapes)),
         scratch_shapes=scratch,
+        compiler_params=pltpu.CompilerParams(vmem_limit_bytes=limit),
     )(*operands_all)
 
 
@@ -240,8 +237,6 @@
             gram[...] = jnp.zeros((size, size), f32)
             gram[:slot, :slot] = jnp.where(same, square * (inverse * inverse), 0.0)
 
-        product[...] = jnp.where(diagonal_mask(size), 1.0, 0.0)
-
         def step(index, carry):
             eye = diagonal_mask(size)
             square = gram[...]
@@ -252,8 +247,15 @@
             shift16 = shift.astype(bf16)
             rest = slope * shift + POLY_THIRD * dot(shift16, shift16)
             rest16 = rest.astype(bf16)
-            before = product[...]
-            product[...] = level * before + dot(rest16, before.astype(bf16))
+
+            @pl.when(index == 0)
+            def _():
+                product[...] = jnp.where(eye, level, 0.0) + rest
+
+            @pl.when(index > 0)
+            def _():
+                before = product[...]
+                product[...] = level * before + dot(rest16, before.astype(bf16))
 
             @pl.when(index < NS_STEPS - 1)
             def _():
@@ -320,6 +322,7 @@
     bf16 = jnp.bfloat16
     tensor_count = lax.axis_size("tensor")
     data_count = lax.axis_size(DATA)
+    major_count = lax.axis_size("major")
     my_data = lax.axis_index(DATA)
     my_tensor = lax.axis_index("tensor")
     own = block_in.shape[0]
@@ -345,14 +348,18 @@
         half = jnp.where(flags[0] == 0, key, value)
         attn = jnp.concatenate([query, half, output], axis=1).astype(bf16)
         gate_up = jnp.concatenate([gate, upper], axis=1).astype(bf16)
-        return repeated(attn, data_count), gate_up, down.astype(bf16)
+        return (
+            repeated(attn, data_count),
+            repeated(gate_up, major_count),
+            repeated(down.astype(bf16), major_count),
+        )
 
     packed_attn, packed_gu, packed_d = on_chip(
         pack,
         [
             jax.ShapeDtypeStruct((data_count, shard_rows, 3 * head_width), bf16),
-            jax.ShapeDtypeStruct((shard_rows, 2 * hidden_width), bf16),
-            jax.ShapeDtypeStruct((shard_rows, hidden_width), bf16),
+            jax.ShapeDtypeStruct((major_count, shard_rows, 2 * hidden_width), bf16),
+            jax.ShapeDtypeStruct((major_count, shard_rows, hidden_width), bf16),
         ],
         w_query,
         w_key,
@@ -362,14 +369,14 @@
         w_up,
         w_down,
         flags=(my_tensor & 1).reshape(1),
-        fetch=True,
+        fetch=0,
     )
     weights_attn = exchange(packed_attn, DATA).reshape(model_width, 3 * head_width)
     packed_gu, weights_attn = lax.optimization_barrier((packed_gu, weights_attn))
-    major_gu = gather_major(packed_gu)
+    major_gu = exchange(packed_gu, "major")
     packed_d, major_gu = lax.optimization_barrier((packed_d, major_gu))
     weights_gu = gather_minor(major_gu)
-    major_d = gather_major(packed_d)
+    major_d = exchange(packed_d, "major")
     weight_d = gather_minor(major_d)
     weight_q = weights_attn[:, :head_width]
     weight_half = weights_attn[:, head_width : 2 * head_width]
@@ -430,12 +437,12 @@
 
     d_branch, g_post_ffn = rms_pull(branch, post_ffn, cot_rows)
     branch_low = both_halves(d_branch.astype(bf16))
-    pair_d = pair_sum(dot_rows(branch_low, hidden))
+    pair_d = pair_sum(dot_rows(branch_low, hidden).astype(bf16))
     arrived_d = exchange(pair_d, "major")
     d_hidden = dot(branch_low, weight_d)
     d_gate, d_upper = jax.vjp(gated, gate, upper)[1](d_hidden)
     gu_low = jnp.concatenate([d_gate.astype(bf16), d_upper.astype(bf16)], axis=1)
-    pair_gu = pair_sum(dot_rows(normed_two, gu_low))
+    pair_gu = pair_sum(dot_rows(normed_two, gu_low).astype(bf16))
     pair_gu, arrived_d = lax.optimization_barrier((pair_gu, arrived_d))
     arrived_gu = exchange(pair_gu, "major")
     d_normed_two = row_sum(dot_cols(gu_low, weights_gu))
@@ -457,8 +464,14 @@
     qkv_low = jnp.concatenate(
         [d_queries.astype(bf16), d_keys.astype(bf16), d_vals.astype(bf16)], axis=1
     )
-    grad_qkv = dot_rows(normed_one, qkv_low).astype(bf16)
-    grad_attn = jnp.concatenate([grad_qkv, grad_o], axis=1)
+    grad_kv = dot_rows(normed_one, qkv_low[:, head_width:])
+    grad_key, grad_value = grad_kv[:, :head_width], grad_kv[:, head_width:]
+    got = swap(jnp.where(first_core, grad_value, grad_key).astype(bf16), "tensor", 1)
+    grad_half = jnp.where(first_core, grad_key, grad_value) + got.astype(f32)
+    grad_query = dot_rows(normed_one, qkv_low[:, :head_width])
+    grad_attn = jnp.concatenate(
+        [grad_query.astype(bf16), grad_half.astype(bf16), grad_o], axis=1
+    )
     grad_attn, arrived_gu = lax.optimization_barrier((grad_attn, arrived_gu))
     arrived_attn = exchange(grad_attn.reshape(data_count, shard_rows, -1), DATA)
 
@@ -485,16 +498,17 @@
         wide = total_of(moved_gu)
         terms = (
             low[:, :head_width],
-            low[:, head_width : 3 * head_width],
-            low[:, 3 * head_width :],
+            low[:, head_width : 2 * head_width],
+            low[:, 2 * head_width :],
             wide[:, :hidden_width],
             wide[:, hidden_width:],
             total_of(moved_d),
         )
-        share = jnp.where(flags[0] == 0, 1.0, 0.0)
+        share = jnp.where(flags[0] < 2, 1.0, 0.0)
+        even = flags[0] % 2 == 0
         held = (
             m_query,
-            jnp.concatenate([m_key, m_value], axis=1) * share,
+            jnp.where(even, m_key, m_value) * share,
             m_output,
             m_gate,
             m_up,
@@ -508,6 +522,11 @@
                 continue
             which = owners.index(index)
             push = (terms[which] + MUON_BETA * moved[which]).astype(bf16)
+            if which == 1:
+                none = jnp.zeros_like(push)
+                push = jnp.concatenate(
+                    [jnp.where(even, push, none), jnp.where(even, none, push)], axis=1
+                )
             if push.shape[1] < slot:
                 empty = jnp.zeros((shard_rows, slot - push.shape[1]), bf16)
                 push = jnp.concatenate([push, empty], axis=1)
@@ -522,7 +541,7 @@
     def rows_of(width):
         return jax.ShapeDtypeStruct((shard_rows, width), f32)
 
-    widths = (head_width, 2 * head_width, head_width, hidden_width, hidden_width, hidden_width)
+    widths = (head_width, head_width, head_width, hidden_width, hidden_width, hidden_width)
     made = on_chip(
         advance,
         [jax.ShapeDtypeStruct((data_count, shard_rows, slot), bf16)]
@@ -539,16 +558,18 @@
         mom_up,
         mom_down,
         flags=my_tensor.reshape(1),
-        fetch=True,
+        fetch=3,
+        limit=24 * 1024 * 1024,
     )
     outgoing, sum_query, part_kv, sum_output, sum_gate, sum_up, sum_down = made[:7]
     moved_query, moved_output, moved_gate, moved_up, moved_down = made[7:]
 
     owned = exchange(outgoing, DATA).reshape(data_count * shard_rows, slot)
 
-    sum_kv = part_kv + swap(part_kv, "tensor", 1)
-    sum_kv = sum_kv + swap(sum_kv, "tensor", 2)
-    sum_key, sum_value = sum_kv[:, :head_width], sum_kv[:, head_width:]
+    sum_half = part_kv + swap(part_kv, "tensor", 2)
+    sum_other = swap(sum_half, "tensor", 1)
+    sum_key = jnp.where(first_core, sum_half, sum_other)
+    sum_value = jnp.where(first_core, sum_other, sum_half)
     moved_key = MUON_BETA * mom_key + sum_key
     moved_value = MUON_BETA * mom_value + sum_value
     gain_half = butterfly(gain_term, ("tensor",))
@@ -578,7 +599,8 @@
         return tuple(results)
 
     updated = on_chip(
-        renew, [rows_of(weight.shape[1]) for weight in weights], returned, *weights, fetch=True
+        renew, [rows_of(weight.shape[1]) for weight in weights], returned, *weights, fetch=1,
+        limit=24 * 1024 * 1024,
     )
     next_first = FIRST_DECAY * adam_first + (1.0 - FIRST_DECAY) * grad_gains
     next_second = SECOND_DECAY * adam_second + (1.0 - SECOND_DECAY) * grad_gains * grad_gains

time: 290 us -> 279 us (0.962)
  waiting for transfers between devices: 132 us -> 126 us
    all_to_all x8, waiting for transfers between devices: 69.5 us -> 64.7 us  [exchange(): return lax.all_to_all(values, axis, split_axis=0, concat_axis=0, tiled=True)]
    ppermute x29 -> x30, waiting for transfers between devices: 63 us -> 61.3 us  [swap(): return lax.ppermute(values, axis, [(i, i ^ mask) for i in range(count)])]
    dot_general x6 -> x7, matrix products: 6.4 us -> 5.42 us  [dot_rows(): lax.dot_general(left, right, (((0,), (0,)), ((), ())), preferred_element_...]
    ppermute x29 -> x30, starting transfers between devices: 19.6 us -> 20.1 us  [swap(): return lax.ppermute(values, axis, [(i, i ^ mask) for i in range(count)])]
    unnamed x165 -> x233, local copies, waits for them, and re-layouts: 9.31 us -> 9.48 us
  transfers between devices with their start and end apart: 37 -> 38, of which waited for: 27 -> 28; matrix products, arithmetic and copies ran while one was open for 16% -> 16% of each run, Pallas kernels for 0% -> 0%
where the time goes in v1:
time: 279 us; the launch traced here: 278 us
  waiting for transfers between devices  126 us (45%)
  starting transfers between devices  55.8 us (20%)
  other arithmetic  32.3 us (12%)
  Pallas kernels  27.6 us (10%)
  matrix products  18.6 us (7%)
  local copies, waits for them, and re-layouts  14.7 us (5%)
  between operations  2.79 us (1%)
    all_to_all x8, waiting for transfers between devices, exchange(): return lax.all_to_all(values, axis, split_axis=0, concat_axis=0, tiled=True)  64.7 us
    ppermute x30, waiting for transfers between devices, swap(): return lax.ppermute(values, axis, [(i, i ^ mask) for i in range(count)])  61.3 us
    all_to_all x8, starting transfers between devices, exchange(): return lax.all_to_all(values, axis, split_axis=0, concat_axis=0, tiled=True)  35.7 us
    pallas_call x1, Pallas kernels, newton_schulz(): pl.pallas_call(kernel, out_shape=jax.ShapeDtypeStruct((size, slot), bf16)...  20.2 us
    ppermute x30, starting transfers between devices, swap(): return lax.ppermute(values, axis, [(i, i ^ mask) for i in range(count)])  20.1 us
    unnamed x233, local copies, waits for them, and re-layouts  9.48 us
    dot_general x6, matrix products, dot(): return jnp.dot(left, right, preferred_element_type=jnp.float32)  8.41 us
    pallas_call x3, Pallas kernels, on_chip(): pl.pallas_call(kernel, out_shape=tuple(shapes), in_specs=specs, out_specs...  7.46 us
  transfers between devices with their start and end apart: 38, of which 28 were waited for; matrix products, arithmetic and copies ran while one was open for 16% of the time, Pallas kernels for 0%

profile of v1, /device:TPU:0, one launch (start us, length us, event | category | flops | bytes accessed | tf_op | source)
XLA Modules:
  0.0 277.7 jit_solution(5269850843827952569)
XLA Ops:
  0.7 2.7 shard_map.403
  3.4 7.3 %all-to-all-start = ((bf16[8,80,768]{2,1,0:T(8,128)(2,1)}), bf16[8,80,768]{2,1,0:T(8,128)(2,1)S(1)}, u32[]{:S(2)}, u32[]{:S(2)}) async-start(bf16[8,80,768]{2,1,0:T(8,128)(2,1)} %get-tuple-element.66), calls=%async_computation | async-start | bytes 1966080 | tf_op jit(solution)/shard_map/all_to_all | solution.py:113
  10.7 1.6 collective-permute-start
  13.1 1.8 multiply_sine_fusion
  16.2 5.2 %collective-permute-done = f32[128,640]{1,0:T(8,128)S(1)} collective-permute-done((f32[128,640]{1,0:T(8,128)S(1)}, f32[128,640]{1,0:T(8,128)S(1)}, u32[]{:S(2)}, u32[]{:S(2)}) %collective-permute-start) | collective-permute-done | bytes 327712 | tf_op jit(solution)/shard_map/ppermute | solution.py:65
  22.5 12.6 %all-to-all-done = bf16[8,80,768]{2,1,0:T(8,128)(2,1)S(1)} async-done(((bf16[8,80,768]{2,1,0:T(8,128)(2,1)}), bf16[8,80,768]{2,1,0:T(8,128)(2,1)S(1)}, u32[]{:S(2)}, u32[]{:S(2)}) %all-to-all-start) | async-done | bytes 983072 | tf_op jit(solution)/shard_map/all_to_all | solution.py:113
  37.7 1.3 pad_maximum_fusion.6
  39.0 1.3 broadcast_select_fusion.1
  46.9 4.2 %all-to-all-start.1 = ((bf16[4,80,1024]{2,1,0:T(8,128)(2,1)}), bf16[4,80,1024]{2,1,0:T(8,128)(2,1)}, u32[]{:S(2)}, u32[]{:S(2)}) async-start(bf16[4,80,1024]{2,1,0:T(8,128)(2,1)} %get-tuple-element.69), calls=%async_computation.1 | async-start | bytes 1310720 | tf_op jit(solution)/shard_map/all_to_all | solution.py:113
  52.3 1.6 collective-permute-start.5
  53.8 8.2 %collective-permute-done.5 = bf16[256,640]{1,0:T(8,128)(2,1)S(1)} collective-permute-done((bf16[256,640]{1,0:T(8,128)(2,1)S(1)}, bf16[256,640]{1,0:T(8,128)(2,1)S(1)}, u32[]{:S(2)}, u32[]{:S(2)}) %collective-permute-start.5) | collective-permute-done | bytes 327712 | tf_op jit(solution)/shard_map/ppermute | solution.py:65
  62.8 6.1 %all-to-all-done.1 = bf16[4,80,1024]{2,1,0:T(8,128)(2,1)} async-done(((bf16[4,80,1024]{2,1,0:T(8,128)(2,1)}), bf16[4,80,1024]{2,1,0:T(8,128)(2,1)}, u32[]{:S(2)}, u32[]{:S(2)}) %all-to-all-start.1) | async-done | bytes 655392 | tf_op jit(solution)/shard_map/all_to_all | solution.py:113
  68.9 1.4 collective-permute-start.7
  70.3 4.3 %all-to-all-start.2 = ((bf16[4,80,512]{2,1,0:T(8,128)(2,1)}), bf16[4,80,512]{2,1,0:T(8,128)(2,1)}, u32[]{:S(2)}, u32[]{:S(2)}) async-start(bf16[4,80,512]{2,1,0:T(8,128)(2,1)} %get-tuple-element.71), calls=%async_computation.2 | async-start | bytes 655360 | tf_op jit(solution)/shard_map/all_to_all | solution.py:113
  74.6 1.4 multiply_reduce_fusion.4
  77.6 6.5 %all-to-all-done.2 = bf16[4,80,512]{2,1,0:T(8,128)(2,1)} async-done(((bf16[4,80,512]{2,1,0:T(8,128)(2,1)}), bf16[4,80,512]{2,1,0:T(8,128)(2,1)}, u32[]{:S(2)}, u32[]{:S(2)}) %all-to-all-start.2) | async-done | bytes 327712 | tf_op jit(solution)/shard_map/all_to_all | solution.py:113
  85.3 1.4 select_bitcast_fusion.1
  87.0 2.2 fusion.43
  89.6 2.4 collective-permute-done.8
  94.0 1.6 collective-permute-done.9
  95.7 1.6 collective-permute-start.10
  97.2 8.3 %collective-permute-done.10 = bf16[256,640]{1,0:T(8,128)(2,1)S(1)} collective-permute-done((bf16[256,640]{1,0:T(8,128)(2,1)S(1)}, bf16[256,640]{1,0:T(8,128)(2,1)S(1)}, u32[]{:S(2)}, u32[]{:S(2)}) %collective-permute-start.10) | collective-permute-done | bytes 327712 | tf_op jit(solution)/shard_map/ppermute | solution.py:65
  107.0 1.8 collective-permute-done.11
  108.8 3.2 %fusion.11 = (bf16[512,512]{1,0:T(8,128)(2,1)S(1)}, bf16[512,512]{1,0:T(8,128)(2,1)S(1)}) fusion(f32[512,1024]{1,0:T(8,128)} %copy-done.20, bf16[640,512]{1,0:T(8,128)(2,1)} %bitcast.72, bf16[256,640]{1,0:T(8,128)(2,1)S(1)} %collective-permute-done.11, bf16[256,640]{1,0:T(8,128)(2,1)} %get-tuple-element.145), kind=kOutput, calls=%fused_computation.24 | convolution fusion | flops 343146496 | bytes 4456448 | tf_op jit(solution)/shard_map/dot_general | solution.py:69
  113.3 1.5 convolution_convert_fusion.1
  114.9 1.5 collective-permute-start.13
  116.3 1.9 convolution_convert_fusion
  119.1 1.5 collective-permute-start.15
  122.1 3.4 %collective-permute-done.13 = bf16[4,80,512]{2,1,0:T(8,128)(2,1)S(1)} collective-permute-done((bf16[4,80,512]{2,1,0:T(8,128)(2,1)S(1)}, bf16[4,80,512]{2,1,0:T(8,128)(2,1)S(1)}, u32[]{:S(2)}, u32[]{:S(2)}) %collective-permute-start.13) | collective-permute-done | bytes 327712 | tf_op jit(solution)/shard_map/ppermute | solution.py:65
  126.4 3.5 %all-to-all-start.3 = ((bf16[4,80,512]{2,1,0:T(8,128)(2,1)}), bf16[4,80,512]{2,1,0:T(8,128)(2,1)S(1)}, u32[]{:S(2)}, u32[]{:S(2)}) async-start(bf16[4,80,512]{2,1,0:T(8,128)(2,1)} %fusion.24), calls=%async_computation.3 | async-start | bytes 655360 | tf_op jit(solution)/shard_map/all_to_all | solution.py:113
  132.4 2.4 multiply_reduce_fusion
  135.2 3.9 %collective-permute-done.12 = bf16[4,80,1024]{2,1,0:T(8,128)(2,1)} collective-permute-done((bf16[4,80,1024]{2,1,0:T(8,128)(2,1)}, bf16[4,80,1024]{2,1,0:T(8,128)(2,1)}, u32[]{:S(2)}, u32[]{:S(2)}) %collective-permute-start.12) | collective-permute-done | bytes 655392 | tf_op jit(solution)/shard_map/ppermute | solution.py:65
  139.1 2.2 fusion.3
  141.3 3.7 %all-to-all-start.4 = ((bf16[4,80,1024]{2,1,0:T(8,128)(2,1)}), bf16[4,80,1024]{2,1,0:T(8,128)(2,1)S(1)}, u32[]{:S(2)}, u32[]{:S(2)}) async-start(bf16[4,80,1024]{2,1,0:T(8,128)(2,1)} %fusion.3), calls=%async_computation.4 | async-start | bytes 1310720 | tf_op jit(solution)/shard_map/all_to_all | solution.py:113
  145.0 1.6 multiply_reduce_fusion.11
  154.4 7.6 %all-to-all-done.4.refs_2_ = bf16[4,80,1024]{2,1,0:T(8,128)(2,1)S(1)} async-done(((bf16[4,80,1024]{2,1,0:T(8,128)(2,1)}), bf16[4,80,1024]{2,1,0:T(8,128)(2,1)S(1)}, u32[]{:S(2)}, u32[]{:S(2)}) %all-to-all-start.4) | async-done | bytes 655392 | tf_op jit(solution)/shard_map/all_to_all | solution.py:113
  162.0 1.4 copy.72
  163.4 3.7 %all-to-all-start.5 = ((bf16[8,80,768]{2,1,0:T(8,128)(2,1)}), bf16[8,80,768]{2,1,0:T(8,128)(2,1)S(1)}, u32[]{:S(2)}, u32[]{:S(2)}) async-start(bf16[8,80,768]{2,1,0:T(8,128)(2,1)} %bitcast.70), calls=%async_computation.5 | async-start | bytes 1966080 | tf_op jit(solution)/shard_map/all_to_all | solution.py:113
  167.2 2.0 fusion.13
  171.1 1.5 collective-permute-start.19
  172.7 1.5 fusion.48
  174.1 3.3 %collective-permute-done.19 = bf16[128,640]{1,0:T(8,128)(2,1)S(1)} collective-permute-done((bf16[128,640]{1,0:T(8,128)(2,1)S(1)}, bf16[128,640]{1,0:T(8,128)(2,1)S(1)}, u32[]{:S(2)}, u32[]{:S(2)}) %collective-permute-start.19) | collective-permute-done | bytes 163872 | tf_op jit(solution)/shard_map/ppermute | solution.py:65
  178.8 12.3 %all-to-all-done.5.refs_3_ = bf16[8,80,768]{2,1,0:T(8,128)(2,1)S(1)} async-done(((bf16[8,80,768]{2,1,0:T(8,128)(2,1)}), bf16[8,80,768]{2,1,0:T(8,128)(2,1)S(1)}, u32[]{:S(2)}, u32[]{:S(2)}) %all-to-all-start.5) | async-done | bytes 983072 | tf_op jit(solution)/shard_map/all_to_all | solution.py:113
  191.2 2.8 shard_map.404
  194.1 3.7 %all-to-all-start.6 = ((bf16[8,80,512]{2,1,0:T(8,128)(2,1)}), bf16[8,80,512]{2,1,0:T(8,128)(2,1)S(1)}, u32[]{:S(2)}, u32[]{:S(2)}) async-start(bf16[8,80,512]{2,1,0:T(8,128)(2,1)} %get-tuple-element.77), calls=%async_computation.6 | async-start | bytes 1310720 | tf_op jit(solution)/shard_map/all_to_all | solution.py:113
  197.8 1.3 constant_dynamic-update-slice_fusion.2
  199.1 1.8 subtract_add_fusion.1
  202.3 1.5 collective-permute-start.21
  203.7 2.2 collective-permute-done.21
  206.0 9.1 %all-to-all-done.6 = bf16[8,80,512]{2,1,0:T(8,128)(2,1)S(1)} async-done(((bf16[8,80,512]{2,1,0:T(8,128)(2,1)}), bf16[8,80,512]{2,1,0:T(8,128)(2,1)S(1)}, u32[]{:S(2)}, u32[]{:S(2)}) %all-to-all-start.6) | async-done | bytes 655392 | tf_op jit(solution)/shard_map/all_to_all | solution.py:113
  215.1 1.5 collective-permute-start.24
  216.5 1.5 collective-permute-start.25
  218.0 2.2 collective-permute-done.25
  220.8 3.1 %collective-permute-done.26 = f32[3072]{0:T(1024)S(1)} collective-permute-done((f32[3072]{0:T(1024)S(1)}, f32[3072]{0:T(1024)S(1)}, u32[]{:S(2)}, u32[]{:S(2)}) %collective-permute-start.26) | collective-permute-done | bytes 12320 | tf_op jit(solution)/shard_map/ppermute | solution.py:65
  224.0 4.7 %collective-permute-done.27 = f32[3072]{0:T(1024)S(1)} collective-permute-done((f32[3072]{0:T(1024)S(1)}, f32[3072]{0:T(1024)S(1)}, u32[]{:S(2)}, u32[]{:S(2)}) %collective-permute-start.27) | collective-permute-done | bytes 12320 | tf_op jit(solution)/shard_map/ppermute | solution.py:65
  228.7 1.5 collective-permute-done.24.across_ref
  230.2 2.1 collective-permute-done.29.far_ref
  232.3 20.2 %shard_map.405 = bf16[640,512]{1,0:T(8,128)(2,1)} custom-call(s32[1]{0:T(128)} %bitcast.22.flag_ref, bf16[640,512]{1,0:T(8,128)(2,1)S(1)} %bitcast.64, bf16[640,512]{1,0:T(8,128)(2,1)S(1)} %collective-permute-done.28.near_ref, bf16[640,512]{1,0:T(8,128)(2,1)S(1)} %collective-permute-done.24.across_ref, bf16[640,512]{1,0:T(8,128)(2,1)S(1)} %collective-permute-done.29.far_ref), custom_call_target="tpu_custom_call" | custom-call | tf_op jit(solution)/shard_map/pallas_call | solution.py:284
  252.6 5.3 %all-to-all-start.7 = ((bf16[8,80,512]{2,1,0:T(8,128)(2,1)}), bf16[8,80,512]{2,1,0:T(8,128)(2,1)S(1)}, u32[]{:S(2)}, u32[]{:S(2)}) async-start(bf16[8,80,512]{2,1,0:T(8,128)(2,1)} %bitcast.23), calls=%async_computation.7 | async-start | bytes 1310720 | tf_op jit(solution)/shard_map/all_to_all | solution.py:113
  257.8 1.5 collective-permute-start.22
  259.3 3.0 %collective-permute-done.22 = f32[80,256]{1,0:T(8,128)S(1)} collective-permute-done((f32[80,256]{1,0:T(8,128)S(1)}, f32[80,256]{1,0:T(8,128)S(1)}, u32[]{:S(2)}, u32[]{:S(2)}) %collective-permute-start.22) | collective-permute-done | bytes 81952 | tf_op jit(solution)/shard_map/ppermute | solution.py:65
  262.4 1.3 collective-permute-done.23
  265.0 10.4 %all-to-all-done.7.refs_0_ = bf16[8,80,512]{2,1,0:T(8,128)(2,1)S(1)} async-done(((bf16[8,80,512]{2,1,0:T(8,128)(2,1)}), bf16[8,80,512]{2,1,0:T(8,128)(2,1)S(1)}, u32[]{:S(2)}, u32[]{:S(2)}) %all-to-all-start.7) | async-done | bytes 655392 | tf_op jit(solution)/shard_map/all_to_all | solution.py:113
  275.5 2.0 shard_map.406
  (366 shorter events, 42.5 us)
Async XLA Ops:
  0.7 11.6 %copy-start.60 = (f32[128,640]{1,0:T(8,128)S(1)}, f32[128,640]{1,0:T(8,128)}, u32[]{:S(2)}) copy-start(f32[128,640]{1,0:T(8,128)} %param.21) | copy-start | bytes 983044
  0.7 12.1 %copy-start.104 = (s32[1,512]{1,0:T(1,128)S(1)}, s32[1,512]{1,0:T(1,128)}, u32[]{:S(2)}) copy-start(s32[1,512]{1,0:T(1,128)} %param.22) | copy-start | bytes 6148
  3.4 11.5 %copy-start.67 = (f32[3072]{0:T(1024)S(1)}, f32[3072]{0:T(1024)}, u32[]{:S(2)}) copy-start(f32[3072]{0:T(1024)} %param.37) | copy-start | bytes 36868
  3.4 31.7 %all-to-all-start = ((bf16[8,80,768]{2,1,0:T(8,128)(2,1)}), bf16[8,80,768]{2,1,0:T(8,128)(2,1)S(1)}, u32[]{:S(2)}, u32[]{:S(2)}) async-start(bf16[8,80,768]{2,1,0:T(8,128)(2,1)} %get-tuple-element.66), calls=%async_computation | async-start | bytes 1966080 | tf_op jit(solution)/shard_map/all_to_all | solution.py:113
  10.7 10.6 %collective-permute-start = (f32[128,640]{1,0:T(8,128)S(1)}, f32[128,640]{1,0:T(8,128)S(1)}, u32[]{:S(2)}, u32[]{:S(2)}) collective-permute-start(f32[128,640]{1,0:T(8,128)S(1)} %copy-done.34), channel_id=1, source_target_pairs={{0,2},{1,3},{2,0},{3,1},{4,6},{5,7},{6,4},{7,5},{8,10},{9,11},{10,... | collective-permute-start | bytes 983048 | tf_op jit(solution)/shard_map/ppermute | solution.py:65
  12.3 24.2 %collective-permute-start.2 = (f32[128,640]{1,0:T(8,128)S(1)}, f32[128,640]{1,0:T(8,128)}, u32[]{:S(2)}, u32[]{:S(2)}) collective-permute-start(f32[128,640]{1,0:T(8,128)S(1)} %copy-done.60), channel_id=1, source_target_pairs={{0,2},{1,3},{2,0},{3,1},{4,6},{5,7},{6,4},{7,5},{8,10},{9,11},{10,... | collective-permute-start | bytes 983048 | tf_op jit(solution)/shard_map/ppermute | solution.py:65
  14.9 27.7 %copy-start.38 = (f32[512,128]{1,0:T(8,128)}, f32[512,128]{1,0:T(8,128)S(1)}, u32[]{:S(2)}) copy-start(f32[512,128]{1,0:T(8,128)S(1)} %get-tuple-element.178) | copy-start | bytes 786436
  22.4 15.2 %collective-permute-start.1 = (bf16[256,640]{1,0:T(8,128)(2,1)S(1)}, bf16[256,640]{1,0:T(8,128)(2,1)}, u32[]{:S(2)}, u32[]{:S(2)}) collective-permute-start(bf16[256,640]{1,0:T(8,128)(2,1)S(1)} %multiply_convert_fusion.3), channel_id=1, source_target_pairs={{0,1},{1,0},{2,3},{3,2},{4,5},{5,4},{6,7},{7,6},{8,9},{9,8},{10,11... | collective-permute-start | bytes 983048 | tf_op jit(solution)/shard_map/ppermute | solution.py:65
  36.5 2.5 collective-permute-start.3
  37.6 94.7 %copy-start.16 = (f32[256,640]{1,0:T(8,128)}, f32[256,640]{1,0:T(8,128)S(1)}, u32[]{:S(2)}) copy-start(f32[256,640]{1,0:T(8,128)S(1)} %pad_maximum_fusion.7) | copy-start | bytes 1966084
  46.4 4.7 %collective-permute-start.4 = (bf16[256,640]{1,0:T(8,128)(2,1)S(1)}, bf16[256,640]{1,0:T(8,128)(2,1)S(1)}, u32[]{:S(2)}, u32[]{:S(2)}) collective-permute-start(bf16[256,640]{1,0:T(8,128)(2,1)S(1)} %slice.326), channel_id=1, source_target_pairs={{0,1},{1,0},{2,3},{3,2},{4,5},{5,4},{6,7},{7,6},{8,9},{9,8},{10,11... | collective-permute-start | bytes 983048 | tf_op jit(solution)/shard_map/ppermute | solution.py:65
  46.9 22.0 %all-to-all-start.1 = ((bf16[4,80,1024]{2,1,0:T(8,128)(2,1)}), bf16[4,80,1024]{2,1,0:T(8,128)(2,1)}, u32[]{:S(2)}, u32[]{:S(2)}) async-start(bf16[4,80,1024]{2,1,0:T(8,128)(2,1)} %get-tuple-element.69), calls=%async_computation.1 | async-start | bytes 1310720 | tf_op jit(solution)/shard_map/all_to_all | solution.py:113
  52.3 9.7 %collective-permute-start.5 = (bf16[256,640]{1,0:T(8,128)(2,1)S(1)}, bf16[256,640]{1,0:T(8,128)(2,1)S(1)}, u32[]{:S(2)}, u32[]{:S(2)}) collective-permute-start(bf16[256,640]{1,0:T(8,128)(2,1)S(1)} %fusion.23), channel_id=1, source_target_pairs={{0,2},{1,3},{2,0},{3,1},{4,6},{5,7},{6,4},{7,5},{8,10},{9,11},{10,... | collective-permute-start | bytes 983048 | tf_op jit(solution)/shard_map/ppermute | solution.py:65
  62.0 14.0 %copy-start.27 = (bf16[128,640]{1,0:T(8,128)(2,1)}, bf16[128,640]{1,0:T(8,128)(2,1)S(1)}, u32[]{:S(2)}) copy-start(bf16[128,640]{1,0:T(8,128)(2,1)S(1)} %get-tuple-element.165) | copy-start | bytes 491524
  62.0 14.0 %copy-start.29 = (bf16[128,640]{1,0:T(8,128)(2,1)}, bf16[128,640]{1,0:T(8,128)(2,1)S(1)}, u32[]{:S(2)}) copy-start(bf16[128,640]{1,0:T(8,128)(2,1)S(1)} %get-tuple-element.166) | copy-start | bytes 491524
  62.2 12.4 %copy-start.96 = (f32[256]{0:T(256)}, f32[256]{0:T(256)S(1)}, u32[]{:S(2)}) copy-start(f32[256]{0:T(256)S(1)} %multiply_reduce_fusion.5) | copy-start | bytes 3076
  68.9 16.4 %collective-permute-start.7 = (bf16[4,80,1024]{2,1,0:T(8,128)(2,1)}, bf16[4,80,1024]{2,1,0:T(8,128)(2,1)}, u32[]{:S(2)}, u32[]{:S(2)}) collective-permute-start(bf16[4,80,1024]{2,1,0:T(8,128)(2,1)} %all-to-all-done.1), channel_id=1, source_target_pairs={{0,4},{4,0},{1,5},{5,1},{2,6},{6,2},{3,7},{7,3},{8,12},{12,8},{9,1... | collective-permute-start | bytes 1966088 | tf_op jit(solution)/shard_map/ppermute | solution.py:65
  70.3 13.8 %all-to-all-start.2 = ((bf16[4,80,512]{2,1,0:T(8,128)(2,1)}), bf16[4,80,512]{2,1,0:T(8,128)(2,1)}, u32[]{:S(2)}, u32[]{:S(2)}) async-start(bf16[4,80,512]{2,1,0:T(8,128)(2,1)} %get-tuple-element.71), calls=%async_computation.2 | async-start | bytes 655360 | tf_op jit(solution)/shard_map/all_to_all | solution.py:113
  76.0 56.3 %copy-start.18 = (f32[256,640]{1,0:T(8,128)}, f32[256,640]{1,0:T(8,128)S(1)}, u32[]{:S(2)}) copy-start(f32[256,640]{1,0:T(8,128)S(1)} %get-tuple-element.127) | copy-start | bytes 1966084
  77.5 9.4 %collective-permute-start.6 = (bf16[256,640]{1,0:T(8,128)(2,1)S(1)}, bf16[256,640]{1,0:T(8,128)(2,1)}, u32[]{:S(2)}, u32[]{:S(2)}) collective-permute-start(bf16[256,640]{1,0:T(8,128)(2,1)S(1)} %multiply_convert_fusion.2), channel_id=1, source_target_pairs={{0,1},{1,0},{2,3},{3,2},{4,5},{5,4},{6,7},{7,6},{8,9},{9,8},{10,11... | collective-permute-start | bytes 983048 | tf_op jit(solution)/shard_map/ppermute | solution.py:65
  84.1 7.9 %collective-permute-start.8 = (bf16[4,80,512]{2,1,0:T(8,128)(2,1)}, bf16[4,80,512]{2,1,0:T(8,128)(2,1)S(1)}, u32[]{:S(2)}, u32[]{:S(2)}) collective-permute-start(bf16[4,80,512]{2,1,0:T(8,128)(2,1)} %all-to-all-done.2), channel_id=1, source_target_pairs={{0,4},{4,0},{1,5},{5,1},{2,6},{6,2},{3,7},{7,3},{8,12},{12,8},{9,1... | collective-permute-start | bytes 983048 | tf_op jit(solution)/shard_map/ppermute | solution.py:65
  94.0 1.6 collective-permute-start.9
  95.7 9.8 %collective-permute-start.10 = (bf16[256,640]{1,0:T(8,128)(2,1)S(1)}, bf16[256,640]{1,0:T(8,128)(2,1)S(1)}, u32[]{:S(2)}, u32[]{:S(2)}) collective-permute-start(bf16[256,640]{1,0:T(8,128)(2,1)S(1)} %fusion.22), channel_id=1, source_target_pairs={{0,2},{1,3},{2,0},{3,1},{4,6},{5,7},{6,4},{7,5},{8,10},{9,11},{10,... | collective-permute-start | bytes 983048 | tf_op jit(solution)/shard_map/ppermute | solution.py:65
  107.0 1.8 collective-permute-start.11
  113.1 5.1 %collective-permute-start.14 = (bf16[256,640]{1,0:T(8,128)(2,1)S(1)}, bf16[256,640]{1,0:T(8,128)(2,1)S(1)}, u32[]{:S(2)}, u32[]{:S(2)}) collective-permute-start(bf16[256,640]{1,0:T(8,128)(2,1)S(1)} %slice.324), channel_id=1, source_target_pairs={{0,1},{1,0},{2,3},{3,2},{4,5},{5,4},{6,7},{7,6},{8,9},{9,8},{10,11... | collective-permute-start | bytes 983048 | tf_op jit(solution)/shard_map/ppermute | solution.py:65
  114.9 10.6 %collective-permute-start.13 = (bf16[4,80,512]{2,1,0:T(8,128)(2,1)S(1)}, bf16[4,80,512]{2,1,0:T(8,128)(2,1)S(1)}, u32[]{:S(2)}, u32[]{:S(2)}) collective-permute-start(bf16[4,80,512]{2,1,0:T(8,128)(2,1)S(1)} %dynamic-slice_bitcast_fusion.1), channel_id=1, source_target_pairs={{0,4},{4,0},{1,5},{5,1},{2,6},{6,2},{3,7},{7,3},{8,12},{12,8},{9,1... | collective-permute-start | bytes 983048 | tf_op jit(solution)/shard_map/ppermute | solution.py:65
  119.1 10.8 %collective-permute-start.15 = (bf16[256,640]{1,0:T(8,128)(2,1)}, bf16[256,640]{1,0:T(8,128)(2,1)}, u32[]{:S(2)}, u32[]{:S(2)}) collective-permute-start(bf16[256,640]{1,0:T(8,128)(2,1)} %fusion.21), channel_id=1, source_target_pairs={{0,2},{1,3},{2,0},{3,1},{4,6},{5,7},{6,4},{7,5},{8,10},{9,11},{10,... | collective-permute-start | bytes 983048 | tf_op jit(solution)/shard_map/ppermute | solution.py:65
  121.5 17.6 %collective-permute-start.12 = (bf16[4,80,1024]{2,1,0:T(8,128)(2,1)}, bf16[4,80,1024]{2,1,0:T(8,128)(2,1)}, u32[]{:S(2)}, u32[]{:S(2)}) collective-permute-start(bf16[4,80,1024]{2,1,0:T(8,128)(2,1)} %dynamic-slice_bitcast_fusion), channel_id=1, source_target_pairs={{0,4},{4,0},{1,5},{5,1},{2,6},{6,2},{3,7},{7,3},{8,12},{12,8},{9,1... | collective-permute-start | bytes 1966088 | tf_op jit(solution)/shard_map/ppermute | solution.py:65
  126.4 14.9 %all-to-all-start.3 = ((bf16[4,80,512]{2,1,0:T(8,128)(2,1)}), bf16[4,80,512]{2,1,0:T(8,128)(2,1)S(1)}, u32[]{:S(2)}, u32[]{:S(2)}) async-start(bf16[4,80,512]{2,1,0:T(8,128)(2,1)} %fusion.24), calls=%async_computation.3 | async-start | bytes 655360 | tf_op jit(solution)/shard_map/all_to_all | solution.py:113
  135.1 9.9 %collective-permute-start.16 = (bf16[256,640]{1,0:T(8,128)(2,1)S(1)}, bf16[256,640]{1,0:T(8,128)(2,1)S(1)}, u32[]{:S(2)}, u32[]{:S(2)}) collective-permute-start(bf16[256,640]{1,0:T(8,128)(2,1)S(1)} %subtract_convert_fusion), channel_id=1, source_target_pairs={{0,1},{1,0},{2,3},{3,2},{4,5},{5,4},{6,7},{7,6},{8,9},{9,8},{10,11... | collective-permute-start | bytes 983048 | tf_op jit(solution)/shard_map/ppermute | solution.py:65
  141.3 20.7 %all-to-all-start.4 = ((bf16[4,80,1024]{2,1,0:T(8,128)(2,1)}), bf16[4,80,1024]{2,1,0:T(8,128)(2,1)S(1)}, u32[]{:S(2)}, u32[]{:S(2)}) async-start(bf16[4,80,1024]{2,1,0:T(8,128)(2,1)} %fusion.3), calls=%async_computation.4 | async-start | bytes 1310720 | tf_op jit(solution)/shard_map/all_to_all | solution.py:113
  152.5 1.7 collective-permute-start.17
  163.4 27.7 %all-to-all-start.5 = ((bf16[8,80,768]{2,1,0:T(8,128)(2,1)}), bf16[8,80,768]{2,1,0:T(8,128)(2,1)S(1)}, u32[]{:S(2)}, u32[]{:S(2)}) async-start(bf16[8,80,768]{2,1,0:T(8,128)(2,1)} %bitcast.70), calls=%async_computation.5 | async-start | bytes 1966080 | tf_op jit(solution)/shard_map/all_to_all | solution.py:113
  169.2 1.7 collective-permute-start.18
  171.0 20.1 %copy-start.3 = (f32[80,256]{1,0:T(8,128)S(1)}, f32[80,256]{1,0:T(8,128)}, u32[]{:S(2)}) copy-start(f32[80,256]{1,0:T(8,128)} %refs_5_.4) | copy-start | bytes 245764
  171.0 20.1 %copy-start.4 = (f32[80,256]{1,0:T(8,128)S(1)}, f32[80,256]{1,0:T(8,128)}, u32[]{:S(2)}) copy-start(f32[80,256]{1,0:T(8,128)} %refs_6_.4) | copy-start | bytes 245764
  171.0 20.1 %copy-start.9 = (f32[80,512]{1,0:T(8,128)S(1)}, f32[80,512]{1,0:T(8,128)}, u32[]{:S(2)}) copy-start(f32[80,512]{1,0:T(8,128)} %refs_8_.1) | copy-start | bytes 491524
  171.0 20.1 %copy-start.10 = (f32[80,512]{1,0:T(8,128)S(1)}, f32[80,512]{1,0:T(8,128)}, u32[]{:S(2)}) copy-start(f32[80,512]{1,0:T(8,128)} %refs_9_.1) | copy-start | bytes 491524
  171.0 20.1 %copy-start.11 = (f32[80,512]{1,0:T(8,128)S(1)}, f32[80,512]{1,0:T(8,128)}, u32[]{:S(2)}) copy-start(f32[80,512]{1,0:T(8,128)} %refs_10_.1) | copy-start | bytes 491524
  171.1 20.1 %copy-start.12 = (f32[80,256]{1,0:T(8,128)S(1)}, f32[80,256]{1,0:T(8,128)}, u32[]{:S(2)}) copy-start(f32[80,256]{1,0:T(8,128)} %refs_4_.4) | copy-start | bytes 245764
  171.1 20.1 %copy-start.13 = (f32[80,256]{1,0:T(8,128)S(1)}, f32[80,256]{1,0:T(8,128)}, u32[]{:S(2)}) copy-start(f32[80,256]{1,0:T(8,128)} %refs_7_.4) | copy-start | bytes 245764
  171.1 6.3 %collective-permute-start.19 = (bf16[128,640]{1,0:T(8,128)(2,1)S(1)}, bf16[128,640]{1,0:T(8,128)(2,1)S(1)}, u32[]{:S(2)}, u32[]{:S(2)}) collective-permute-start(bf16[128,640]{1,0:T(8,128)(2,1)S(1)} %slice.225), channel_id=1, source_target_pairs={{0,2},{1,3},{2,0},{3,1},{4,6},{5,7},{6,4},{7,5},{8,10},{9,11},{10,... | collective-permute-start | bytes 491528 | tf_op jit(solution)/shard_map/ppermute | solution.py:65
  194.1 21.0 %all-to-all-start.6 = ((bf16[8,80,512]{2,1,0:T(8,128)(2,1)}), bf16[8,80,512]{2,1,0:T(8,128)(2,1)S(1)}, u32[]{:S(2)}, u32[]{:S(2)}) async-start(bf16[8,80,512]{2,1,0:T(8,128)(2,1)} %get-tuple-element.77), calls=%async_computation.6 | async-start | bytes 1310720 | tf_op jit(solution)/shard_map/all_to_all | solution.py:113
  201.0 1.2 collective-permute-start.20
  202.3 3.7 %collective-permute-start.21 = (f32[3072]{0:T(1024)S(1)}, f32[3072]{0:T(1024)S(1)}, u32[]{:S(2)}, u32[]{:S(2)}) collective-permute-start(f32[3072]{0:T(1024)S(1)} %add.328), channel_id=1, source_target_pairs={{0,2},{1,3},{2,0},{3,1},{4,6},{5,7},{6,4},{7,5},{8,10},{9,11},{10,... | collective-permute-start | bytes 36872 | tf_op jit(solution)/shard_map/ppermute | solution.py:65
  215.1 15.1 %collective-permute-start.24 = (bf16[640,512]{1,0:T(8,128)(2,1)S(1)}, bf16[640,512]{1,0:T(8,128)(2,1)S(1)}, u32[]{:S(2)}, u32[]{:S(2)}) collective-permute-start(bf16[640,512]{1,0:T(8,128)(2,1)S(1)} %bitcast.62), channel_id=1, source_target_pairs={{0,2},{1,3},{2,0},{3,1},{4,6},{5,7},{6,4},{7,5},{8,10},{9,11},{10,... | collective-permute-start | bytes 1966088 | tf_op jit(solution)/shard_map/ppermute | solution.py:65
  216.5 3.7 %collective-permute-start.25 = (f32[3072]{0:T(1024)S(1)}, f32[3072]{0:T(1024)S(1)}, u32[]{:S(2)}, u32[]{:S(2)}) collective-permute-start(f32[3072]{0:T(1024)S(1)} %add.329), channel_id=1, source_target_pairs={{0,4},{4,0},{1,5},{5,1},{2,6},{6,2},{3,7},{7,3},{8,12},{12,8},{9,1... | collective-permute-start | bytes 36872 | tf_op jit(solution)/shard_map/ppermute | solution.py:65
  220.2 3.7 %collective-permute-start.26 = (f32[3072]{0:T(1024)S(1)}, f32[3072]{0:T(1024)S(1)}, u32[]{:S(2)}, u32[]{:S(2)}) collective-permute-start(f32[3072]{0:T(1024)S(1)} %add.332), channel_id=1, source_target_pairs={{0,8},{8,0},{16,24},{24,16},{1,9},{9,1},{17,25},{25,17},{2,10},{10... | collective-permute-start | bytes 36872 | tf_op jit(solution)/shard_map/ppermute | solution.py:65
  223.9 4.7 %collective-permute-start.27 = (f32[3072]{0:T(1024)S(1)}, f32[3072]{0:T(1024)S(1)}, u32[]{:S(2)}, u32[]{:S(2)}) collective-permute-start(f32[3072]{0:T(1024)S(1)} %add.333), channel_id=1, source_target_pairs={{0,16},{8,24},{16,0},{24,8},{1,17},{9,25},{17,1},{25,9},{2,18},{10... | collective-permute-start | bytes 36872 | tf_op jit(solution)/shard_map/ppermute | solution.py:65
  223.9 6.3 %collective-permute-start.28 = (bf16[640,512]{1,0:T(8,128)(2,1)S(1)}, bf16[640,512]{1,0:T(8,128)(2,1)S(1)}, u32[]{:S(2)}, u32[]{:S(2)}) collective-permute-start(bf16[640,512]{1,0:T(8,128)(2,1)S(1)} %bitcast.63), channel_id=1, source_target_pairs={{0,1},{1,0},{2,3},{3,2},{4,5},{5,4},{6,7},{7,6},{8,9},{9,8},{10,11... | collective-permute-start | bytes 1966088 | tf_op jit(solution)/shard_map/ppermute | solution.py:65
  228.7 35.7 %copy-start.73 = (f32[3072]{0:T(1024)}, f32[3072]{0:T(1024)S(1)}, u32[]{:S(2)}) copy-start(f32[3072]{0:T(1024)S(1)} %add.334) | copy-start | bytes 36868
  230.2 2.1 collective-permute-start.29
  252.5 11.9 %copy-start.91 = (f32[3072]{0:T(1024)S(1)}, f32[3072]{0:T(1024)}, u32[]{:S(2)}) copy-start(f32[3072]{0:T(1024)} %param.38) | copy-start | bytes 36868
  252.5 11.9 %copy-start.92 = (f32[3072]{0:T(1024)S(1)}, f32[3072]{0:T(1024)}, u32[]{:S(2)}) copy-start(f32[3072]{0:T(1024)} %param.39) | copy-start | bytes 36868
  252.5 23.0 %copy-start = (f32[80,512]{1,0:T(8,128)S(1)}, f32[80,512]{1,0:T(8,128)}, u32[]{:S(2)}) copy-start(f32[80,512]{1,0:T(8,128)} %refs_5_.5) | copy-start | bytes 491524
  252.5 23.0 %copy-start.1 = (f32[80,512]{1,0:T(8,128)S(1)}, f32[80,512]{1,0:T(8,128)}, u32[]{:S(2)}) copy-start(f32[80,512]{1,0:T(8,128)} %refs_6_.5) | copy-start | bytes 491524
  252.5 23.0 %copy-start.2 = (f32[80,512]{1,0:T(8,128)S(1)}, f32[80,512]{1,0:T(8,128)}, u32[]{:S(2)}) copy-start(f32[80,512]{1,0:T(8,128)} %refs_7_.5) | copy-start | bytes 491524
  252.5 23.0 %copy-start.5 = (f32[80,256]{1,0:T(8,128)S(1)}, f32[80,256]{1,0:T(8,128)}, u32[]{:S(2)}) copy-start(f32[80,256]{1,0:T(8,128)} %refs_1_.3) | copy-start | bytes 245764
  252.5 23.0 %copy-start.6 = (f32[80,256]{1,0:T(8,128)S(1)}, f32[80,256]{1,0:T(8,128)}, u32[]{:S(2)}) copy-start(f32[80,256]{1,0:T(8,128)} %refs_2_.3) | copy-start | bytes 245764
  252.5 23.0 %copy-start.7 = (f32[80,256]{1,0:T(8,128)S(1)}, f32[80,256]{1,0:T(8,128)}, u32[]{:S(2)}) copy-start(f32[80,256]{1,0:T(8,128)} %refs_3_.3) | copy-start | bytes 245764
  252.5 23.0 %copy-start.8 = (f32[80,256]{1,0:T(8,128)S(1)}, f32[80,256]{1,0:T(8,128)}, u32[]{:S(2)}) copy-start(f32[80,256]{1,0:T(8,128)} %refs_4_.5) | copy-start | bytes 245764
  252.6 22.9 %all-to-all-start.7 = ((bf16[8,80,512]{2,1,0:T(8,128)(2,1)}), bf16[8,80,512]{2,1,0:T(8,128)(2,1)S(1)}, u32[]{:S(2)}, u32[]{:S(2)}) async-start(bf16[8,80,512]{2,1,0:T(8,128)(2,1)} %bitcast.23), calls=%async_computation.7 | async-start | bytes 1310720 | tf_op jit(solution)/shard_map/all_to_all | solution.py:113
  257.8 4.4 %collective-permute-start.22 = (f32[80,256]{1,0:T(8,128)S(1)}, f32[80,256]{1,0:T(8,128)S(1)}, u32[]{:S(2)}, u32[]{:S(2)}) collective-permute-start(f32[80,256]{1,0:T(8,128)S(1)} %get-tuple-element.80), channel_id=1, source_target_pairs={{0,2},{1,3},{2,0},{3,1},{4,6},{5,7},{6,4},{7,5},{8,10},{9,11},{10,... | collective-permute-start | bytes 245768 | tf_op jit(solution)/shard_map/ppermute | solution.py:65
  262.3 1.3 collective-permute-start.23
  (90 other events, 287.5 us)

commit v2 on v1

--- a/solution.py
+++ b/solution.py
@@ -349,17 +349,17 @@
         attn = jnp.concatenate([query, half, output], axis=1).astype(bf16)
         gate_up = jnp.concatenate([gate, upper], axis=1).astype(bf16)
         return (
-            repeated(attn, data_count),
+            repeated(attn, major_count),
             repeated(gate_up, major_count),
-            repeated(down.astype(bf16), major_count),
+            down.astype(bf16),
         )
 
     packed_attn, packed_gu, packed_d = on_chip(
         pack,
         [
-            jax.ShapeDtypeStruct((data_count, shard_rows, 3 * head_width), bf16),
+            jax.ShapeDtypeStruct((major_count, shard_rows, 3 * head_width), bf16),
             jax.ShapeDtypeStruct((major_count, shard_rows, 2 * hidden_width), bf16),
-            jax.ShapeDtypeStruct((major_count, shard_rows, hidden_width), bf16),
+            jax.ShapeDtypeStruct((shard_rows, hidden_width), bf16),
         ],
         w_query,
         w_key,
@@ -371,13 +371,18 @@
         flags=(my_tensor & 1).reshape(1),
         fetch=0,
     )
-    weights_attn = exchange(packed_attn, DATA).reshape(model_width, 3 * head_width)
-    packed_gu, weights_attn = lax.optimization_barrier((packed_gu, weights_attn))
+    major_attn = exchange(packed_attn, "major")
+    packed_gu, major_attn = lax.optimization_barrier((packed_gu, major_attn))
+    weights_attn = gather_minor(major_attn)
     major_gu = exchange(packed_gu, "major")
-    packed_d, major_gu = lax.optimization_barrier((packed_d, major_gu))
+    other_d = swap(packed_d, "minor", 1)
+    even = lax.axis_index("minor") == 0
+    pair_rows = jnp.concatenate(
+        [jnp.where(even, packed_d, other_d), jnp.where(even, other_d, packed_d)], axis=0
+    )
+    pair_rows, major_gu = lax.optimization_barrier((repeated(pair_rows, major_count), major_gu))
     weights_gu = gather_minor(major_gu)
-    major_d = exchange(packed_d, "major")
-    weight_d = gather_minor(major_d)
+    weight_d = exchange(pair_rows, "major").reshape(model_width, hidden_width)
     weight_q = weights_attn[:, :head_width]
     weight_half = weights_attn[:, head_width : 2 * head_width]
     weight_o = weights_attn[:, 2 * head_width :]
@@ -391,8 +396,11 @@
         axis=1,
     )
 
-    rows_in = jnp.concatenate([block_in, swap(block_in, "tensor", 2)], axis=0)
-    normed_one = both_halves(rms_norm(rows_in, pre_attn).astype(bf16))
+    other_in = swap(block_in, "tensor", 2)
+    rows_in = jnp.concatenate([block_in, other_in], axis=0)
+    normed_half = rms_norm(rows_in, pre_attn).astype(bf16)
+    other_half = swap(normed_half, "tensor", 1)
+    normed_one = jnp.concatenate([normed_half, other_half], axis=0)
     cot_rows = jnp.concatenate([d_output, swap(d_output, "tensor", 2)], axis=0)
     normed_one, cot_rows = lax.optimization_barrier((normed_one, cot_rows))
 
@@ -437,13 +445,18 @@
 
     d_branch, g_post_ffn = rms_pull(branch, post_ffn, cot_rows)
     branch_low = both_halves(d_branch.astype(bf16))
-    pair_d = pair_sum(dot_rows(branch_low, hidden).astype(bf16))
-    arrived_d = exchange(pair_d, "major")
+    grad_d = dot_rows(branch_low, hidden).astype(bf16)
+    arrived_d = exchange(grad_d.reshape(major_count, -1, hidden_width), "major")
     d_hidden = dot(branch_low, weight_d)
     d_gate, d_upper = jax.vjp(gated, gate, upper)[1](d_hidden)
     gu_low = jnp.concatenate([d_gate.astype(bf16), d_upper.astype(bf16)], axis=1)
     pair_gu = pair_sum(dot_rows(normed_two, gu_low).astype(bf16))
     pair_gu, arrived_d = lax.optimization_barrier((pair_gu, arrived_d))
+    both_d = total_of(arrived_d).reshape(2, shard_rows, hidden_width)
+    low = lax.axis_index("minor")
+    away_d = lax.dynamic_index_in_dim(both_d, 1 - low, 0, keepdims=False).astype(bf16)
+    away_d = swap(away_d, "minor", 1)
+    total_d = lax.dynamic_index_in_dim(both_d, low, 0, keepdims=False) + away_d.astype(f32)
     arrived_gu = exchange(pair_gu, "major")
     d_normed_two = row_sum(dot_cols(gu_low, weights_gu))
     d_mid_extra, g_pre_ffn = rms_pull(middle, pre_ffn, d_normed_two)
@@ -492,7 +505,7 @@
     slot = hidden_width
     owners = [index * data_count // 6 for index in range(6)]
 
-    def advance(flags, moved_d, moved_gu, moved_attn, *moments):
+    def advance(flags, whole_d, moved_gu, moved_attn, *moments):
         m_query, m_key, m_value, m_output, m_gate, m_up, m_down = moments
         low = total_of(moved_attn)
         wide = total_of(moved_gu)
@@ -502,7 +515,7 @@
             low[:, 2 * head_width :],
             wide[:, :hidden_width],
             wide[:, hidden_width:],
-            total_of(moved_d),
+            whole_d,
         )
         share = jnp.where(flags[0] < 2, 1.0, 0.0)
         even = flags[0] % 2 == 0
@@ -547,7 +560,7 @@
         [jax.ShapeDtypeStruct((data_count, shard_rows, slot), bf16)]
         + [rows_of(width) for width in widths]
         + [rows_of(widths[index]) for index in (0, 2, 3, 4, 5)],
-        arrived_d,
+        total_d,
         arrived_gu,
         arrived_attn,
         mom_query,

time: 279 us -> 278 us (level)
  other arithmetic: 32.3 us -> 27.3 us
  local copies, waits for them, and re-layouts: 14.7 us -> 18.2 us
    all_to_all x8, waiting for transfers between devices: 64.7 us -> 45.8 us  [exchange(): return lax.all_to_all(values, axis, split_axis=0, concat_axis=0, tiled=True)]
    ppermute x30 -> x31, waiting for transfers between devices: 61.3 us -> 80 us  [swap(): return lax.ppermute(values, axis, [(i, i ^ mask) for i in range(count)])]
    unnamed x233 -> x229, local copies, waits for them, and re-layouts: 9.48 us -> 12.7 us
    ppermute x30 -> x31, starting transfers between devices: 20.1 us -> 19.2 us  [swap(): return lax.ppermute(values, axis, [(i, i ^ mask) for i in range(count)])]
  transfers between devices with their start and end apart: 38 -> 39, of which waited for: 28 -> 28; matrix products, arithmetic and copies ran while one was open for 16% -> 16% of each run, Pallas kernels for 0% -> 0%
where the time goes in v2:
time: 278 us; the launch traced here: 277 us
  waiting for transfers between devices  126 us (45%)
  starting transfers between devices  55.7 us (20%)
  Pallas kernels  27.3 us (10%)
  other arithmetic  27.3 us (10%)
  matrix products  19.5 us (7%)
  local copies, waits for them, and re-layouts  18.2 us (7%)
    ppermute x31, waiting for transfers between devices, swap(): return lax.ppermute(values, axis, [(i, i ^ mask) for i in range(count)])  80 us
    all_to_all x8, waiting for transfers between devices, exchange(): return lax.all_to_all(values, axis, split_axis=0, concat_axis=0, tiled=True)  45.8 us
    all_to_all x8, starting transfers between devices, exchange(): return lax.all_to_all(values, axis, split_axis=0, concat_axis=0, tiled=True)  36.5 us
    pallas_call x1, Pallas kernels, newton_schulz(): pl.pallas_call(kernel, out_shape=jax.ShapeDtypeStruct((size, slot), bf16)...  20.2 us
    ppermute x31, starting transfers between devices, swap(): return lax.ppermute(values, axis, [(i, i ^ mask) for i in range(count)])  19.2 us
    unnamed x229, local copies, waits for them, and re-layouts  12.7 us
    dot_general x6, matrix products, dot_cols(): lax.dot_general(left, right, (((1,), (1,)), ((), ())), preferred_element_...  7.33 us
    pallas_call x3, Pallas kernels, on_chip(): pl.pallas_call(kernel, out_shape=tuple(shapes), in_specs=specs, out_specs...  7.16 us
  transfers between devices with their start and end apart: 39, of which 28 were waited for; matrix products, arithmetic and copies ran while one was open for 16% of the time, Pallas kernels for 0%

profile of v2, /device:TPU:0, one launch (start us, length us, event | category | flops | bytes accessed | tf_op | source)
XLA Modules:
  0.0 276.6 jit_solution(10543676943199336044)
XLA Ops:
  0.7 2.4 shard_map.403
  3.1 6.4 %all-to-all-start = ((bf16[4,80,768]{2,1,0:T(8,128)(2,1)}), bf16[4,80,768]{2,1,0:T(8,128)(2,1)S(1)}, u32[]{:S(2)}, u32[]{:S(2)}) async-start(bf16[4,80,768]{2,1,0:T(8,128)(2,1)} %get-tuple-element.66), calls=%async_computation | async-start | bytes 983040 | tf_op jit(solution)/shard_map/all_to_all | solution.py:113
  9.5 1.5 collective-permute-start
  14.2 5.9 %collective-permute-done = f32[128,640]{1,0:T(8,128)S(1)} collective-permute-done((f32[128,640]{1,0:T(8,128)S(1)}, f32[128,640]{1,0:T(8,128)S(1)}, u32[]{:S(2)}, u32[]{:S(2)}) %collective-permute-start) | collective-permute-done | bytes 327712 | tf_op jit(solution)/shard_map/ppermute | solution.py:65
  20.1 3.2 %all-to-all-done = bf16[4,80,768]{2,1,0:T(8,128)(2,1)S(1)} async-done(((bf16[4,80,768]{2,1,0:T(8,128)(2,1)}), bf16[4,80,768]{2,1,0:T(8,128)(2,1)S(1)}, u32[]{:S(2)}, u32[]{:S(2)}) %all-to-all-start) | async-done | bytes 491552 | tf_op jit(solution)/shard_map/all_to_all | solution.py:113
  23.3 1.5 collective-permute-start.3
  25.2 10.4 %collective-permute-done.3 = bf16[4,80,768]{2,1,0:T(8,128)(2,1)S(1)} collective-permute-done((bf16[4,80,768]{2,1,0:T(8,128)(2,1)S(1)}, bf16[4,80,768]{2,1,0:T(8,128)(2,1)S(1)}, u32[]{:S(2)}, u32[]{:S(2)}) %collective-permute-start.3) | collective-permute-done | bytes 491552 | tf_op jit(solution)/shard_map/ppermute | solution.py:65
  37.2 1.3 pad_maximum_fusion.7
  38.5 4.2 %all-to-all-start.1 = ((bf16[4,80,1024]{2,1,0:T(8,128)(2,1)}), bf16[4,80,1024]{2,1,0:T(8,128)(2,1)}, u32[]{:S(2)}, u32[]{:S(2)}) async-start(bf16[4,80,1024]{2,1,0:T(8,128)(2,1)} %get-tuple-element.69), calls=%async_computation.1 | async-start | bytes 1310720 | tf_op jit(solution)/shard_map/all_to_all | solution.py:113
  48.9 1.5 fusion.52
  51.0 1.5 collective-permute-start.8
  52.6 1.6 collective-permute-start.6
  54.1 1.3 collective-permute-done.8
  55.4 5.5 %all-to-all-done.1 = bf16[4,80,1024]{2,1,0:T(8,128)(2,1)} async-done(((bf16[4,80,1024]{2,1,0:T(8,128)(2,1)}), bf16[4,80,1024]{2,1,0:T(8,128)(2,1)}, u32[]{:S(2)}, u32[]{:S(2)}) %all-to-all-start.1) | async-done | bytes 655392 | tf_op jit(solution)/shard_map/all_to_all | solution.py:113
  61.9 1.5 collective-permute-start.9
  63.4 4.3 %all-to-all-start.2 = ((bf16[4,160,512]{2,1,0:T(8,128)(2,1)}), bf16[4,160,512]{2,1,0:T(8,128)(2,1)}, u32[]{:S(2)}, u32[]{:S(2)}) async-start(bf16[4,160,512]{2,1,0:T(8,128)(2,1)} %broadcast_in_dim.6), calls=%async_computation.2 | async-start | bytes 1310720 | tf_op jit(solution)/shard_map/all_to_all | solution.py:113
  68.6 1.4 multiply_reduce_fusion.4
  70.6 7.9 %collective-permute-done.9 = bf16[4,80,1024]{2,1,0:T(8,128)(2,1)} collective-permute-done((bf16[4,80,1024]{2,1,0:T(8,128)(2,1)}, bf16[4,80,1024]{2,1,0:T(8,128)(2,1)}, u32[]{:S(2)}, u32[]{:S(2)}) %collective-permute-start.9) | collective-permute-done | bytes 655392 | tf_op jit(solution)/shard_map/ppermute | solution.py:65
  78.4 1.4 select_bitcast_fusion.1
  81.2 1.3 copy-done.20
  84.7 1.8 fusion.88
  86.7 1.6 collective-permute-done.10
  88.4 1.6 collective-permute-start.11
  89.9 8.3 %collective-permute-done.11 = bf16[256,640]{1,0:T(8,128)(2,1)S(1)} collective-permute-done((bf16[256,640]{1,0:T(8,128)(2,1)S(1)}, bf16[256,640]{1,0:T(8,128)(2,1)S(1)}, u32[]{:S(2)}, u32[]{:S(2)}) %collective-permute-start.11) | collective-permute-done | bytes 327712 | tf_op jit(solution)/shard_map/ppermute | solution.py:65
  99.5 1.6 collective-permute-done.12
  101.2 2.4 fusion.11
  106.6 1.8 collective-permute-done.15
  108.5 2.0 fusion.21
  110.4 1.5 collective-permute-start.16
  111.9 1.4 convolution_convert_fusion.1
  113.3 4.2 %all-to-all-start.3 = ((bf16[4,160,512]{2,1,0:T(8,128)(2,1)}), bf16[4,160,512]{2,1,0:T(8,128)(2,1)}, u32[]{:S(2)}, u32[]{:S(2)}) async-start(bf16[4,160,512]{2,1,0:T(8,128)(2,1)} %bitcast.73), calls=%async_computation.3 | async-start | bytes 1310720 | tf_op jit(solution)/shard_map/all_to_all | solution.py:113
  117.5 2.3 convolution_convert_fusion
  123.6 2.4 multiply_reduce_fusion
  126.8 10.8 %collective-permute-done.13 = bf16[4,80,1024]{2,1,0:T(8,128)(2,1)} collective-permute-done((bf16[4,80,1024]{2,1,0:T(8,128)(2,1)}, bf16[4,80,1024]{2,1,0:T(8,128)(2,1)}, u32[]{:S(2)}, u32[]{:S(2)}) %collective-permute-start.13) | collective-permute-done | bytes 655392 | tf_op jit(solution)/shard_map/ppermute | solution.py:65
  137.6 2.4 fusion.3
  139.9 4.8 %all-to-all-start.4 = ((bf16[4,80,1024]{2,1,0:T(8,128)(2,1)}), bf16[4,80,1024]{2,1,0:T(8,128)(2,1)S(1)}, u32[]{:S(2)}, u32[]{:S(2)}) async-start(bf16[4,80,1024]{2,1,0:T(8,128)(2,1)} %fusion.3), calls=%async_computation.4 | async-start | bytes 1310720 | tf_op jit(solution)/shard_map/all_to_all | solution.py:113
  144.7 1.6 multiply_reduce_fusion.11
  154.1 6.8 %all-to-all-done.4.refs_2_ = bf16[4,80,1024]{2,1,0:T(8,128)(2,1)S(1)} async-done(((bf16[4,80,1024]{2,1,0:T(8,128)(2,1)}), bf16[4,80,1024]{2,1,0:T(8,128)(2,1)S(1)}, u32[]{:S(2)}, u32[]{:S(2)}) %all-to-all-start.4) | async-done | bytes 655392 | tf_op jit(solution)/shard_map/all_to_all | solution.py:113
  160.9 1.4 copy.69
  162.3 3.7 %all-to-all-start.5 = ((bf16[8,80,768]{2,1,0:T(8,128)(2,1)}), bf16[8,80,768]{2,1,0:T(8,128)(2,1)S(1)}, u32[]{:S(2)}, u32[]{:S(2)}) async-start(bf16[8,80,768]{2,1,0:T(8,128)(2,1)} %bitcast.65), calls=%async_computation.5 | async-start | bytes 1966080 | tf_op jit(solution)/shard_map/all_to_all | solution.py:113
  166.8 2.2 fusion.13
  169.2 1.5 fusion.47
  170.6 1.2 convert_reduce_fusion
  172.0 2.0 collective-permute-start.14
  174.7 4.3 %collective-permute-done.14 = bf16[80,512]{1,0:T(8,128)(2,1)S(1)} collective-permute-done((bf16[80,512]{1,0:T(8,128)(2,1)S(1)}, bf16[80,512]{1,0:T(8,128)(2,1)S(1)}, u32[]{:S(2)}, u32[]{:S(2)}) %collective-permute-start.14) | collective-permute-done | bytes 81952 | tf_op jit(solution)/shard_map/ppermute | solution.py:65
  179.0 1.4 collective-permute-done.20
  181.2 8.8 %all-to-all-done.5.refs_3_ = bf16[8,80,768]{2,1,0:T(8,128)(2,1)S(1)} async-done(((bf16[8,80,768]{2,1,0:T(8,128)(2,1)}), bf16[8,80,768]{2,1,0:T(8,128)(2,1)S(1)}, u32[]{:S(2)}, u32[]{:S(2)}) %all-to-all-start.5) | async-done | bytes 983072 | tf_op jit(solution)/shard_map/all_to_all | solution.py:113
  190.1 2.7 shard_map.404
  192.9 3.7 %all-to-all-start.6 = ((bf16[8,80,512]{2,1,0:T(8,128)(2,1)}), bf16[8,80,512]{2,1,0:T(8,128)(2,1)S(1)}, u32[]{:S(2)}, u32[]{:S(2)}) async-start(bf16[8,80,512]{2,1,0:T(8,128)(2,1)} %get-tuple-element.77), calls=%async_computation.6 | async-start | bytes 1310720 | tf_op jit(solution)/shard_map/all_to_all | solution.py:113
  196.6 1.3 constant_dynamic-update-slice_fusion.2
  200.7 3.2 %collective-permute-done.22 = f32[3072]{0:T(1024)S(1)} collective-permute-done((f32[3072]{0:T(1024)S(1)}, f32[3072]{0:T(1024)S(1)}, u32[]{:S(2)}, u32[]{:S(2)}) %collective-permute-start.22) | collective-permute-done | bytes 12320 | tf_op jit(solution)/shard_map/ppermute | solution.py:65
  203.9 10.0 %all-to-all-done.6 = bf16[8,80,512]{2,1,0:T(8,128)(2,1)S(1)} async-done(((bf16[8,80,512]{2,1,0:T(8,128)(2,1)}), bf16[8,80,512]{2,1,0:T(8,128)(2,1)S(1)}, u32[]{:S(2)}, u32[]{:S(2)}) %all-to-all-start.6) | async-done | bytes 655392 | tf_op jit(solution)/shard_map/all_to_all | solution.py:113
  214.4 1.5 collective-permute-start.26
  215.9 2.2 collective-permute-done.26
  218.7 3.1 %collective-permute-done.27 = f32[3072]{0:T(1024)S(1)} collective-permute-done((f32[3072]{0:T(1024)S(1)}, f32[3072]{0:T(1024)S(1)}, u32[]{:S(2)}, u32[]{:S(2)}) %collective-permute-start.27) | collective-permute-done | bytes 12320 | tf_op jit(solution)/shard_map/ppermute | solution.py:65
  221.9 4.6 %collective-permute-done.28 = f32[3072]{0:T(1024)S(1)} collective-permute-done((f32[3072]{0:T(1024)S(1)}, f32[3072]{0:T(1024)S(1)}, u32[]{:S(2)}, u32[]{:S(2)}) %collective-permute-start.28) | collective-permute-done | bytes 12320 | tf_op jit(solution)/shard_map/ppermute | solution.py:65
  226.5 2.6 collective-permute-done.25.across_ref
  229.0 2.1 collective-permute-done.30.far_ref
  231.1 20.2 %shard_map.405 = bf16[640,512]{1,0:T(8,128)(2,1)} custom-call(s32[1]{0:T(128)} %bitcast.23.flag_ref, bf16[640,512]{1,0:T(8,128)(2,1)S(1)} %bitcast.62, bf16[640,512]{1,0:T(8,128)(2,1)S(1)} %collective-permute-done.29.near_ref, bf16[640,512]{1,0:T(8,128)(2,1)S(1)} %collective-permute-done.25.across_ref, bf16[640,512]{1,0:T(8,128)(2,1)S(1)} %collective-permute-done.30.far_ref), custom_call_target="tpu_custom_call" | custom-call | tf_op jit(solution)/shard_map/pallas_call | solution.py:284
  251.4 5.3 %all-to-all-start.7 = ((bf16[8,80,512]{2,1,0:T(8,128)(2,1)}), bf16[8,80,512]{2,1,0:T(8,128)(2,1)S(1)}, u32[]{:S(2)}, u32[]{:S(2)}) async-start(bf16[8,80,512]{2,1,0:T(8,128)(2,1)} %bitcast.24), calls=%async_computation.7 | async-start | bytes 1310720 | tf_op jit(solution)/shard_map/all_to_all | solution.py:113
  257.2 3.9 %collective-permute-done.23 = f32[80,256]{1,0:T(8,128)S(1)} collective-permute-done((f32[80,256]{1,0:T(8,128)S(1)}, f32[80,256]{1,0:T(8,128)S(1)}, u32[]{:S(2)}, u32[]{:S(2)}) %collective-permute-start.23) | collective-permute-done | bytes 81952 | tf_op jit(solution)/shard_map/ppermute | solution.py:65
  261.2 1.3 collective-permute-done.24
  263.9 10.4 %all-to-all-done.7.refs_0_ = bf16[8,80,512]{2,1,0:T(8,128)(2,1)S(1)} async-done(((bf16[8,80,512]{2,1,0:T(8,128)(2,1)}), bf16[8,80,512]{2,1,0:T(8,128)(2,1)S(1)}, u32[]{:S(2)}, u32[]{:S(2)}) %all-to-all-start.7) | async-done | bytes 655392 | tf_op jit(solution)/shard_map/all_to_all | solution.py:113
  274.3 2.0 shard_map.406
  (367 shorter events, 42.4 us)
Async XLA Ops:
  0.7 12.1 %copy-start.61 = (f32[3072]{0:T(1024)S(1)}, f32[3072]{0:T(1024)}, u32[]{:S(2)}) copy-start(f32[3072]{0:T(1024)} %param.37) | copy-start | bytes 36868
  3.1 20.1 %all-to-all-start = ((bf16[4,80,768]{2,1,0:T(8,128)(2,1)}), bf16[4,80,768]{2,1,0:T(8,128)(2,1)S(1)}, u32[]{:S(2)}, u32[]{:S(2)}) async-start(bf16[4,80,768]{2,1,0:T(8,128)(2,1)} %get-tuple-element.66), calls=%async_computation | async-start | bytes 983040 | tf_op jit(solution)/shard_map/all_to_all | solution.py:113
  9.5 10.6 %collective-permute-start = (f32[128,640]{1,0:T(8,128)S(1)}, f32[128,640]{1,0:T(8,128)S(1)}, u32[]{:S(2)}, u32[]{:S(2)}) collective-permute-start(f32[128,640]{1,0:T(8,128)S(1)} %copy-done.30), channel_id=1, source_target_pairs={{0,2},{1,3},{2,0},{3,1},{4,6},{5,7},{6,4},{7,5},{8,10},{9,11},{10,... | collective-permute-start | bytes 983048 | tf_op jit(solution)/shard_map/ppermute | solution.py:65
  11.0 26.1 %collective-permute-start.2 = (f32[128,640]{1,0:T(8,128)S(1)}, f32[128,640]{1,0:T(8,128)S(1)}, u32[]{:S(2)}, u32[]{:S(2)}) collective-permute-start(f32[128,640]{1,0:T(8,128)S(1)} %copy-done.53), channel_id=1, source_target_pairs={{0,2},{1,3},{2,0},{3,1},{4,6},{5,7},{6,4},{7,5},{8,10},{9,11},{10,... | collective-permute-start | bytes 983048 | tf_op jit(solution)/shard_map/ppermute | solution.py:65
  12.8 34.0 %copy-start.33 = (f32[512,128]{1,0:T(8,128)}, f32[512,128]{1,0:T(8,128)S(1)}, u32[]{:S(2)}) copy-start(f32[512,128]{1,0:T(8,128)S(1)} %get-tuple-element.181) | copy-start | bytes 786436
  12.8 34.0 %copy-start.35 = (f32[512,128]{1,0:T(8,128)}, f32[512,128]{1,0:T(8,128)S(1)}, u32[]{:S(2)}) copy-start(f32[512,128]{1,0:T(8,128)S(1)} %get-tuple-element.180) | copy-start | bytes 786436
  20.1 15.5 %copy-start.22 = (f32[256,640]{1,0:T(8,128)}, f32[256,640]{1,0:T(8,128)S(1)}, u32[]{:S(2)}) copy-start(f32[256,640]{1,0:T(8,128)S(1)} %constant_dynamic-update-slice_fusion) | copy-start | bytes 1966084
  23.3 12.2 %collective-permute-start.3 = (bf16[4,80,768]{2,1,0:T(8,128)(2,1)S(1)}, bf16[4,80,768]{2,1,0:T(8,128)(2,1)S(1)}, u32[]{:S(2)}, u32[]{:S(2)}) collective-permute-start(bf16[4,80,768]{2,1,0:T(8,128)(2,1)S(1)} %all-to-all-done), channel_id=1, source_target_pairs={{0,4},{4,0},{1,5},{5,1},{2,6},{6,2},{3,7},{7,3},{8,12},{12,8},{9,1... | collective-permute-start | bytes 1474568 | tf_op jit(solution)/shard_map/ppermute | solution.py:65
  25.1 12.1 %collective-permute-start.1 = (bf16[256,640]{1,0:T(8,128)(2,1)S(1)}, bf16[256,640]{1,0:T(8,128)(2,1)}, u32[]{:S(2)}, u32[]{:S(2)}) collective-permute-start(bf16[256,640]{1,0:T(8,128)(2,1)S(1)} %multiply_convert_fusion.3), channel_id=1, source_target_pairs={{0,1},{1,0},{2,3},{3,2},{4,5},{5,4},{6,7},{7,6},{8,9},{9,8},{10,11... | collective-permute-start | bytes 983048 | tf_op jit(solution)/shard_map/ppermute | solution.py:65
  37.0 6.6 %collective-permute-start.4 = (bf16[640,256]{0,1:T(8,128)(2,1)S(1)}, bf16[640,256]{0,1:T(8,128)(2,1)S(1)}, u32[]{:S(2)}, u32[]{:S(2)}) collective-permute-start(bf16[640,256]{0,1:T(8,128)(2,1)S(1)} %copy.76), channel_id=1, source_target_pairs={{0,1},{1,0},{2,3},{3,2},{4,5},{5,4},{6,7},{7,6},{8,9},{9,8},{10,11... | collective-permute-start | bytes 983048 | tf_op jit(solution)/shard_map/ppermute | solution.py:65
  37.2 86.3 %copy-start.16 = (f32[256,640]{1,0:T(8,128)}, f32[256,640]{1,0:T(8,128)S(1)}, u32[]{:S(2)}) copy-start(f32[256,640]{1,0:T(8,128)S(1)} %pad_maximum_fusion.8) | copy-start | bytes 1966084
  38.5 22.5 %all-to-all-start.1 = ((bf16[4,80,1024]{2,1,0:T(8,128)(2,1)}), bf16[4,80,1024]{2,1,0:T(8,128)(2,1)}, u32[]{:S(2)}, u32[]{:S(2)}) async-start(bf16[4,80,1024]{2,1,0:T(8,128)(2,1)} %get-tuple-element.69), calls=%async_computation.1 | async-start | bytes 1310720 | tf_op jit(solution)/shard_map/all_to_all | solution.py:113
  50.4 2.1 collective-permute-start.5
  51.0 4.4 %collective-permute-start.8 = (bf16[80,512]{1,0:T(8,128)(2,1)S(1)}, bf16[80,512]{1,0:T(8,128)(2,1)S(1)}, u32[]{:S(2)}, u32[]{:S(2)}) collective-permute-start(bf16[80,512]{1,0:T(8,128)(2,1)S(1)} %copy-done.60), channel_id=1, source_target_pairs={{0,4},{4,0},{1,5},{5,1},{2,6},{6,2},{3,7},{7,3},{8,12},{12,8},{9,1... | collective-permute-start | bytes 245768 | tf_op jit(solution)/shard_map/ppermute | solution.py:65
  52.6 15.2 %collective-permute-start.6 = (bf16[256,640]{1,0:T(8,128)(2,1)S(1)}, bf16[256,640]{1,0:T(8,128)(2,1)S(1)}, u32[]{:S(2)}, u32[]{:S(2)}) collective-permute-start(bf16[256,640]{1,0:T(8,128)(2,1)S(1)} %fusion.23), channel_id=1, source_target_pairs={{0,2},{1,3},{2,0},{3,1},{4,6},{5,7},{6,4},{7,5},{8,10},{9,11},{10,... | collective-permute-start | bytes 983048 | tf_op jit(solution)/shard_map/ppermute | solution.py:65
  61.9 16.6 %collective-permute-start.9 = (bf16[4,80,1024]{2,1,0:T(8,128)(2,1)}, bf16[4,80,1024]{2,1,0:T(8,128)(2,1)}, u32[]{:S(2)}, u32[]{:S(2)}) collective-permute-start(bf16[4,80,1024]{2,1,0:T(8,128)(2,1)} %all-to-all-done.1), channel_id=1, source_target_pairs={{0,4},{4,0},{1,5},{5,1},{2,6},{6,2},{3,7},{7,3},{8,12},{12,8},{9,1... | collective-permute-start | bytes 1966088 | tf_op jit(solution)/shard_map/ppermute | solution.py:65
  63.4 21.3 %all-to-all-start.2 = ((bf16[4,160,512]{2,1,0:T(8,128)(2,1)}), bf16[4,160,512]{2,1,0:T(8,128)(2,1)}, u32[]{:S(2)}, u32[]{:S(2)}) async-start(bf16[4,160,512]{2,1,0:T(8,128)(2,1)} %broadcast_in_dim.6), calls=%async_computation.2 | async-start | bytes 1310720 | tf_op jit(solution)/shard_map/all_to_all | solution.py:113
  69.9 53.6 %copy-start.18 = (f32[256,640]{1,0:T(8,128)}, f32[256,640]{1,0:T(8,128)S(1)}, u32[]{:S(2)}) copy-start(f32[256,640]{1,0:T(8,128)S(1)} %get-tuple-element.127) | copy-start | bytes 1966084
  70.1 9.9 %collective-permute-start.7 = (bf16[256,640]{1,0:T(8,128)(2,1)S(1)}, bf16[256,640]{1,0:T(8,128)(2,1)S(1)}, u32[]{:S(2)}, u32[]{:S(2)}) collective-permute-start(bf16[256,640]{1,0:T(8,128)(2,1)S(1)} %multiply_convert_fusion.2), channel_id=1, source_target_pairs={{0,1},{1,0},{2,3},{3,2},{4,5},{5,4},{6,7},{7,6},{8,9},{9,8},{10,11... | collective-permute-start | bytes 983048 | tf_op jit(solution)/shard_map/ppermute | solution.py:65
  86.6 1.7 collective-permute-start.10
  88.4 9.8 %collective-permute-start.11 = (bf16[256,640]{1,0:T(8,128)(2,1)S(1)}, bf16[256,640]{1,0:T(8,128)(2,1)S(1)}, u32[]{:S(2)}, u32[]{:S(2)}) collective-permute-start(bf16[256,640]{1,0:T(8,128)(2,1)S(1)} %fusion.22), channel_id=1, source_target_pairs={{0,2},{1,3},{2,0},{3,1},{4,6},{5,7},{6,4},{7,5},{8,10},{9,11},{10,... | collective-permute-start | bytes 983048 | tf_op jit(solution)/shard_map/ppermute | solution.py:65
  99.5 1.6 collective-permute-start.12
  106.5 2.0 collective-permute-start.15
  110.4 10.8 %collective-permute-start.16 = (bf16[256,640]{1,0:T(8,128)(2,1)}, bf16[256,640]{1,0:T(8,128)(2,1)}, u32[]{:S(2)}, u32[]{:S(2)}) collective-permute-start(bf16[256,640]{1,0:T(8,128)(2,1)} %fusion.21), channel_id=1, source_target_pairs={{0,2},{1,3},{2,0},{3,1},{4,6},{5,7},{6,4},{7,5},{8,10},{9,11},{10,... | collective-permute-start | bytes 983048 | tf_op jit(solution)/shard_map/ppermute | solution.py:65
  113.3 26.6 %all-to-all-start.3 = ((bf16[4,160,512]{2,1,0:T(8,128)(2,1)}), bf16[4,160,512]{2,1,0:T(8,128)(2,1)}, u32[]{:S(2)}, u32[]{:S(2)}) async-start(bf16[4,160,512]{2,1,0:T(8,128)(2,1)} %bitcast.73), calls=%async_computation.3 | async-start | bytes 1310720 | tf_op jit(solution)/shard_map/all_to_all | solution.py:113
  120.7 16.8 %collective-permute-start.13 = (bf16[4,80,1024]{2,1,0:T(8,128)(2,1)}, bf16[4,80,1024]{2,1,0:T(8,128)(2,1)}, u32[]{:S(2)}, u32[]{:S(2)}) collective-permute-start(bf16[4,80,1024]{2,1,0:T(8,128)(2,1)} %dynamic-slice_bitcast_fusion), channel_id=1, source_target_pairs={{0,4},{4,0},{1,5},{5,1},{2,6},{6,2},{3,7},{7,3},{8,12},{12,8},{9,1... | collective-permute-start | bytes 1966088 | tf_op jit(solution)/shard_map/ppermute | solution.py:65
  126.8 17.9 %collective-permute-start.17 = (bf16[256,640]{1,0:T(8,128)(2,1)S(1)}, bf16[256,640]{1,0:T(8,128)(2,1)S(1)}, u32[]{:S(2)}, u32[]{:S(2)}) collective-permute-start(bf16[256,640]{1,0:T(8,128)(2,1)S(1)} %subtract_convert_fusion), channel_id=1, source_target_pairs={{0,1},{1,0},{2,3},{3,2},{4,5},{5,4},{6,7},{7,6},{8,9},{9,8},{10,11... | collective-permute-start | bytes 983048 | tf_op jit(solution)/shard_map/ppermute | solution.py:65
  126.8 17.9 %copy-start.51 = (bf16[512,256]{0,1:T(8,128)(2,1)S(1)}, bf16[512,256]{0,1:T(8,128)(2,1)}, u32[]{:S(2)}) copy-start(bf16[512,256]{0,1:T(8,128)(2,1)} %copy-done.50) | copy-start | bytes 786436
  139.9 21.0 %all-to-all-start.4 = ((bf16[4,80,1024]{2,1,0:T(8,128)(2,1)}), bf16[4,80,1024]{2,1,0:T(8,128)(2,1)S(1)}, u32[]{:S(2)}, u32[]{:S(2)}) async-start(bf16[4,80,1024]{2,1,0:T(8,128)(2,1)} %fusion.3), calls=%async_computation.4 | async-start | bytes 1310720 | tf_op jit(solution)/shard_map/all_to_all | solution.py:113
  152.2 1.7 collective-permute-start.18
  162.3 27.7 %all-to-all-start.5 = ((bf16[8,80,768]{2,1,0:T(8,128)(2,1)}), bf16[8,80,768]{2,1,0:T(8,128)(2,1)S(1)}, u32[]{:S(2)}, u32[]{:S(2)}) async-start(bf16[8,80,768]{2,1,0:T(8,128)(2,1)} %bitcast.65), calls=%async_computation.5 | async-start | bytes 1966080 | tf_op jit(solution)/shard_map/all_to_all | solution.py:113
  166.0 14.4 %copy-start.100 = (f32[128]{0:T(128)}, f32[128]{0:T(128)S(1)}, u32[]{:S(2)}) copy-start(f32[128]{0:T(128)S(1)} %add_rsqrt_fusion.6) | copy-start | bytes 1540
  169.1 4.9 %collective-permute-start.19 = (bf16[256,640]{1,0:T(8,128)(2,1)S(1)}, bf16[256,640]{1,0:T(8,128)(2,1)S(1)}, u32[]{:S(2)}, u32[]{:S(2)}) collective-permute-start(bf16[256,640]{1,0:T(8,128)(2,1)S(1)} %slice.322), channel_id=1, source_target_pairs={{0,1},{1,0},{2,3},{3,2},{4,5},{5,4},{6,7},{7,6},{8,9},{9,8},{10,11... | collective-permute-start | bytes 983048 | tf_op jit(solution)/shard_map/ppermute | solution.py:65
  171.9 18.1 %copy-start.3 = (f32[80,256]{1,0:T(8,128)S(1)}, f32[80,256]{1,0:T(8,128)}, u32[]{:S(2)}) copy-start(f32[80,256]{1,0:T(8,128)} %refs_5_.4) | copy-start | bytes 245764
  171.9 18.1 %copy-start.4 = (f32[80,256]{1,0:T(8,128)S(1)}, f32[80,256]{1,0:T(8,128)}, u32[]{:S(2)}) copy-start(f32[80,256]{1,0:T(8,128)} %refs_6_.4) | copy-start | bytes 245764
  171.9 18.1 %copy-start.9 = (f32[80,512]{1,0:T(8,128)S(1)}, f32[80,512]{1,0:T(8,128)}, u32[]{:S(2)}) copy-start(f32[80,512]{1,0:T(8,128)} %refs_8_.1) | copy-start | bytes 491524
  171.9 18.1 %copy-start.10 = (f32[80,512]{1,0:T(8,128)S(1)}, f32[80,512]{1,0:T(8,128)}, u32[]{:S(2)}) copy-start(f32[80,512]{1,0:T(8,128)} %refs_9_.1) | copy-start | bytes 491524
  171.9 18.1 %copy-start.11 = (f32[80,512]{1,0:T(8,128)S(1)}, f32[80,512]{1,0:T(8,128)}, u32[]{:S(2)}) copy-start(f32[80,512]{1,0:T(8,128)} %refs_10_.1) | copy-start | bytes 491524
  171.9 18.1 %copy-start.12 = (f32[80,256]{1,0:T(8,128)S(1)}, f32[80,256]{1,0:T(8,128)}, u32[]{:S(2)}) copy-start(f32[80,256]{1,0:T(8,128)} %refs_4_.4) | copy-start | bytes 245764
  172.0 18.1 %copy-start.13 = (f32[80,256]{1,0:T(8,128)S(1)}, f32[80,256]{1,0:T(8,128)}, u32[]{:S(2)}) copy-start(f32[80,256]{1,0:T(8,128)} %refs_7_.4) | copy-start | bytes 245764
  172.0 7.0 %collective-permute-start.14 = (bf16[80,512]{1,0:T(8,128)(2,1)S(1)}, bf16[80,512]{1,0:T(8,128)(2,1)S(1)}, u32[]{:S(2)}, u32[]{:S(2)}) collective-permute-start(bf16[80,512]{1,0:T(8,128)(2,1)S(1)} %fusion.56), channel_id=1, source_target_pairs={{0,4},{4,0},{1,5},{5,1},{2,6},{6,2},{3,7},{7,3},{8,12},{12,8},{9,1... | collective-permute-start | bytes 245768 | tf_op jit(solution)/shard_map/ppermute | solution.py:65
  174.0 6.4 %collective-permute-start.20 = (bf16[128,640]{1,0:T(8,128)(2,1)S(1)}, bf16[128,640]{1,0:T(8,128)(2,1)S(1)}, u32[]{:S(2)}, u32[]{:S(2)}) collective-permute-start(bf16[128,640]{1,0:T(8,128)(2,1)S(1)} %slice.226), channel_id=1, source_target_pairs={{0,2},{1,3},{2,0},{3,1},{4,6},{5,7},{6,4},{7,5},{8,10},{9,11},{10,... | collective-permute-start | bytes 491528 | tf_op jit(solution)/shard_map/ppermute | solution.py:65
  192.9 21.0 %all-to-all-start.6 = ((bf16[8,80,512]{2,1,0:T(8,128)(2,1)}), bf16[8,80,512]{2,1,0:T(8,128)(2,1)S(1)}, u32[]{:S(2)}, u32[]{:S(2)}) async-start(bf16[8,80,512]{2,1,0:T(8,128)(2,1)} %get-tuple-element.77), calls=%async_computation.6 | async-start | bytes 1310720 | tf_op jit(solution)/shard_map/all_to_all | solution.py:113
  199.0 1.2 collective-permute-start.21
  200.2 3.7 %collective-permute-start.22 = (f32[3072]{0:T(1024)S(1)}, f32[3072]{0:T(1024)S(1)}, u32[]{:S(2)}, u32[]{:S(2)}) collective-permute-start(f32[3072]{0:T(1024)S(1)} %add.328), channel_id=1, source_target_pairs={{0,2},{1,3},{2,0},{3,1},{4,6},{5,7},{6,4},{7,5},{8,10},{9,11},{10,... | collective-permute-start | bytes 36872 | tf_op jit(solution)/shard_map/ppermute | solution.py:65
  213.9 15.1 %collective-permute-start.25 = (bf16[640,512]{1,0:T(8,128)(2,1)S(1)}, bf16[640,512]{1,0:T(8,128)(2,1)S(1)}, u32[]{:S(2)}, u32[]{:S(2)}) collective-permute-start(bf16[640,512]{1,0:T(8,128)(2,1)S(1)} %bitcast.60), channel_id=1, source_target_pairs={{0,2},{1,3},{2,0},{3,1},{4,6},{5,7},{6,4},{7,5},{8,10},{9,11},{10,... | collective-permute-start | bytes 1966088 | tf_op jit(solution)/shard_map/ppermute | solution.py:65
  214.4 3.7 %collective-permute-start.26 = (f32[3072]{0:T(1024)S(1)}, f32[3072]{0:T(1024)S(1)}, u32[]{:S(2)}, u32[]{:S(2)}) collective-permute-start(f32[3072]{0:T(1024)S(1)} %add.329), channel_id=1, source_target_pairs={{0,4},{4,0},{1,5},{5,1},{2,6},{6,2},{3,7},{7,3},{8,12},{12,8},{9,1... | collective-permute-start | bytes 36872 | tf_op jit(solution)/shard_map/ppermute | solution.py:65
  218.1 3.7 %collective-permute-start.27 = (f32[3072]{0:T(1024)S(1)}, f32[3072]{0:T(1024)S(1)}, u32[]{:S(2)}, u32[]{:S(2)}) collective-permute-start(f32[3072]{0:T(1024)S(1)} %add.332), channel_id=1, source_target_pairs={{0,8},{8,0},{16,24},{24,16},{1,9},{9,1},{17,25},{25,17},{2,10},{10... | collective-permute-start | bytes 36872 | tf_op jit(solution)/shard_map/ppermute | solution.py:65
  221.8 4.6 %collective-permute-start.28 = (f32[3072]{0:T(1024)S(1)}, f32[3072]{0:T(1024)S(1)}, u32[]{:S(2)}, u32[]{:S(2)}) collective-permute-start(f32[3072]{0:T(1024)S(1)} %add.333), channel_id=1, source_target_pairs={{0,16},{8,24},{16,0},{24,8},{1,17},{9,25},{17,1},{25,9},{2,18},{10... | collective-permute-start | bytes 36872 | tf_op jit(solution)/shard_map/ppermute | solution.py:65
  221.8 7.2 %collective-permute-start.29 = (bf16[640,512]{1,0:T(8,128)(2,1)S(1)}, bf16[640,512]{1,0:T(8,128)(2,1)S(1)}, u32[]{:S(2)}, u32[]{:S(2)}) collective-permute-start(bf16[640,512]{1,0:T(8,128)(2,1)S(1)} %bitcast.61), channel_id=1, source_target_pairs={{0,1},{1,0},{2,3},{3,2},{4,5},{5,4},{6,7},{7,6},{8,9},{9,8},{10,11... | collective-permute-start | bytes 1966088 | tf_op jit(solution)/shard_map/ppermute | solution.py:65
  226.5 36.8 %copy-start.67 = (f32[3072]{0:T(1024)}, f32[3072]{0:T(1024)S(1)}, u32[]{:S(2)}) copy-start(f32[3072]{0:T(1024)S(1)} %add.334) | copy-start | bytes 36868
  229.0 2.1 collective-permute-start.30
  251.3 11.9 %copy-start.85 = (f32[3072]{0:T(1024)S(1)}, f32[3072]{0:T(1024)}, u32[]{:S(2)}) copy-start(f32[3072]{0:T(1024)} %param.38) | copy-start | bytes 36868
  251.3 11.9 %copy-start.86 = (f32[3072]{0:T(1024)S(1)}, f32[3072]{0:T(1024)}, u32[]{:S(2)}) copy-start(f32[3072]{0:T(1024)} %param.39) | copy-start | bytes 36868
  251.3 23.0 %copy-start = (f32[80,512]{1,0:T(8,128)S(1)}, f32[80,512]{1,0:T(8,128)}, u32[]{:S(2)}) copy-start(f32[80,512]{1,0:T(8,128)} %refs_5_.5) | copy-start | bytes 491524
  251.3 23.0 %copy-start.1 = (f32[80,512]{1,0:T(8,128)S(1)}, f32[80,512]{1,0:T(8,128)}, u32[]{:S(2)}) copy-start(f32[80,512]{1,0:T(8,128)} %refs_6_.5) | copy-start | bytes 491524
  251.3 23.0 %copy-start.2 = (f32[80,512]{1,0:T(8,128)S(1)}, f32[80,512]{1,0:T(8,128)}, u32[]{:S(2)}) copy-start(f32[80,512]{1,0:T(8,128)} %refs_7_.5) | copy-start | bytes 491524
  251.3 23.0 %copy-start.5 = (f32[80,256]{1,0:T(8,128)S(1)}, f32[80,256]{1,0:T(8,128)}, u32[]{:S(2)}) copy-start(f32[80,256]{1,0:T(8,128)} %refs_1_.3) | copy-start | bytes 245764
  251.3 23.0 %copy-start.6 = (f32[80,256]{1,0:T(8,128)S(1)}, f32[80,256]{1,0:T(8,128)}, u32[]{:S(2)}) copy-start(f32[80,256]{1,0:T(8,128)} %refs_2_.3) | copy-start | bytes 245764
  251.4 23.0 %copy-start.7 = (f32[80,256]{1,0:T(8,128)S(1)}, f32[80,256]{1,0:T(8,128)}, u32[]{:S(2)}) copy-start(f32[80,256]{1,0:T(8,128)} %refs_3_.3) | copy-start | bytes 245764
  251.4 23.0 %copy-start.8 = (f32[80,256]{1,0:T(8,128)S(1)}, f32[80,256]{1,0:T(8,128)}, u32[]{:S(2)}) copy-start(f32[80,256]{1,0:T(8,128)} %refs_4_.5) | copy-start | bytes 245764
  251.4 22.9 %all-to-all-start.7 = ((bf16[8,80,512]{2,1,0:T(8,128)(2,1)}), bf16[8,80,512]{2,1,0:T(8,128)(2,1)S(1)}, u32[]{:S(2)}, u32[]{:S(2)}) async-start(bf16[8,80,512]{2,1,0:T(8,128)(2,1)} %bitcast.24), calls=%async_computation.7 | async-start | bytes 1310720 | tf_op jit(solution)/shard_map/all_to_all | solution.py:113
  256.7 4.4 %collective-permute-start.23 = (f32[80,256]{1,0:T(8,128)S(1)}, f32[80,256]{1,0:T(8,128)S(1)}, u32[]{:S(2)}, u32[]{:S(2)}) collective-permute-start(f32[80,256]{1,0:T(8,128)S(1)} %get-tuple-element.80), channel_id=1, source_target_pairs={{0,2},{1,3},{2,0},{3,1},{4,6},{5,7},{6,4},{7,5},{8,10},{9,11},{10,... | collective-permute-start | bytes 245768 | tf_op jit(solution)/shard_map/ppermute | solution.py:65
  261.1 1.3 collective-permute-start.24
  (88 other events, 279.7 us)

commit v3 on v2

--- a/solution.py
+++ b/solution.py
@@ -248,24 +248,32 @@
             rest = slope * shift + POLY_THIRD * dot(shift16, shift16)
             rest16 = rest.astype(bf16)
 
-            @pl.when(index == 0)
-            def _():
-                product[...] = jnp.where(eye, level, 0.0) + rest
-
-            @pl.when(index > 0)
-            def _():
-                before = product[...]
-                product[...] = level * before + dot(rest16, before.astype(bf16))
-
-            @pl.when(index < NS_STEPS - 1)
-            def _():
-                wide = 2.0 * level * rest + dot(rest16, rest16)
+            def advance(square_rest):
+                wide = 2.0 * level * rest + square_rest
                 gram[...] = (
                     jnp.where(eye, level * level * mean, 0.0)
                     + level * level * shift
                     + mean * wide
                     + dot(wide.astype(bf16), shift16)
                 )
+
+            @pl.when(index == 0)
+            def _():
+                product[...] = jnp.where(eye, level, 0.0) + rest
+                advance(dot(rest16, rest16))
+
+            @pl.when((index > 0) & (index < NS_STEPS - 1))
+            def _():
+                before = product[...]
+                pair = jnp.concatenate([before.astype(bf16), rest16], axis=1)
+                made = dot(rest16, pair)
+                product[...] = level * before + made[:, :size]
+                advance(made[:, size:])
+
+            @pl.when(index == NS_STEPS - 1)
+            def _():
+                before = product[...]
+                product[...] = level * before + dot(rest16, before.astype(bf16))
 
             return carry
 
@@ -482,10 +490,10 @@
     got = swap(jnp.where(first_core, grad_value, grad_key).astype(bf16), "tensor", 1)
     grad_half = jnp.where(first_core, grad_key, grad_value) + got.astype(f32)
     grad_query = dot_rows(normed_one, qkv_low[:, :head_width])
+    grad_o, arrived_gu = lax.optimization_barrier((grad_o, arrived_gu))
     grad_attn = jnp.concatenate(
         [grad_query.astype(bf16), grad_half.astype(bf16), grad_o], axis=1
     )
-    grad_attn, arrived_gu = lax.optimization_barrier((grad_attn, arrived_gu))
     arrived_attn = exchange(grad_attn.reshape(data_count, shard_rows, -1), DATA)
 
     d_normed_one = row_sum_own(dot_cols(qkv_low, weights_qkv))
@@ -571,7 +579,6 @@
         mom_up,
         mom_down,
         flags=my_tensor.reshape(1),
-        fetch=3,
         limit=24 * 1024 * 1024,
     )
     outgoing, sum_query, part_kv, sum_output, sum_gate, sum_up, sum_down = made[:7]
@@ -612,7 +619,7 @@
         return tuple(results)
 
     updated = on_chip(
-        renew, [rows_of(weight.shape[1]) for weight in weights], returned, *weights, fetch=1,
+        renew, [rows_of(weight.shape[1]) for weight in weights], returned, *weights,
         limit=24 * 1024 * 1024,
     )
     next_first = FIRST_DECAY * adam_first + (1.0 - FIRST_DECAY) * grad_gains

time: 278 us -> 275 us (0.989)
  other arithmetic: 27.3 us -> 31.2 us
    unnamed x229 -> x225, local copies, waits for them, and re-layouts: 12.7 us -> 11.4 us
where the time goes in v3:
time: 275 us; the launch traced here: 274 us
  waiting for transfers between devices  127 us (46%)
  starting transfers between devices  55.3 us (20%)
  other arithmetic  31.2 us (11%)
  Pallas kernels  24.7 us (9%)
  matrix products  18.3 us (7%)
  local copies, waits for them, and re-layouts  15.5 us (6%)
    ppermute x31, waiting for transfers between devices, swap(): return lax.ppermute(values, axis, [(i, i ^ mask) for i in range(count)])  79.5 us
    all_to_all x8, waiting for transfers between devices, exchange(): return lax.all_to_all(values, axis, split_axis=0, concat_axis=0, tiled=True)  47 us
    all_to_all x8, starting transfers between devices, exchange(): return lax.all_to_all(values, axis, split_axis=0, concat_axis=0, tiled=True)  36.3 us
    pallas_call x1, Pallas kernels, newton_schulz(): pl.pallas_call(kernel, out_shape=jax.ShapeDtypeStruct((size, slot), bf16)...  19.8 us
    ppermute x31, starting transfers between devices, swap(): return lax.ppermute(values, axis, [(i, i ^ mask) for i in range(count)])  18.9 us
    unnamed x225, local copies, waits for them, and re-layouts  11.4 us
    dot_general x6, matrix products, dot(): return jnp.dot(left, right, preferred_element_type=jnp.float32)  6.43 us
    dot_general x6, matrix products, dot_cols(): lax.dot_general(left, right, (((1,), (1,)), ((), ())), preferred_element_...  6.26 us
  transfers between devices with their start and end apart: 39, of which 28 were waited for; matrix products, arithmetic and copies ran while one was open for 16% of the time, Pallas kernels for 0%

profile of v3, /device:TPU:0, one launch (start us, length us, event | category | flops | bytes accessed | tf_op | source)
XLA Modules:
  0.0 273.9 jit_solution(16021174793227233157)
XLA Ops:
  0.7 2.4 shard_map.403
  3.1 6.4 %all-to-all-start = ((bf16[4,80,768]{2,1,0:T(8,128)(2,1)}), bf16[4,80,768]{2,1,0:T(8,128)(2,1)S(1)}, u32[]{:S(2)}, u32[]{:S(2)}) async-start(bf16[4,80,768]{2,1,0:T(8,128)(2,1)} %get-tuple-element.66), calls=%async_computation | async-start | bytes 983040 | tf_op jit(solution)/shard_map/all_to_all | solution.py:113
  9.5 1.5 collective-permute-start
  11.8 1.8 multiply_sine_fusion
  14.9 5.2 %collective-permute-done = f32[128,640]{1,0:T(8,128)S(1)} collective-permute-done((f32[128,640]{1,0:T(8,128)S(1)}, f32[128,640]{1,0:T(8,128)S(1)}, u32[]{:S(2)}, u32[]{:S(2)}) %collective-permute-start) | collective-permute-done | bytes 327712 | tf_op jit(solution)/shard_map/ppermute | solution.py:65
  20.1 3.2 %all-to-all-done = bf16[4,80,768]{2,1,0:T(8,128)(2,1)S(1)} async-done(((bf16[4,80,768]{2,1,0:T(8,128)(2,1)}), bf16[4,80,768]{2,1,0:T(8,128)(2,1)S(1)}, u32[]{:S(2)}, u32[]{:S(2)}) %all-to-all-start) | async-done | bytes 491552 | tf_op jit(solution)/shard_map/all_to_all | solution.py:113
  23.3 1.5 collective-permute-start.3
  25.2 10.4 %collective-permute-done.3 = bf16[4,80,768]{2,1,0:T(8,128)(2,1)S(1)} collective-permute-done((bf16[4,80,768]{2,1,0:T(8,128)(2,1)S(1)}, bf16[4,80,768]{2,1,0:T(8,128)(2,1)S(1)}, u32[]{:S(2)}, u32[]{:S(2)}) %collective-permute-start.3) | collective-permute-done | bytes 491552 | tf_op jit(solution)/shard_map/ppermute | solution.py:65
  36.0 1.3 pad_maximum_fusion.8
  37.3 2.2 pad_maximum_fusion.7
  39.5 4.2 %all-to-all-start.1 = ((bf16[4,80,1024]{2,1,0:T(8,128)(2,1)}), bf16[4,80,1024]{2,1,0:T(8,128)(2,1)}, u32[]{:S(2)}, u32[]{:S(2)}) async-start(bf16[4,80,1024]{2,1,0:T(8,128)(2,1)} %get-tuple-element.69), calls=%async_computation.1 | async-start | bytes 1310720 | tf_op jit(solution)/shard_map/all_to_all | solution.py:113
  50.4 1.5 collective-permute-start.8
  52.0 1.6 collective-permute-start.6
  53.5 1.5 collective-permute-done.8
  55.0 6.7 %all-to-all-done.1 = bf16[4,80,1024]{2,1,0:T(8,128)(2,1)} async-done(((bf16[4,80,1024]{2,1,0:T(8,128)(2,1)}), bf16[4,80,1024]{2,1,0:T(8,128)(2,1)}, u32[]{:S(2)}, u32[]{:S(2)}) %all-to-all-start.1) | async-done | bytes 655392 | tf_op jit(solution)/shard_map/all_to_all | solution.py:113
  62.6 1.5 collective-permute-start.9
  64.1 4.2 %all-to-all-start.2 = ((bf16[4,160,512]{2,1,0:T(8,128)(2,1)}), bf16[4,160,512]{2,1,0:T(8,128)(2,1)}, u32[]{:S(2)}, u32[]{:S(2)}) async-start(bf16[4,160,512]{2,1,0:T(8,128)(2,1)} %broadcast_in_dim.6), calls=%async_computation.2 | async-start | bytes 1310720 | tf_op jit(solution)/shard_map/all_to_all | solution.py:113
  69.1 1.4 multiply_reduce_fusion.4
  71.1 7.9 %collective-permute-done.9 = bf16[4,80,1024]{2,1,0:T(8,128)(2,1)} collective-permute-done((bf16[4,80,1024]{2,1,0:T(8,128)(2,1)}, bf16[4,80,1024]{2,1,0:T(8,128)(2,1)}, u32[]{:S(2)}, u32[]{:S(2)}) %collective-permute-start.9) | collective-permute-done | bytes 655392 | tf_op jit(solution)/shard_map/ppermute | solution.py:65
  79.0 1.4 select_bitcast_fusion.1
  81.8 1.3 copy-done.20
  85.3 1.8 fusion.87
  87.2 1.6 collective-permute-done.10
  88.9 1.6 collective-permute-start.11
  90.5 8.3 %collective-permute-done.11 = bf16[256,640]{1,0:T(8,128)(2,1)S(1)} collective-permute-done((bf16[256,640]{1,0:T(8,128)(2,1)S(1)}, bf16[256,640]{1,0:T(8,128)(2,1)S(1)}, u32[]{:S(2)}, u32[]{:S(2)}) %collective-permute-start.11) | collective-permute-done | bytes 327712 | tf_op jit(solution)/shard_map/ppermute | solution.py:65
  100.1 1.6 collective-permute-done.12
  101.7 2.4 fusion.11
  107.2 1.8 collective-permute-done.15
  109.0 2.0 fusion.21
  111.0 1.5 collective-permute-start.16
  112.5 1.4 convolution_convert_fusion.1
  113.8 4.4 %all-to-all-start.3 = ((bf16[4,160,512]{2,1,0:T(8,128)(2,1)}), bf16[4,160,512]{2,1,0:T(8,128)(2,1)}, u32[]{:S(2)}, u32[]{:S(2)}) async-start(bf16[4,160,512]{2,1,0:T(8,128)(2,1)} %bitcast.74), calls=%async_computation.3 | async-start | bytes 1310720 | tf_op jit(solution)/shard_map/all_to_all | solution.py:113
  118.2 2.3 convolution_convert_fusion
  123.0 1.2 multiply_reduce_fusion.1
  124.3 2.4 multiply_reduce_fusion
  127.5 10.8 %collective-permute-done.13 = bf16[4,80,1024]{2,1,0:T(8,128)(2,1)} collective-permute-done((bf16[4,80,1024]{2,1,0:T(8,128)(2,1)}, bf16[4,80,1024]{2,1,0:T(8,128)(2,1)}, u32[]{:S(2)}, u32[]{:S(2)}) %collective-permute-start.13) | collective-permute-done | bytes 655392 | tf_op jit(solution)/shard_map/ppermute | solution.py:65
  138.3 2.4 fusion.3
  140.7 4.6 %all-to-all-start.4 = ((bf16[4,80,1024]{2,1,0:T(8,128)(2,1)}), bf16[4,80,1024]{2,1,0:T(8,128)(2,1)S(1)}, u32[]{:S(2)}, u32[]{:S(2)}) async-start(bf16[4,80,1024]{2,1,0:T(8,128)(2,1)} %fusion.3), calls=%async_computation.4 | async-start | bytes 1310720 | tf_op jit(solution)/shard_map/all_to_all | solution.py:113
  145.3 1.6 multiply_reduce_fusion.11
  154.5 7.0 %all-to-all-done.4.refs_2_ = bf16[4,80,1024]{2,1,0:T(8,128)(2,1)S(1)} async-done(((bf16[4,80,1024]{2,1,0:T(8,128)(2,1)}), bf16[4,80,1024]{2,1,0:T(8,128)(2,1)S(1)}, u32[]{:S(2)}, u32[]{:S(2)}) %all-to-all-start.4) | async-done | bytes 655392 | tf_op jit(solution)/shard_map/all_to_all | solution.py:113
  162.5 3.7 %all-to-all-start.5 = ((bf16[8,80,768]{2,1,0:T(8,128)(2,1)}), bf16[8,80,768]{2,1,0:T(8,128)(2,1)S(1)}, u32[]{:S(2)}, u32[]{:S(2)}) async-start(bf16[8,80,768]{2,1,0:T(8,128)(2,1)} %bitcast.69), calls=%async_computation.5 | async-start | bytes 1966080 | tf_op jit(solution)/shard_map/all_to_all | solution.py:113
  167.0 2.2 fusion.13
  169.4 1.5 fusion.47
  170.8 1.2 convert_reduce_fusion
  172.2 2.0 collective-permute-start.14
  174.9 4.3 %collective-permute-done.14 = bf16[80,512]{1,0:T(8,128)(2,1)S(1)} collective-permute-done((bf16[80,512]{1,0:T(8,128)(2,1)S(1)}, bf16[80,512]{1,0:T(8,128)(2,1)S(1)}, u32[]{:S(2)}, u32[]{:S(2)}) %collective-permute-start.14) | collective-permute-done | bytes 81952 | tf_op jit(solution)/shard_map/ppermute | solution.py:65
  179.2 1.4 collective-permute-done.20
  181.4 8.8 %all-to-all-done.5.refs_3_ = bf16[8,80,768]{2,1,0:T(8,128)(2,1)S(1)} async-done(((bf16[8,80,768]{2,1,0:T(8,128)(2,1)}), bf16[8,80,768]{2,1,0:T(8,128)(2,1)S(1)}, u32[]{:S(2)}, u32[]{:S(2)}) %all-to-all-start.5) | async-done | bytes 983072 | tf_op jit(solution)/shard_map/all_to_all | solution.py:113
  190.3 1.5 shard_map.404
  191.9 3.7 %all-to-all-start.6 = ((bf16[8,80,512]{2,1,0:T(8,128)(2,1)}), bf16[8,80,512]{2,1,0:T(8,128)(2,1)S(1)}, u32[]{:S(2)}, u32[]{:S(2)}) async-start(bf16[8,80,512]{2,1,0:T(8,128)(2,1)} %get-tuple-element.77), calls=%async_computation.6 | async-start | bytes 1310720 | tf_op jit(solution)/shard_map/all_to_all | solution.py:113
  195.6 1.3 constant_dynamic-update-slice_fusion.2
  199.7 3.2 %collective-permute-done.22 = f32[3072]{0:T(1024)S(1)} collective-permute-done((f32[3072]{0:T(1024)S(1)}, f32[3072]{0:T(1024)S(1)}, u32[]{:S(2)}, u32[]{:S(2)}) %collective-permute-start.22) | collective-permute-done | bytes 12320 | tf_op jit(solution)/shard_map/ppermute | solution.py:65
  202.9 10.0 %all-to-all-done.6 = bf16[8,80,512]{2,1,0:T(8,128)(2,1)S(1)} async-done(((bf16[8,80,512]{2,1,0:T(8,128)(2,1)}), bf16[8,80,512]{2,1,0:T(8,128)(2,1)S(1)}, u32[]{:S(2)}, u32[]{:S(2)}) %all-to-all-start.6) | async-done | bytes 655392 | tf_op jit(solution)/shard_map/all_to_all | solution.py:113
  213.4 1.5 collective-permute-start.26
  214.9 2.2 collective-permute-done.26
  217.7 3.1 %collective-permute-done.27 = f32[3072]{0:T(1024)S(1)} collective-permute-done((f32[3072]{0:T(1024)S(1)}, f32[3072]{0:T(1024)S(1)}, u32[]{:S(2)}, u32[]{:S(2)}) %collective-permute-start.27) | collective-permute-done | bytes 12320 | tf_op jit(solution)/shard_map/ppermute | solution.py:65
  220.8 4.6 %collective-permute-done.28 = f32[3072]{0:T(1024)S(1)} collective-permute-done((f32[3072]{0:T(1024)S(1)}, f32[3072]{0:T(1024)S(1)}, u32[]{:S(2)}, u32[]{:S(2)}) %collective-permute-start.28) | collective-permute-done | bytes 12320 | tf_op jit(solution)/shard_map/ppermute | solution.py:65
  225.4 2.6 collective-permute-done.25.across_ref
  228.0 2.1 collective-permute-done.30.far_ref
  230.1 19.8 %shard_map.405 = bf16[640,512]{1,0:T(8,128)(2,1)} custom-call(s32[1]{0:T(128)} %bitcast.23.flag_ref, bf16[640,512]{1,0:T(8,128)(2,1)S(1)} %bitcast.62, bf16[640,512]{1,0:T(8,128)(2,1)S(1)} %collective-permute-done.29.near_ref, bf16[640,512]{1,0:T(8,128)(2,1)S(1)} %collective-permute-done.25.across_ref, bf16[640,512]{1,0:T(8,128)(2,1)S(1)} %collective-permute-done.30.far_ref), custom_call_target="tpu_custom_call" | custom-call | tf_op jit(solution)/shard_map/pallas_call | solution.py:292
  249.9 5.3 %all-to-all-start.7 = ((bf16[8,80,512]{2,1,0:T(8,128)(2,1)}), bf16[8,80,512]{2,1,0:T(8,128)(2,1)S(1)}, u32[]{:S(2)}, u32[]{:S(2)}) async-start(bf16[8,80,512]{2,1,0:T(8,128)(2,1)} %bitcast.24), calls=%async_computation.7 | async-start | bytes 1310720 | tf_op jit(solution)/shard_map/all_to_all | solution.py:113
  255.8 3.9 %collective-permute-done.23 = f32[80,256]{1,0:T(8,128)S(1)} collective-permute-done((f32[80,256]{1,0:T(8,128)S(1)}, f32[80,256]{1,0:T(8,128)S(1)}, u32[]{:S(2)}, u32[]{:S(2)}) %collective-permute-start.23) | collective-permute-done | bytes 81952 | tf_op jit(solution)/shard_map/ppermute | solution.py:65
  259.8 1.3 collective-permute-done.24
  262.4 10.4 %all-to-all-done.7.refs_0_ = bf16[8,80,512]{2,1,0:T(8,128)(2,1)S(1)} async-done(((bf16[8,80,512]{2,1,0:T(8,128)(2,1)}), bf16[8,80,512]{2,1,0:T(8,128)(2,1)S(1)}, u32[]{:S(2)}, u32[]{:S(2)}) %all-to-all-start.7) | async-done | bytes 655392 | tf_op jit(solution)/shard_map/all_to_all | solution.py:113
  (362 shorter events, 40.7 us)
Async XLA Ops:
  0.7 12.9 %copy-start.60 = (f32[3072]{0:T(1024)S(1)}, f32[3072]{0:T(1024)}, u32[]{:S(2)}) copy-start(f32[3072]{0:T(1024)} %param.37) | copy-start | bytes 36868
  3.1 20.1 %all-to-all-start = ((bf16[4,80,768]{2,1,0:T(8,128)(2,1)}), bf16[4,80,768]{2,1,0:T(8,128)(2,1)S(1)}, u32[]{:S(2)}, u32[]{:S(2)}) async-start(bf16[4,80,768]{2,1,0:T(8,128)(2,1)} %get-tuple-element.66), calls=%async_computation | async-start | bytes 983040 | tf_op jit(solution)/shard_map/all_to_all | solution.py:113
  9.5 10.6 %collective-permute-start = (f32[128,640]{1,0:T(8,128)S(1)}, f32[128,640]{1,0:T(8,128)S(1)}, u32[]{:S(2)}, u32[]{:S(2)}) collective-permute-start(f32[128,640]{1,0:T(8,128)S(1)} %copy-done.28), channel_id=1, source_target_pairs={{0,2},{1,3},{2,0},{3,1},{4,6},{5,7},{6,4},{7,5},{8,10},{9,11},{10,... | collective-permute-start | bytes 983048 | tf_op jit(solution)/shard_map/ppermute | solution.py:65
  11.0 25.0 %collective-permute-start.2 = (f32[128,640]{1,0:T(8,128)}, f32[128,640]{1,0:T(8,128)}, u32[]{:S(2)}, u32[]{:S(2)}) collective-permute-start(f32[128,640]{1,0:T(8,128)} %param.21), channel_id=1, source_target_pairs={{0,2},{1,3},{2,0},{3,1},{4,6},{5,7},{6,4},{7,5},{8,10},{9,11},{10,... | collective-permute-start | bytes 983048 | tf_op jit(solution)/shard_map/ppermute | solution.py:65
  13.6 33.6 %copy-start.33 = (f32[512,128]{1,0:T(8,128)}, f32[512,128]{1,0:T(8,128)S(1)}, u32[]{:S(2)}) copy-start(f32[512,128]{1,0:T(8,128)S(1)} %get-tuple-element.180) | copy-start | bytes 786436
  20.1 15.5 %copy-start.22 = (f32[256,640]{1,0:T(8,128)}, f32[256,640]{1,0:T(8,128)S(1)}, u32[]{:S(2)}) copy-start(f32[256,640]{1,0:T(8,128)S(1)} %constant_dynamic-update-slice_fusion) | copy-start | bytes 1966084
  23.3 12.2 %collective-permute-start.3 = (bf16[4,80,768]{2,1,0:T(8,128)(2,1)S(1)}, bf16[4,80,768]{2,1,0:T(8,128)(2,1)S(1)}, u32[]{:S(2)}, u32[]{:S(2)}) collective-permute-start(bf16[4,80,768]{2,1,0:T(8,128)(2,1)S(1)} %all-to-all-done), channel_id=1, source_target_pairs={{0,4},{4,0},{1,5},{5,1},{2,6},{6,2},{3,7},{7,3},{8,12},{12,8},{9,1... | collective-permute-start | bytes 1474568 | tf_op jit(solution)/shard_map/ppermute | solution.py:65
  25.1 12.2 %collective-permute-start.1 = (bf16[256,640]{1,0:T(8,128)(2,1)S(1)}, bf16[256,640]{1,0:T(8,128)(2,1)}, u32[]{:S(2)}, u32[]{:S(2)}) collective-permute-start(bf16[256,640]{1,0:T(8,128)(2,1)S(1)} %multiply_convert_fusion.3), channel_id=1, source_target_pairs={{0,1},{1,0},{2,3},{3,2},{4,5},{5,4},{6,7},{7,6},{8,9},{9,8},{10,11... | collective-permute-start | bytes 983048 | tf_op jit(solution)/shard_map/ppermute | solution.py:65
  35.8 13.4 %copy-start.23 = (bf16[4,2,80,768]{3,2,1,0:T(8,128)(2,1)}, bf16[4,2,80,768]{3,2,1,0:T(8,128)(2,1)S(1)}, u32[]{:S(2)}) copy-start(bf16[4,2,80,768]{3,2,1,0:T(8,128)(2,1)S(1)} %copy.58) | copy-start | bytes 2949124
  35.8 7.8 %collective-permute-start.4 = (bf16[640,256]{1,0:T(8,128)(2,1)S(1)}, bf16[640,256]{1,0:T(8,128)(2,1)S(1)}, u32[]{:S(2)}, u32[]{:S(2)}) collective-permute-start(bf16[640,256]{1,0:T(8,128)(2,1)S(1)} %slice.192), channel_id=1, source_target_pairs={{0,1},{1,0},{2,3},{3,2},{4,5},{5,4},{6,7},{7,6},{8,9},{9,8},{10,11... | collective-permute-start | bytes 983048 | tf_op jit(solution)/shard_map/ppermute | solution.py:65
  37.3 87.0 %copy-start.16 = (f32[256,640]{1,0:T(8,128)}, f32[256,640]{1,0:T(8,128)S(1)}, u32[]{:S(2)}) copy-start(f32[256,640]{1,0:T(8,128)S(1)} %pad_maximum_fusion.8) | copy-start | bytes 1966084
  39.5 22.3 %all-to-all-start.1 = ((bf16[4,80,1024]{2,1,0:T(8,128)(2,1)}), bf16[4,80,1024]{2,1,0:T(8,128)(2,1)}, u32[]{:S(2)}, u32[]{:S(2)}) async-start(bf16[4,80,1024]{2,1,0:T(8,128)(2,1)} %get-tuple-element.69), calls=%async_computation.1 | async-start | bytes 1310720 | tf_op jit(solution)/shard_map/all_to_all | solution.py:113
  49.9 2.0 collective-permute-start.5
  50.4 4.6 %collective-permute-start.8 = (bf16[80,512]{1,0:T(8,128)(2,1)S(1)}, bf16[80,512]{1,0:T(8,128)(2,1)S(1)}, u32[]{:S(2)}, u32[]{:S(2)}) collective-permute-start(bf16[80,512]{1,0:T(8,128)(2,1)S(1)} %copy-done.59), channel_id=1, source_target_pairs={{0,4},{4,0},{1,5},{5,1},{2,6},{6,2},{3,7},{7,3},{8,12},{12,8},{9,1... | collective-permute-start | bytes 245768 | tf_op jit(solution)/shard_map/ppermute | solution.py:65
  52.0 16.3 %collective-permute-start.6 = (bf16[256,640]{1,0:T(8,128)(2,1)S(1)}, bf16[256,640]{1,0:T(8,128)(2,1)S(1)}, u32[]{:S(2)}, u32[]{:S(2)}) collective-permute-start(bf16[256,640]{1,0:T(8,128)(2,1)S(1)} %fusion.23), channel_id=1, source_target_pairs={{0,2},{1,3},{2,0},{3,1},{4,6},{5,7},{6,4},{7,5},{8,10},{9,11},{10,... | collective-permute-start | bytes 983048 | tf_op jit(solution)/shard_map/ppermute | solution.py:65
  62.6 16.4 %collective-permute-start.9 = (bf16[4,80,1024]{2,1,0:T(8,128)(2,1)}, bf16[4,80,1024]{2,1,0:T(8,128)(2,1)}, u32[]{:S(2)}, u32[]{:S(2)}) collective-permute-start(bf16[4,80,1024]{2,1,0:T(8,128)(2,1)} %all-to-all-done.1), channel_id=1, source_target_pairs={{0,4},{4,0},{1,5},{5,1},{2,6},{6,2},{3,7},{7,3},{8,12},{12,8},{9,1... | collective-permute-start | bytes 1966088 | tf_op jit(solution)/shard_map/ppermute | solution.py:65
  64.1 21.1 %all-to-all-start.2 = ((bf16[4,160,512]{2,1,0:T(8,128)(2,1)}), bf16[4,160,512]{2,1,0:T(8,128)(2,1)}, u32[]{:S(2)}, u32[]{:S(2)}) async-start(bf16[4,160,512]{2,1,0:T(8,128)(2,1)} %broadcast_in_dim.6), calls=%async_computation.2 | async-start | bytes 1310720 | tf_op jit(solution)/shard_map/all_to_all | solution.py:113
  70.5 53.8 %copy-start.18 = (f32[256,640]{1,0:T(8,128)}, f32[256,640]{1,0:T(8,128)S(1)}, u32[]{:S(2)}) copy-start(f32[256,640]{1,0:T(8,128)S(1)} %get-tuple-element.127) | copy-start | bytes 1966084
  70.7 9.9 %collective-permute-start.7 = (bf16[256,640]{1,0:T(8,128)(2,1)S(1)}, bf16[256,640]{1,0:T(8,128)(2,1)S(1)}, u32[]{:S(2)}, u32[]{:S(2)}) collective-permute-start(bf16[256,640]{1,0:T(8,128)(2,1)S(1)} %multiply_convert_fusion.2), channel_id=1, source_target_pairs={{0,1},{1,0},{2,3},{3,2},{4,5},{5,4},{6,7},{7,6},{8,9},{9,8},{10,11... | collective-permute-start | bytes 983048 | tf_op jit(solution)/shard_map/ppermute | solution.py:65
  87.1 1.7 collective-permute-start.10
  88.9 9.8 %collective-permute-start.11 = (bf16[256,640]{1,0:T(8,128)(2,1)S(1)}, bf16[256,640]{1,0:T(8,128)(2,1)S(1)}, u32[]{:S(2)}, u32[]{:S(2)}) collective-permute-start(bf16[256,640]{1,0:T(8,128)(2,1)S(1)} %fusion.22), channel_id=1, source_target_pairs={{0,2},{1,3},{2,0},{3,1},{4,6},{5,7},{6,4},{7,5},{8,10},{9,11},{10,... | collective-permute-start | bytes 983048 | tf_op jit(solution)/shard_map/ppermute | solution.py:65
  100.1 1.6 collective-permute-start.12
  107.0 2.0 collective-permute-start.15
  111.0 11.0 %collective-permute-start.16 = (bf16[256,640]{1,0:T(8,128)(2,1)}, bf16[256,640]{1,0:T(8,128)(2,1)}, u32[]{:S(2)}, u32[]{:S(2)}) collective-permute-start(bf16[256,640]{1,0:T(8,128)(2,1)} %fusion.21), channel_id=1, source_target_pairs={{0,2},{1,3},{2,0},{3,1},{4,6},{5,7},{6,4},{7,5},{8,10},{9,11},{10,... | collective-permute-start | bytes 983048 | tf_op jit(solution)/shard_map/ppermute | solution.py:65
  113.8 26.8 %all-to-all-start.3 = ((bf16[4,160,512]{2,1,0:T(8,128)(2,1)}), bf16[4,160,512]{2,1,0:T(8,128)(2,1)}, u32[]{:S(2)}, u32[]{:S(2)}) async-start(bf16[4,160,512]{2,1,0:T(8,128)(2,1)} %bitcast.74), calls=%async_computation.3 | async-start | bytes 1310720 | tf_op jit(solution)/shard_map/all_to_all | solution.py:113
  121.5 16.8 %collective-permute-start.13 = (bf16[4,80,1024]{2,1,0:T(8,128)(2,1)}, bf16[4,80,1024]{2,1,0:T(8,128)(2,1)}, u32[]{:S(2)}, u32[]{:S(2)}) collective-permute-start(bf16[4,80,1024]{2,1,0:T(8,128)(2,1)} %dynamic-slice_bitcast_fusion), channel_id=1, source_target_pairs={{0,4},{4,0},{1,5},{5,1},{2,6},{6,2},{3,7},{7,3},{8,12},{12,8},{9,1... | collective-permute-start | bytes 1966088 | tf_op jit(solution)/shard_map/ppermute | solution.py:65
  127.5 17.7 %collective-permute-start.17 = (bf16[256,640]{1,0:T(8,128)(2,1)S(1)}, bf16[256,640]{1,0:T(8,128)(2,1)S(1)}, u32[]{:S(2)}, u32[]{:S(2)}) collective-permute-start(bf16[256,640]{1,0:T(8,128)(2,1)S(1)} %subtract_convert_fusion), channel_id=1, source_target_pairs={{0,1},{1,0},{2,3},{3,2},{4,5},{5,4},{6,7},{7,6},{8,9},{9,8},{10,11... | collective-permute-start | bytes 983048 | tf_op jit(solution)/shard_map/ppermute | solution.py:65
  127.5 17.7 %copy-start.50 = (bf16[512,256]{0,1:T(8,128)(2,1)S(1)}, bf16[512,256]{0,1:T(8,128)(2,1)}, u32[]{:S(2)}) copy-start(bf16[512,256]{0,1:T(8,128)(2,1)} %copy-done.49) | copy-start | bytes 786436
  140.7 20.8 %all-to-all-start.4 = ((bf16[4,80,1024]{2,1,0:T(8,128)(2,1)}), bf16[4,80,1024]{2,1,0:T(8,128)(2,1)S(1)}, u32[]{:S(2)}, u32[]{:S(2)}) async-start(bf16[4,80,1024]{2,1,0:T(8,128)(2,1)} %fusion.3), calls=%async_computation.4 | async-start | bytes 1310720 | tf_op jit(solution)/shard_map/all_to_all | solution.py:113
  152.7 1.7 collective-permute-start.18
  162.5 27.7 %all-to-all-start.5 = ((bf16[8,80,768]{2,1,0:T(8,128)(2,1)}), bf16[8,80,768]{2,1,0:T(8,128)(2,1)S(1)}, u32[]{:S(2)}, u32[]{:S(2)}) async-start(bf16[8,80,768]{2,1,0:T(8,128)(2,1)} %bitcast.69), calls=%async_computation.5 | async-start | bytes 1966080 | tf_op jit(solution)/shard_map/all_to_all | solution.py:113
  166.2 14.4 %copy-start.99 = (f32[128]{0:T(128)}, f32[128]{0:T(128)S(1)}, u32[]{:S(2)}) copy-start(f32[128]{0:T(128)S(1)} %add_rsqrt_fusion.6) | copy-start | bytes 1540
  169.3 4.9 %collective-permute-start.19 = (bf16[256,640]{1,0:T(8,128)(2,1)S(1)}, bf16[256,640]{1,0:T(8,128)(2,1)S(1)}, u32[]{:S(2)}, u32[]{:S(2)}) collective-permute-start(bf16[256,640]{1,0:T(8,128)(2,1)S(1)} %slice.324), channel_id=1, source_target_pairs={{0,1},{1,0},{2,3},{3,2},{4,5},{5,4},{6,7},{7,6},{8,9},{9,8},{10,11... | collective-permute-start | bytes 983048 | tf_op jit(solution)/shard_map/ppermute | solution.py:65
  172.1 18.1 %copy-start.3 = (f32[80,256]{1,0:T(8,128)S(1)}, f32[80,256]{1,0:T(8,128)}, u32[]{:S(2)}) copy-start(f32[80,256]{1,0:T(8,128)} %refs_5_.4) | copy-start | bytes 245764
  172.1 18.1 %copy-start.4 = (f32[80,256]{1,0:T(8,128)S(1)}, f32[80,256]{1,0:T(8,128)}, u32[]{:S(2)}) copy-start(f32[80,256]{1,0:T(8,128)} %refs_6_.4) | copy-start | bytes 245764
  172.1 18.1 %copy-start.9 = (f32[80,512]{1,0:T(8,128)S(1)}, f32[80,512]{1,0:T(8,128)}, u32[]{:S(2)}) copy-start(f32[80,512]{1,0:T(8,128)} %refs_8_.1) | copy-start | bytes 491524
  172.2 18.1 %copy-start.10 = (f32[80,512]{1,0:T(8,128)S(1)}, f32[80,512]{1,0:T(8,128)}, u32[]{:S(2)}) copy-start(f32[80,512]{1,0:T(8,128)} %refs_9_.1) | copy-start | bytes 491524
  172.2 18.1 %copy-start.11 = (f32[80,512]{1,0:T(8,128)S(1)}, f32[80,512]{1,0:T(8,128)}, u32[]{:S(2)}) copy-start(f32[80,512]{1,0:T(8,128)} %refs_10_.1) | copy-start | bytes 491524
  172.2 18.1 %copy-start.12 = (f32[80,256]{1,0:T(8,128)S(1)}, f32[80,256]{1,0:T(8,128)}, u32[]{:S(2)}) copy-start(f32[80,256]{1,0:T(8,128)} %refs_4_.4) | copy-start | bytes 245764
  172.2 18.1 %copy-start.13 = (f32[80,256]{1,0:T(8,128)S(1)}, f32[80,256]{1,0:T(8,128)}, u32[]{:S(2)}) copy-start(f32[80,256]{1,0:T(8,128)} %refs_7_.4) | copy-start | bytes 245764
  172.2 7.0 %collective-permute-start.14 = (bf16[80,512]{1,0:T(8,128)(2,1)S(1)}, bf16[80,512]{1,0:T(8,128)(2,1)S(1)}, u32[]{:S(2)}, u32[]{:S(2)}) collective-permute-start(bf16[80,512]{1,0:T(8,128)(2,1)S(1)} %fusion.56), channel_id=1, source_target_pairs={{0,4},{4,0},{1,5},{5,1},{2,6},{6,2},{3,7},{7,3},{8,12},{12,8},{9,1... | collective-permute-start | bytes 245768 | tf_op jit(solution)/shard_map/ppermute | solution.py:65
  174.3 6.4 %collective-permute-start.20 = (bf16[128,640]{1,0:T(8,128)(2,1)S(1)}, bf16[128,640]{1,0:T(8,128)(2,1)S(1)}, u32[]{:S(2)}, u32[]{:S(2)}) collective-permute-start(bf16[128,640]{1,0:T(8,128)(2,1)S(1)} %slice.226), channel_id=1, source_target_pairs={{0,2},{1,3},{2,0},{3,1},{4,6},{5,7},{6,4},{7,5},{8,10},{9,11},{10,... | collective-permute-start | bytes 491528 | tf_op jit(solution)/shard_map/ppermute | solution.py:65
  191.9 21.0 %all-to-all-start.6 = ((bf16[8,80,512]{2,1,0:T(8,128)(2,1)}), bf16[8,80,512]{2,1,0:T(8,128)(2,1)S(1)}, u32[]{:S(2)}, u32[]{:S(2)}) async-start(bf16[8,80,512]{2,1,0:T(8,128)(2,1)} %get-tuple-element.77), calls=%async_computation.6 | async-start | bytes 1310720 | tf_op jit(solution)/shard_map/all_to_all | solution.py:113
  197.9 1.2 collective-permute-start.21
  199.2 3.7 %collective-permute-start.22 = (f32[3072]{0:T(1024)S(1)}, f32[3072]{0:T(1024)S(1)}, u32[]{:S(2)}, u32[]{:S(2)}) collective-permute-start(f32[3072]{0:T(1024)S(1)} %add.328), channel_id=1, source_target_pairs={{0,2},{1,3},{2,0},{3,1},{4,6},{5,7},{6,4},{7,5},{8,10},{9,11},{10,... | collective-permute-start | bytes 36872 | tf_op jit(solution)/shard_map/ppermute | solution.py:65
  212.9 15.1 %collective-permute-start.25 = (bf16[640,512]{1,0:T(8,128)(2,1)S(1)}, bf16[640,512]{1,0:T(8,128)(2,1)S(1)}, u32[]{:S(2)}, u32[]{:S(2)}) collective-permute-start(bf16[640,512]{1,0:T(8,128)(2,1)S(1)} %bitcast.60), channel_id=1, source_target_pairs={{0,2},{1,3},{2,0},{3,1},{4,6},{5,7},{6,4},{7,5},{8,10},{9,11},{10,... | collective-permute-start | bytes 1966088 | tf_op jit(solution)/shard_map/ppermute | solution.py:65
  213.4 3.7 %collective-permute-start.26 = (f32[3072]{0:T(1024)S(1)}, f32[3072]{0:T(1024)S(1)}, u32[]{:S(2)}, u32[]{:S(2)}) collective-permute-start(f32[3072]{0:T(1024)S(1)} %add.329), channel_id=1, source_target_pairs={{0,4},{4,0},{1,5},{5,1},{2,6},{6,2},{3,7},{7,3},{8,12},{12,8},{9,1... | collective-permute-start | bytes 36872 | tf_op jit(solution)/shard_map/ppermute | solution.py:65
  217.1 3.7 %collective-permute-start.27 = (f32[3072]{0:T(1024)S(1)}, f32[3072]{0:T(1024)S(1)}, u32[]{:S(2)}, u32[]{:S(2)}) collective-permute-start(f32[3072]{0:T(1024)S(1)} %add.332), channel_id=1, source_target_pairs={{0,8},{8,0},{16,24},{24,16},{1,9},{9,1},{17,25},{25,17},{2,10},{10... | collective-permute-start | bytes 36872 | tf_op jit(solution)/shard_map/ppermute | solution.py:65
  220.8 4.6 %collective-permute-start.28 = (f32[3072]{0:T(1024)S(1)}, f32[3072]{0:T(1024)S(1)}, u32[]{:S(2)}, u32[]{:S(2)}) collective-permute-start(f32[3072]{0:T(1024)S(1)} %add.333), channel_id=1, source_target_pairs={{0,16},{8,24},{16,0},{24,8},{1,17},{9,25},{17,1},{25,9},{2,18},{10... | collective-permute-start | bytes 36872 | tf_op jit(solution)/shard_map/ppermute | solution.py:65
  220.8 7.2 %collective-permute-start.29 = (bf16[640,512]{1,0:T(8,128)(2,1)S(1)}, bf16[640,512]{1,0:T(8,128)(2,1)S(1)}, u32[]{:S(2)}, u32[]{:S(2)}) collective-permute-start(bf16[640,512]{1,0:T(8,128)(2,1)S(1)} %bitcast.61), channel_id=1, source_target_pairs={{0,1},{1,0},{2,3},{3,2},{4,5},{5,4},{6,7},{7,6},{8,9},{9,8},{10,11... | collective-permute-start | bytes 1966088 | tf_op jit(solution)/shard_map/ppermute | solution.py:65
  225.4 36.4 %copy-start.66 = (f32[3072]{0:T(1024)}, f32[3072]{0:T(1024)S(1)}, u32[]{:S(2)}) copy-start(f32[3072]{0:T(1024)S(1)} %add.334) | copy-start | bytes 36868
  228.0 2.1 collective-permute-start.30
  249.9 11.9 %copy-start.84 = (f32[3072]{0:T(1024)S(1)}, f32[3072]{0:T(1024)}, u32[]{:S(2)}) copy-start(f32[3072]{0:T(1024)} %param.38) | copy-start | bytes 36868
  249.9 11.9 %copy-start.85 = (f32[3072]{0:T(1024)S(1)}, f32[3072]{0:T(1024)}, u32[]{:S(2)}) copy-start(f32[3072]{0:T(1024)} %param.39) | copy-start | bytes 36868
  249.9 23.0 %copy-start = (f32[80,512]{1,0:T(8,128)S(1)}, f32[80,512]{1,0:T(8,128)}, u32[]{:S(2)}) copy-start(f32[80,512]{1,0:T(8,128)} %refs_5_.5) | copy-start | bytes 491524
  249.9 23.0 %copy-start.1 = (f32[80,512]{1,0:T(8,128)S(1)}, f32[80,512]{1,0:T(8,128)}, u32[]{:S(2)}) copy-start(f32[80,512]{1,0:T(8,128)} %refs_6_.5) | copy-start | bytes 491524
  249.9 23.0 %copy-start.2 = (f32[80,512]{1,0:T(8,128)S(1)}, f32[80,512]{1,0:T(8,128)}, u32[]{:S(2)}) copy-start(f32[80,512]{1,0:T(8,128)} %refs_7_.5) | copy-start | bytes 491524
  249.9 23.0 %copy-start.5 = (f32[80,256]{1,0:T(8,128)S(1)}, f32[80,256]{1,0:T(8,128)}, u32[]{:S(2)}) copy-start(f32[80,256]{1,0:T(8,128)} %refs_1_.3) | copy-start | bytes 245764
  249.9 23.0 %copy-start.6 = (f32[80,256]{1,0:T(8,128)S(1)}, f32[80,256]{1,0:T(8,128)}, u32[]{:S(2)}) copy-start(f32[80,256]{1,0:T(8,128)} %refs_2_.3) | copy-start | bytes 245764
  249.9 23.0 %copy-start.7 = (f32[80,256]{1,0:T(8,128)S(1)}, f32[80,256]{1,0:T(8,128)}, u32[]{:S(2)}) copy-start(f32[80,256]{1,0:T(8,128)} %refs_3_.3) | copy-start | bytes 245764
  249.9 22.9 %copy-start.8 = (f32[80,256]{1,0:T(8,128)S(1)}, f32[80,256]{1,0:T(8,128)}, u32[]{:S(2)}) copy-start(f32[80,256]{1,0:T(8,128)} %refs_4_.5) | copy-start | bytes 245764
  249.9 22.9 %all-to-all-start.7 = ((bf16[8,80,512]{2,1,0:T(8,128)(2,1)}), bf16[8,80,512]{2,1,0:T(8,128)(2,1)S(1)}, u32[]{:S(2)}, u32[]{:S(2)}) async-start(bf16[8,80,512]{2,1,0:T(8,128)(2,1)} %bitcast.24), calls=%async_computation.7 | async-start | bytes 1310720 | tf_op jit(solution)/shard_map/all_to_all | solution.py:113
  255.2 4.4 %collective-permute-start.23 = (f32[80,256]{1,0:T(8,128)S(1)}, f32[80,256]{1,0:T(8,128)S(1)}, u32[]{:S(2)}, u32[]{:S(2)}) collective-permute-start(f32[80,256]{1,0:T(8,128)S(1)} %get-tuple-element.80), channel_id=1, source_target_pairs={{0,2},{1,3},{2,0},{3,1},{4,6},{5,7},{6,4},{7,5},{8,10},{9,11},{10,... | collective-permute-start | bytes 245768 | tf_op jit(solution)/shard_map/ppermute | solution.py:65
  259.7 1.3 collective-permute-start.24
  (87 other events, 267.3 us)
